TPU v7x, 256 devices: a whole 4x4x8 slice. The times are simulated.
256 devices in a mesh: req: 32 (over y, x, core), head: 8 (over z).
Axes of the slice: x: 4, y: 4, z: 8, core: 2. Of those that a mesh axis runs over, the one named last changes fastest.
Arguments:
- queries: bfloat16 [1024, 16384], P(('req', 'head')), may hold values from -15 to 15
- cache_keys: bfloat16 [8, 32768, 1024], P(None, 'req', 'head'), may hold values from -6 to 6
- cache_values: bfloat16 [8, 32768, 1024], P(None, 'req', 'head'), may hold values from -6 to 6
- tree_keys: bfloat16 [1024, 1024], P('req', 'head'), may hold values from -10 to 10
- tree_values: bfloat16 [1024, 1024], P('req', 'head'), may hold values from -6 to 6
- parents: int32 [8, 128], replicated, may hold values from -1 to 126, as said below
- tree_sizes: int32 [8], replicated, may hold values from 16 to 128
- cache_lens: int32 [8], replicated, may hold values from 2 to 32768
Outputs:
- attended: bfloat16 [1024, 16384], P('req', 'head')
Inputs may be any that keep to these rules, and one draw needn't show every extreme that they name: parents[a, 0] = -1 (the root); for node i >= 1, parents[a, i] is a node of 0 to i - 1.
All inputs are finite; a program needn't handle non-finite values.
Results may differ from a plain program's by a relative error of at most 0.003.
Values may be sent and summed in bfloat16 or wider, within the bound.
A program may use at most 128 MiB of HBM per device.

v0:
```python
import math

import jax
import jax.numpy as jnp
from jax import lax
from jax.sharding import PartitionSpec as P

NH = 128
KVH = 8
HD = 128


negative_fill = -1e30


def ancestry(parents):
    node_count = parents.shape[1]
    node_ids = jnp.arange(node_count, dtype=jnp.int32)
    linked = jnp.logical_or(
        parents[:, :, None] == node_ids[None, None, :], node_ids[:, None] == node_ids[None, :]
    )
    reached = linked.astype(jnp.bfloat16)
    for doubling in range((node_count - 1).bit_length()):
        squared = jnp.einsum("aij,ajk->aik", reached, reached, preferred_element_type=jnp.float32)
        reached = jnp.minimum(squared, 1.0).astype(jnp.bfloat16)
    return reached


def body(
    queries, cache_keys, cache_values, tree_keys, tree_values, parents, tree_sizes, cache_lens
):
    group_size = NH // KVH
    softmax_scale = 1.0 / math.sqrt(HD)
    owner_index = lax.axis_index("req")
    request_count = cache_keys.shape[0]
    cache_block = cache_keys.shape[1]
    kv_local = cache_keys.shape[2] // HD
    heads_local = kv_local * group_size
    node_count = parents.shape[1]
    rows_owned = tree_keys.shape[0]
    by_head = lax.all_to_all(queries, "head", split_axis=1, concat_axis=0, tiled=True)
    all_rows = lax.all_gather(by_head, "req", axis=0, tiled=True)
    reached = ancestry(parents)
    node_ids = jnp.arange(node_count, dtype=jnp.int32)
    key_rows = owner_index * rows_owned + jnp.arange(rows_owned, dtype=jnp.int32)
    key_request = key_rows // node_count
    key_node = key_rows % node_count
    node_select = (node_ids[:, None] == key_node[None, :]).astype(jnp.bfloat16)
    positions = owner_index * cache_block + jnp.arange(cache_block, dtype=jnp.int32)
    local_tree_keys = tree_keys.reshape(rows_owned, kv_local, HD)
    local_tree_values = tree_values.reshape(rows_owned, kv_local, HD)

    def one_request(request):
        query_block = lax.dynamic_slice_in_dim(all_rows, request * node_count, node_count, 0)
        query_block = query_block.reshape(node_count, kv_local, group_size, HD)
        block_keys = lax.dynamic_index_in_dim(cache_keys, request, 0, keepdims=False).reshape(
            cache_block, kv_local, HD
        )
        block_values = lax.dynamic_index_in_dim(cache_values, request, 0, keepdims=False).reshape(
            cache_block, kv_local, HD
        )
        length = lax.dynamic_index_in_dim(cache_lens, request, 0, keepdims=False)
        live_cache = positions < length
        ancestors = lax.dynamic_index_in_dim(reached, request, 0, keepdims=False)
        ancestor_cols = jnp.dot(ancestors, node_select, preferred_element_type=jnp.float32)
        live_tree = jnp.logical_and(ancestor_cols > 0.5, (key_request == request)[None, :])
        cache_scores = (
            jnp.einsum(
                "igqd,pgd->igqp", query_block, block_keys, preferred_element_type=jnp.float32
            )
            * softmax_scale
        )
        cache_scores = jnp.where(live_cache[None, None, None, :], cache_scores, negative_fill)
        tree_scores = (
            jnp.einsum(
                "igqd,rgd->igqr", query_block, local_tree_keys, preferred_element_type=jnp.float32
            )
            * softmax_scale
        )
        tree_scores = jnp.where(live_tree[:, None, None, :], tree_scores, negative_fill)
        peaks = jnp.maximum(jnp.max(cache_scores, axis=3), jnp.max(tree_scores, axis=3))
        cache_weights = jnp.where(
            live_cache[None, None, None, :], jnp.exp(cache_scores - peaks[..., None]), 0.0
        )
        tree_weights = jnp.where(
            live_tree[:, None, None, :], jnp.exp(tree_scores - peaks[..., None]), 0.0
        )
        totals = jnp.sum(cache_weights, axis=3) + jnp.sum(tree_weights, axis=3)
        group_sums = jnp.einsum(
            "igqp,pgd->igqd",
            cache_weights.astype(jnp.bfloat16),
            block_values,
            preferred_element_type=jnp.float32,
        )
        group_sums = group_sums + jnp.einsum(
            "igqr,rgd->igqd",
            tree_weights.astype(jnp.bfloat16),
            local_tree_values,
            preferred_element_type=jnp.float32,
        )
        floored = jnp.maximum(totals, 1.0)
        partial_value = group_sums / floored[..., None]
        log_total = peaks + jnp.log(floored)
        return (
            partial_value.reshape(node_count, heads_local * HD),
            log_total.reshape(node_count, heads_local),
        )

    partials, log_totals = lax.map(one_request, jnp.arange(request_count, dtype=jnp.int32))
    partials = partials.reshape(request_count * node_count, heads_local * HD)
    log_totals = log_totals.reshape(request_count * node_count, heads_local)
    highest = lax.pmax(log_totals, "req")
    weights = jnp.exp(log_totals - highest)
    summed = lax.psum(weights, "req")
    shares = weights / summed
    piece = partials.reshape(rows_owned * lax.axis_size("req"), heads_local, HD)
    merged = lax.psum_scatter(
        (shares[..., None] * piece).reshape(rows_owned * lax.axis_size("req"), heads_local * HD),
        "req",
        scatter_dimension=0,
        tiled=True,
    )
    own_rows = owner_index * rows_owned + jnp.arange(rows_owned, dtype=jnp.int32)
    row_request = own_rows // node_count
    request_ids = jnp.arange(request_count, dtype=jnp.int32)
    row_sizes = jnp.sum(
        jnp.where(row_request[:, None] == request_ids[None, :], tree_sizes[None, :], 0), axis=1
    )
    live_rows = own_rows % node_count < row_sizes
    return jnp.where(live_rows[:, None], merged, 0.0).astype(jnp.bfloat16)


def solution(mesh):
    placed = (
        P(("req", "head"), None),
        P(None, "req", "head"),
        P(None, "req", "head"),
        P("req", "head"),
        P("req", "head"),
        P(),
        P(),
        P(),
    )
    return jax.shard_map(
        body, mesh=mesh, in_specs=placed, out_specs=P("req", "head"), check_vma=False
    )
```

profile of v0, /device:TPU:1, one launch (start us, length us, event | category | flops | bytes accessed | tf_op | source)
XLA Modules:
  0.0 562.4 jit_solution(5107307987589632554)
XLA Ops:
  6.5 16.8 %all_to_all.19 = bf16[4,8,2048]{2,0,1:T(4,128)(2,1)S(1)} all-to-all(bf16[4,8,2048]{2,0,1:T(4,128)(2,1)} %bitcast.165), channel_id=1, replica_groups=mesh['req'=32,'head'=8] {'head'}, dimensions={1} | all-to-all | bytes 262144 | tf_op jit(solution)/shard_map/all_to_all | solution.py:41
  27.0 46.6 %all-gather.2.cloned.1.call-done = bf16[1024,2048]{1,0:T(8,128)(2,1)} async-done(((bf16[32,2048]{1,0:T(8,128)(2,1)}), bf16[1024,2048]{1,0:T(8,128)(2,1)}) %all-gather.2.cloned.1.call-update) | async-done | bytes 4194320 | tf_op jit(solution)/shard_map/all_gather | solution.py:42
  73.6 148.6 %while.13 = (s32[]{:T(128)}, f32[8,128,2048]{2,1,0:T(8,128)}, f32[8,128,16]{1,0,2:T(8,128)S(1)}, s32[8]{0:T(128)S(1)}, bf16[8,1024,128]{2,1,0:T(8,128)(2,1)}, /*...) while((s32[]{:T(128)}, f32[8,128,2048]{2,1,0:T(8,128)}, ...), condition=%wide.region_6.7_spmd.clone, body=%wide.region_1.6_spmd.clone.sunk | while | flops 1136740864 | bytes 37222784 | solution.py:109
  81.9 2.6 bitcast_reduce_fusion.2
  84.6 2.6 fusion.105
  87.2 3.2 fusion.104
  100.5 2.6 bitcast_reduce_fusion.2
  103.1 2.6 fusion.105
  105.8 3.2 fusion.104
  119.1 2.6 bitcast_reduce_fusion.2
  121.8 2.6 fusion.105
  124.4 3.2 fusion.104
  137.7 2.6 bitcast_reduce_fusion.2
  140.3 2.6 fusion.105
  142.9 3.2 fusion.104
  156.2 2.6 bitcast_reduce_fusion.2
  158.9 2.6 fusion.105
  161.5 3.2 fusion.104
  174.8 2.6 bitcast_reduce_fusion.2
  177.4 2.6 fusion.105
  180.0 3.2 fusion.104
  193.3 2.6 bitcast_reduce_fusion.2
  196.0 2.6 fusion.105
  198.6 3.2 fusion.104
  211.9 2.6 bitcast_reduce_fusion.2
  214.6 2.6 fusion.105
  217.2 3.2 fusion.104
  222.9 105.2 %all-reduce.3.cloned.1.call-done = f32[1024,16]{0,1:T(8,128)} async-done(((f32[1024,16]{0,1:T(8,128)}), f32[1024,16]{0,1:T(8,128)}) %all-reduce.3.cloned.1.call-update) | async-done | bytes 65552 | tf_op jit(solution)/shard_map/pmax | solution.py:112
  329.9 106.2 %all-reduce.5.cloned.1.call-done = f32[1024,16]{0,1:T(8,128)} async-done(((f32[1024,16]{0,1:T(8,128)}), f32[1024,16]{0,1:T(8,128)}) %all-reduce.5.cloned.1.call-update) | async-done | bytes 65552 | tf_op jit(solution)/shard_map/psum | solution.py:114
  437.1 5.9 %mul.42 = f32[1024,16,128]{2,1,0:T(8,128)} broadcast(f32[1024,16]{1,0:T(8,128)S(1)} %copy.37), dimensions={0,1} | broadcast | bytes 8454144 | tf_op jit(solution)/shard_map/mul | solution.py:118
  443.0 13.7 %bitcast_multiply_fusion = f32[1024,2048]{1,0:T(8,128)} fusion(f32[128,8,16,128]{3,2,1,0:T(8,128)} %bitcast.157, f32[8,128,2048]{2,1,0:T(8,128)} %get-tuple-element.79), kind=kLoop, calls=%fused_computation.59 | loop fusion | flops 2097152 | bytes 25165824 | tf_op jit(solution)/shard_map/mul | solution.py:118
  457.4 96.8 %reduce-scatter.2.cloned.1.call-done = f32[32,2048]{1,0:T(8,128)} async-done(((f32[1024,2048]{1,0:T(8,128)}), f32[32,2048]{1,0:T(8,128)}) %reduce-scatter.2.cloned.1.call-update) | async-done | bytes 262160 | tf_op jit(solution)/shard_map/reduce_scatter | solution.py:117
  (164 shorter events, 69.9 us)
Async XLA Ops:
  6.5 67.1 %all-gather.2.cloned.1.call-start = ((), (), s32[]{:S(2)}) async-start(), calls=%async_computation.2 | async-start | bytes 4325376 | tf_op jit(solution)/shard_map/all_gather | solution.py:42
  24.0 304.1 %all-reduce.3.cloned.1.call-start = ((), (), s32[]{:S(2)}) async-start(), calls=%async_computation.3 | async-start | bytes 131072 | tf_op jit(solution)/shard_map/pmax | solution.py:112
  87.2 3.2 copy-start
  105.7 3.2 copy-start
  124.3 3.2 copy-start
  142.9 3.2 copy-start
  161.5 3.2 copy-start
  180.0 3.2 copy-start
  198.6 3.2 copy-start
  217.2 3.2 copy-start
  222.9 213.1 %all-reduce.5.cloned.1.call-start = ((), (), s32[]{:S(2)}) async-start(), calls=%async_computation.4 | async-start | bytes 131072 | tf_op jit(solution)/shard_map/psum | solution.py:114
  329.6 224.5 %reduce-scatter.2.cloned.1.call-start = ((), (), s32[]{:S(2)}) async-start(), calls=%async_computation.5 | async-start | bytes 8650752 | tf_op jit(solution)/shard_map/reduce_scatter | solution.py:117
  456.7 0.7 copy-start.1
Sparse Core Ops, SparseCore 0:
  24.2 49.4 all-gather.1
  223.0 105.0 all-reduce.2
  331.4 104.5 all-reduce.4
  456.8 97.3 reduce-scatter.1
where the time goes:
time: 565 us; the launch traced here: 562 us
  waiting for transfers between devices  355 us (63%)
  matrix products  60.3 us (11%)
  other arithmetic  49.5 us (9%)
  local copies, waits for them, and re-layouts  45.8 us (8%)
  loops' own time  21.7 us (4%)
  blocking collectives  16.8 us (3%)
  between operations  13.2 us (2%)
    psum x1, waiting for transfers between devices, body(): summed = lax.psum(weights, 'req')  106 us
    pmax x1, waiting for transfers between devices, body(): highest = lax.pmax(log_totals, 'req')  105 us
    reduce_scatter x1, waiting for transfers between devices, body(): lax.psum_scatter((shares[..., None] * piece).reshape(rows_owned * lax.axi...  96.8 us
    all_gather x1, waiting for transfers between devices, body(): all_rows = lax.all_gather(by_head, 'req', axis=0, tiled=True)  46.6 us
    dot_general x8, matrix products, one_request(): jnp.einsum('igqp,pgd->igqd', cache_weights.astype(jnp.bfloat16), block_va...  25.2 us
    another operation x1, loops' own time, body(): lax.map(one_request, jnp.arange(request_count, dtype=jnp.int32))  21.7 us
    reduce_sum x16, other arithmetic, one_request(): totals = jnp.sum(cache_weights, axis=3) + jnp.sum(tree_weights, axis=3)  21.2 us
    dot_general x8, matrix products, one_request(): jnp.einsum('igqd,pgd->igqp', query_block, block_keys, preferred_element_t...  20.6 us
  transfers between devices with their start and end apart: 4, of which 4 were waited for; matrix products, arithmetic and copies ran while one was open for 1% of the time, Pallas kernels for 0%

commit v1 on v0

v1 whole, which is shorter than its diff:
```python
import math

import jax
import jax.numpy as jnp
from jax import lax
from jax.sharding import Mesh
from jax.sharding import PartitionSpec as P

NH = 128
KVH = 8
HD = 128


negative_fill = -1e30


def ancestry(parents):
    node_count = parents.shape[1]
    node_ids = jnp.arange(node_count, dtype=jnp.int32)
    linked = jnp.logical_or(
        parents[:, :, None] == node_ids[None, None, :], node_ids[:, None] == node_ids[None, :]
    )
    reached = linked.astype(jnp.bfloat16)
    for doubling in range((node_count - 1).bit_length()):
        squared = jnp.einsum("aij,ajk->aik", reached, reached, preferred_element_type=jnp.float32)
        reached = jnp.minimum(squared, 1.0).astype(jnp.bfloat16)
    return reached


def body(
    queries, cache_keys, cache_values, tree_keys, tree_values, parents, tree_sizes, cache_lens
):
    group_size = NH // KVH
    softmax_scale = 1.0 / math.sqrt(HD)
    request = lax.axis_index("rh")
    quarter = lax.axis_index("rl")
    n_lo = lax.axis_size("rl")
    n_hi = lax.axis_size("rh")
    cache_block = cache_keys.shape[1]
    kv_local = cache_keys.shape[2] // HD
    heads_local = kv_local * group_size
    node_count = parents.shape[1]
    rows_owned = tree_keys.shape[0]

    by_head = lax.all_to_all(queries, "head", split_axis=1, concat_axis=0, tiled=True)
    query_block = lax.all_gather(by_head, "rl", axis=0, tiled=True)
    query_block = query_block.reshape(node_count, kv_local, group_size, HD)

    both = jnp.concatenate([cache_keys, cache_values], axis=2)
    mine = lax.all_to_all(both, "rh", split_axis=0, concat_axis=1, tiled=True)[0]
    mine = mine.reshape(n_hi, cache_block, 2, kv_local, HD)

    reached = ancestry(parents)
    ancestors = lax.dynamic_index_in_dim(reached, request, 0, keepdims=False)
    ancestors = lax.dynamic_slice_in_dim(ancestors, quarter * rows_owned, rows_owned, 1)
    live_tree_all = ancestors > 0.5
    length = lax.dynamic_index_in_dim(cache_lens, request, 0, keepdims=False)
    local_tree_keys = tree_keys.reshape(rows_owned, kv_local, HD)
    local_tree_values = tree_values.reshape(rows_owned, kv_local, HD)

    def one_group(s):
        block = s * n_lo + quarter
        positions = block * cache_block + jnp.arange(cache_block, dtype=jnp.int32)
        live_cache = positions < length
        live_tree = jnp.logical_and(live_tree_all, s == request)
        block_keys = mine[s, :, 0]
        block_values = mine[s, :, 1]
        cache_scores = (
            jnp.einsum(
                "igqd,pgd->igqp", query_block, block_keys, preferred_element_type=jnp.float32
            )
            * softmax_scale
        )
        cache_scores = jnp.where(live_cache[None, None, None, :], cache_scores, negative_fill)
        tree_scores = (
            jnp.einsum(
                "igqd,rgd->igqr", query_block, local_tree_keys, preferred_element_type=jnp.float32
            )
            * softmax_scale
        )
        tree_scores = jnp.where(live_tree[:, None, None, :], tree_scores, negative_fill)
        peaks = jnp.maximum(jnp.max(cache_scores, axis=3), jnp.max(tree_scores, axis=3))
        cache_weights = jnp.where(
            live_cache[None, None, None, :], jnp.exp(cache_scores - peaks[..., None]), 0.0
        )
        tree_weights = jnp.where(
            live_tree[:, None, None, :], jnp.exp(tree_scores - peaks[..., None]), 0.0
        )
        totals = jnp.sum(cache_weights, axis=3) + jnp.sum(tree_weights, axis=3)
        group_sums = jnp.einsum(
            "igqp,pgd->igqd",
            cache_weights.astype(jnp.bfloat16),
            block_values,
            preferred_element_type=jnp.float32,
        )
        group_sums = group_sums + jnp.einsum(
            "igqr,rgd->igqd",
            tree_weights.astype(jnp.bfloat16),
            local_tree_values,
            preferred_element_type=jnp.float32,
        )
        floored = jnp.maximum(totals, 1.0)
        partial_value = group_sums / floored[..., None]
        log_total = peaks + jnp.log(floored)
        return (
            partial_value.reshape(node_count, heads_local, HD),
            log_total.reshape(node_count, heads_local),
        )

    partials, log_totals = lax.map(one_group, jnp.arange(n_hi, dtype=jnp.int32))
    top = jnp.max(log_totals, axis=0)
    weights = jnp.exp(log_totals - top)
    den = jnp.sum(weights, axis=0)
    acc = jnp.sum(weights[..., None] * partials, axis=0)

    payload = jnp.concatenate(
        [acc.reshape(node_count, heads_local * HD), den, top], axis=1
    ).reshape(n_lo, rows_owned, heads_local * HD + 2 * heads_local)
    gathered = lax.all_to_all(payload, "rl", split_axis=0, concat_axis=0, tiled=True)
    got_acc = gathered[:, :, : heads_local * HD].reshape(n_lo, rows_owned, heads_local, HD)
    got_den = gathered[:, :, heads_local * HD : heads_local * HD + heads_local]
    got_top = gathered[:, :, heads_local * HD + heads_local :]
    highest = jnp.max(got_top, axis=0)
    scale = jnp.exp(got_top - highest)
    num = jnp.sum(scale[..., None] * got_acc, axis=0)
    total = jnp.sum(scale * got_den, axis=0)
    merged = (num / total[..., None]).reshape(rows_owned, heads_local * HD)

    row_nodes = quarter * rows_owned + jnp.arange(rows_owned, dtype=jnp.int32)
    live_size = lax.dynamic_index_in_dim(tree_sizes, request, 0, keepdims=False)
    live_rows = row_nodes < live_size
    return jnp.where(live_rows[:, None], merged, 0.0).astype(jnp.bfloat16)


def solution(mesh):
    def run(queries, cache_keys, cache_values, tree_keys, tree_values, parents, tree_sizes, cache_lens):
        n_hi = cache_keys.shape[0]
        n_lo = mesh.shape["req"] // n_hi
        split = Mesh(mesh.devices.reshape(n_hi, n_lo, mesh.shape["head"]), ("rh", "rl", "head"))
        rows = ("rh", "rl")
        placed = (
            P(("rh", "rl", "head"), None),
            P(None, rows, "head"),
            P(None, rows, "head"),
            P(rows, "head"),
            P(rows, "head"),
            P(),
            P(),
            P(),
        )
        return jax.shard_map(
            body, mesh=split, in_specs=placed, out_specs=P(rows, "head"), check_vma=False
        )(queries, cache_keys, cache_values, tree_keys, tree_values, parents, tree_sizes, cache_lens)

    return run
```

time: 565 us -> 275 us (0.49)
  waiting for transfers between devices: 355 us -> 13.1 us
  matrix products: 60.3 us -> 103 us
  blocking collectives: 16.8 us -> 47.9 us
  local copies, waits for them, and re-layouts: 45.8 us -> 23.5 us
  starting transfers between devices: 0.31 us -> 21 us
  between operations: 13.2 us -> 0.23 us
  other arithmetic: 49.5 us -> 36.8 us
  loops' own time: 21.7 us -> 27.8 us
    psum x1 -> x0, waiting for transfers between devices: 106 us -> none  [body(): summed = lax.psum(weights, 'req')]
    pmax x1 -> x0, waiting for transfers between devices: 105 us -> none  [body(): highest = lax.pmax(log_totals, 'req')]
    reduce_scatter x1 -> x0, waiting for transfers between devices: 96.8 us -> none  [body(): lax.psum_scatter((shares[..., None] * piece).reshape(rows_owned * lax.axi...]
    all_gather x0 -> x1, blocking collectives: none -> 47.9 us  [body(): query_block = lax.all_gather(by_head, 'rl', axis=0, tiled=True)]
    all_gather x1 -> x0, waiting for transfers between devices: 46.6 us -> none  [body(): all_rows = lax.all_gather(by_head, 'req', axis=0, tiled=True)]
    dot_general x40 -> x25, matrix products: 57.4 us -> 101 us  [the longest x8 46.3 us: one_group(): jnp.einsum('igqp,pgd->igqd', cache_weights.astype(jnp.bfloat16), block_va...]
    all_to_all x0 -> x3, starting transfers between devices: none -> 21 us  [the longest x1 9.15 us: body(): lax.all_to_all(queries, 'head', split_axis=1, concat_axis=0, tiled=True)]
    dynamic_slice x32 -> x10, local copies, waits for them, and re-layouts: 25.9 us -> 6.39 us  [the longest x8 5.23 us: body(): partials, log_totals = lax.map(one_group, jnp.arange(n_hi, dtype=jnp.int32))]
  transfers between devices with their start and end apart: 4 -> 3, of which waited for: 4 -> 1; matrix products, arithmetic and copies ran while one was open for 1% -> 6% of each run, Pallas kernels for 0% -> 0%
where the time goes in v1:
time: 275 us; the launch traced here: 273 us
  matrix products  103 us (37%)
  blocking collectives  47.9 us (17%)
  other arithmetic  36.8 us (13%)
  loops' own time  27.8 us (10%)
  local copies, waits for them, and re-layouts  23.5 us (9%)
  starting transfers between devices  21 us (8%)
  waiting for transfers between devices  13.1 us (5%)
    all_gather x1, blocking collectives, body(): query_block = lax.all_gather(by_head, 'rl', axis=0, tiled=True)  47.9 us
    dot_general x8, matrix products, one_group(): jnp.einsum('igqp,pgd->igqd', cache_weights.astype(jnp.bfloat16), block_va...  46.3 us
    dot_general x8, matrix products, one_group(): jnp.einsum('igqd,pgd->igqp', query_block, block_keys, preferred_element_t...  43.9 us
    another operation x1, loops' own time, body(): partials, log_totals = lax.map(one_group, jnp.arange(n_hi, dtype=jnp.int32))  27.8 us
    reduce_sum x16, other arithmetic, one_group(): totals = jnp.sum(cache_weights, axis=3) + jnp.sum(tree_weights, axis=3)  20.8 us
    all_to_all x1, waiting for transfers between devices, body(): lax.all_to_all(payload, 'rl', split_axis=0, concat_axis=0, tiled=True)  13.1 us
    dot_general x8, matrix products, one_group(): jnp.einsum('igqr,rgd->igqd', tree_weights.astype(jnp.bfloat16), local_tre...  10.8 us
    all_to_all x1, starting transfers between devices, body(): lax.all_to_all(queries, 'head', split_axis=1, concat_axis=0, tiled=True)  9.15 us
  transfers between devices with their start and end apart: 3, of which 1 were waited for; matrix products, arithmetic and copies ran while one was open for 6% of the time, Pallas kernels for 0%

profile of v1, /device:TPU:1, one launch (start us, length us, event | category | flops | bytes accessed | tf_op | source)
XLA Modules:
  0.0 273.4 jit_solution(10835699050133776124)
XLA Ops:
  0.0 9.1 %all-to-all-start.1 = ((bf16[4,8,2048]{2,0,1:T(4,128)(2,1)}), bf16[4,8,2048]{2,0,1:T(4,128)(2,1)S(1)}, u32[]{:S(2)}, u32[]{:S(2)}) async-start(bf16[4,8,2048]{2,0,1:T(4,128)(2,1)} %bitcast.168), calls=%async_computation.1 | async-start | bytes 262144 | tf_op jit(solution)/shard_map/all_to_all | solution.py:45
  9.2 2.9 %copy.62 = bf16[8,1024,128]{1,2,0:T(8,128)(2,1)S(1)} copy(bf16[8,1024,128]{2,1,0:T(8,128)(2,1)} %param.12) | data formatting | bytes 4194304 | tf_op args[2]
  12.0 3.9 %copy.61 = bf16[8,1024,128]{1,2,0:T(8,128)(2,1)} copy(bf16[8,1024,128]{2,1,0:T(8,128)(2,1)} %param.11) | data formatting | bytes 4194304 | tf_op args[1]
  16.0 4.2 %pad_maximum_fusion = bf16[8,1024,256]{1,2,0:T(8,128)(2,1)} fusion(bf16[8,1024,128]{1,2,0:T(8,128)(2,1)S(1)} %copy.62, bf16[8,1024,128]{1,2,0:T(8,128)(2,1)} %copy.61), kind=kLoop, calls=%fused_computation.47 | loop fusion | flops 8388608 | bytes 8388608 | tf_op jit(solution)/shard_map/concatenate | solution.py:49
  20.2 6.7 %all-to-all-start = ((bf16[8,1024,256]{1,2,0:T(8,128)(2,1)}), bf16[8,1024,256]{1,2,0:T(8,128)(2,1)}, u32[]{:S(2)}, u32[]{:S(2)}) async-start(bf16[8,1024,256]{1,2,0:T(8,128)(2,1)} %pad_maximum_fusion), calls=%async_computation | async-start | bytes 8388608 | tf_op jit(solution)/shard_map/all_to_all | solution.py:50
  29.7 47.9 %all_gather.3 = bf16[128,2048]{1,0:T(8,128)(2,1)S(1)} all-gather(bf16[32,2048]{1,0:T(8,128)(2,1)S(1)} %all_to_all.28), channel_id=1, replica_groups=mesh['rh'=8,'rl'=4,'head'=8] {'rl'}, dimensions={0}, use_global_device_ids=true | all-gather | bytes 655360 | tf_op jit(solution)/shard_map/all_gather | solution.py:46
  78.5 6.5 %copy.69 = bf16[8,1024,2,1,128]{4,1,3,2,0:T(8,128)(2,1)} copy(bf16[8,1024,2,1,128]{1,4,2,0,3:T(8,128)(2,1)} %bitcast.20) | data formatting | bytes 8388608 | tf_op jit(solution)/shard_map/while | solution.py:110
  85.0 160.4 %while.14 = (s32[]{:T(128)}, f32[8,128,16,128]{1,3,2,0:T(8,128)}, f32[8,128,16]{1,2,0:T(8,128)S(1)}, s32[8]{0:T(128)S(1)}, bf16[8,1024,2,1,128]{4,1,3,2,0:T(8,12...) while((s32[]{:T(128)}, f32[8,128,16,128]{1,3,2,0:T(8,128)}, ...), condition=%wide.region_5.6_spmd, body=%wide.region_0.5_spmd.sunk | while | flops 1119164416 | bytes 55485768 | solution.py:110
  88.9 5.5 %bitcast_reduce_fusion.2 = (f32[128,16]{0,1:T(8,128)S(1)}, f32[1024,128,16]{1,0,2:T(8,128)}) fusion(pred[1024]{0:T(1024)(128)(4,1)S(1)} %add_compare_fusion.3, bf16[128,1,16,128]{3,0,2,1:T(8,128)(2,1)S(1)} %get-tuple-element.349, bf16[8,1024,2,1,128]{4,1,3,2,0:T(8,128)(2,1)} %get-tuple-element.346, s32[]{:T(128)S(6)} %select_n.118), kind=kOutput, calls=%fused_computation.1.clone.1 | convolution fusion | flops 543160320 | bytes 9184260 | tf_op jit(solution)/shard_map/while/body/eval_jaxpr/igqd,pgd->igqp/dot_general | solution.py:69
  95.2 5.8 %fusion.85 = f32[128,128,16]{1,0,2:T(8,128)S(1)} fusion(f32[1024,128,16]{1,0,2:T(8,128)} %get-tuple-element.304, f32[128,16]{0,1:T(8,128)S(1)} %max.47, pred[1024]{0:T(1024)(128)(4,1)S(1)} %add_compare_fusion.3, bf16[8,1024,2,1,128]{4,1,3,2,0:T(8,128)(2,1)} %get-tuple-element.346, s32[]{:T(128)S(6)} %select_n.118), kind=kOutput, calls=%fused_computation.8.clone.1 | convolution fusion | flops 547356672 | bytes 9709572 | tf_op jit(solution)/shard_map/while/body/eval_jaxpr/igqp,pgd->igqd/dot_general | solution.py:90
  101.0 2.5 fusion.86
  108.9 5.5 %bitcast_reduce_fusion.2 = (f32[128,16]{0,1:T(8,128)S(1)}, f32[1024,128,16]{1,0,2:T(8,128)}) fusion(pred[1024]{0:T(1024)(128)(4,1)S(1)} %add_compare_fusion.3, bf16[128,1,16,128]{3,0,2,1:T(8,128)(2,1)S(1)} %get-tuple-element.349, bf16[8,1024,2,1,128]{4,1,3,2,0:T(8,128)(2,1)} %get-tuple-element.346, s32[]{:T(128)S(6)} %select_n.118), kind=kOutput, calls=%fused_computation.1.clone.1 | convolution fusion | flops 543160320 | bytes 9184260 | tf_op jit(solution)/shard_map/while/body/eval_jaxpr/igqd,pgd->igqp/dot_general | solution.py:69
  115.2 5.8 %fusion.85 = f32[128,128,16]{1,0,2:T(8,128)S(1)} fusion(f32[1024,128,16]{1,0,2:T(8,128)} %get-tuple-element.304, f32[128,16]{0,1:T(8,128)S(1)} %max.47, pred[1024]{0:T(1024)(128)(4,1)S(1)} %add_compare_fusion.3, bf16[8,1024,2,1,128]{4,1,3,2,0:T(8,128)(2,1)} %get-tuple-element.346, s32[]{:T(128)S(6)} %select_n.118), kind=kOutput, calls=%fused_computation.8.clone.1 | convolution fusion | flops 547356672 | bytes 9709572 | tf_op jit(solution)/shard_map/while/body/eval_jaxpr/igqp,pgd->igqd/dot_general | solution.py:90
  121.1 2.5 fusion.86
  129.0 5.5 %bitcast_reduce_fusion.2 = (f32[128,16]{0,1:T(8,128)S(1)}, f32[1024,128,16]{1,0,2:T(8,128)}) fusion(pred[1024]{0:T(1024)(128)(4,1)S(1)} %add_compare_fusion.3, bf16[128,1,16,128]{3,0,2,1:T(8,128)(2,1)S(1)} %get-tuple-element.349, bf16[8,1024,2,1,128]{4,1,3,2,0:T(8,128)(2,1)} %get-tuple-element.346, s32[]{:T(128)S(6)} %select_n.118), kind=kOutput, calls=%fused_computation.1.clone.1 | convolution fusion | flops 543160320 | bytes 9184260 | tf_op jit(solution)/shard_map/while/body/eval_jaxpr/igqd,pgd->igqp/dot_general | solution.py:69
  135.3 5.8 %fusion.85 = f32[128,128,16]{1,0,2:T(8,128)S(1)} fusion(f32[1024,128,16]{1,0,2:T(8,128)} %get-tuple-element.304, f32[128,16]{0,1:T(8,128)S(1)} %max.47, pred[1024]{0:T(1024)(128)(4,1)S(1)} %add_compare_fusion.3, bf16[8,1024,2,1,128]{4,1,3,2,0:T(8,128)(2,1)} %get-tuple-element.346, s32[]{:T(128)S(6)} %select_n.118), kind=kOutput, calls=%fused_computation.8.clone.1 | convolution fusion | flops 547356672 | bytes 9709572 | tf_op jit(solution)/shard_map/while/body/eval_jaxpr/igqp,pgd->igqd/dot_general | solution.py:90
  141.2 2.5 fusion.86
  149.1 5.5 %bitcast_reduce_fusion.2 = (f32[128,16]{0,1:T(8,128)S(1)}, f32[1024,128,16]{1,0,2:T(8,128)}) fusion(pred[1024]{0:T(1024)(128)(4,1)S(1)} %add_compare_fusion.3, bf16[128,1,16,128]{3,0,2,1:T(8,128)(2,1)S(1)} %get-tuple-element.349, bf16[8,1024,2,1,128]{4,1,3,2,0:T(8,128)(2,1)} %get-tuple-element.346, s32[]{:T(128)S(6)} %select_n.118), kind=kOutput, calls=%fused_computation.1.clone.1 | convolution fusion | flops 543160320 | bytes 9184260 | tf_op jit(solution)/shard_map/while/body/eval_jaxpr/igqd,pgd->igqp/dot_general | solution.py:69
  155.3 5.8 %fusion.85 = f32[128,128,16]{1,0,2:T(8,128)S(1)} fusion(f32[1024,128,16]{1,0,2:T(8,128)} %get-tuple-element.304, f32[128,16]{0,1:T(8,128)S(1)} %max.47, pred[1024]{0:T(1024)(128)(4,1)S(1)} %add_compare_fusion.3, bf16[8,1024,2,1,128]{4,1,3,2,0:T(8,128)(2,1)} %get-tuple-element.346, s32[]{:T(128)S(6)} %select_n.118), kind=kOutput, calls=%fused_computation.8.clone.1 | convolution fusion | flops 547356672 | bytes 9709572 | tf_op jit(solution)/shard_map/while/body/eval_jaxpr/igqp,pgd->igqd/dot_general | solution.py:90
  161.2 2.5 fusion.86
  169.1 5.5 %bitcast_reduce_fusion.2 = (f32[128,16]{0,1:T(8,128)S(1)}, f32[1024,128,16]{1,0,2:T(8,128)}) fusion(pred[1024]{0:T(1024)(128)(4,1)S(1)} %add_compare_fusion.3, bf16[128,1,16,128]{3,0,2,1:T(8,128)(2,1)S(1)} %get-tuple-element.349, bf16[8,1024,2,1,128]{4,1,3,2,0:T(8,128)(2,1)} %get-tuple-element.346, s32[]{:T(128)S(6)} %select_n.118), kind=kOutput, calls=%fused_computation.1.clone.1 | convolution fusion | flops 543160320 | bytes 9184260 | tf_op jit(solution)/shard_map/while/body/eval_jaxpr/igqd,pgd->igqp/dot_general | solution.py:69
  175.4 5.8 %fusion.85 = f32[128,128,16]{1,0,2:T(8,128)S(1)} fusion(f32[1024,128,16]{1,0,2:T(8,128)} %get-tuple-element.304, f32[128,16]{0,1:T(8,128)S(1)} %max.47, pred[1024]{0:T(1024)(128)(4,1)S(1)} %add_compare_fusion.3, bf16[8,1024,2,1,128]{4,1,3,2,0:T(8,128)(2,1)} %get-tuple-element.346, s32[]{:T(128)S(6)} %select_n.118), kind=kOutput, calls=%fused_computation.8.clone.1 | convolution fusion | flops 547356672 | bytes 9709572 | tf_op jit(solution)/shard_map/while/body/eval_jaxpr/igqp,pgd->igqd/dot_general | solution.py:90
  181.2 2.5 fusion.86
  189.1 5.5 %bitcast_reduce_fusion.2 = (f32[128,16]{0,1:T(8,128)S(1)}, f32[1024,128,16]{1,0,2:T(8,128)}) fusion(pred[1024]{0:T(1024)(128)(4,1)S(1)} %add_compare_fusion.3, bf16[128,1,16,128]{3,0,2,1:T(8,128)(2,1)S(1)} %get-tuple-element.349, bf16[8,1024,2,1,128]{4,1,3,2,0:T(8,128)(2,1)} %get-tuple-element.346, s32[]{:T(128)S(6)} %select_n.118), kind=kOutput, calls=%fused_computation.1.clone.1 | convolution fusion | flops 543160320 | bytes 9184260 | tf_op jit(solution)/shard_map/while/body/eval_jaxpr/igqd,pgd->igqp/dot_general | solution.py:69
  195.4 5.8 %fusion.85 = f32[128,128,16]{1,0,2:T(8,128)S(1)} fusion(f32[1024,128,16]{1,0,2:T(8,128)} %get-tuple-element.304, f32[128,16]{0,1:T(8,128)S(1)} %max.47, pred[1024]{0:T(1024)(128)(4,1)S(1)} %add_compare_fusion.3, bf16[8,1024,2,1,128]{4,1,3,2,0:T(8,128)(2,1)} %get-tuple-element.346, s32[]{:T(128)S(6)} %select_n.118), kind=kOutput, calls=%fused_computation.8.clone.1 | convolution fusion | flops 547356672 | bytes 9709572 | tf_op jit(solution)/shard_map/while/body/eval_jaxpr/igqp,pgd->igqd/dot_general | solution.py:90
  209.2 5.5 %bitcast_reduce_fusion.2 = (f32[128,16]{0,1:T(8,128)S(1)}, f32[1024,128,16]{1,0,2:T(8,128)}) fusion(pred[1024]{0:T(1024)(128)(4,1)S(1)} %add_compare_fusion.3, bf16[128,1,16,128]{3,0,2,1:T(8,128)(2,1)S(1)} %get-tuple-element.349, bf16[8,1024,2,1,128]{4,1,3,2,0:T(8,128)(2,1)} %get-tuple-element.346, s32[]{:T(128)S(6)} %select_n.118), kind=kOutput, calls=%fused_computation.1.clone.1 | convolution fusion | flops 543160320 | bytes 9184260 | tf_op jit(solution)/shard_map/while/body/eval_jaxpr/igqd,pgd->igqp/dot_general | solution.py:69
  215.5 5.8 %fusion.85 = f32[128,128,16]{1,0,2:T(8,128)S(1)} fusion(f32[1024,128,16]{1,0,2:T(8,128)} %get-tuple-element.304, f32[128,16]{0,1:T(8,128)S(1)} %max.47, pred[1024]{0:T(1024)(128)(4,1)S(1)} %add_compare_fusion.3, bf16[8,1024,2,1,128]{4,1,3,2,0:T(8,128)(2,1)} %get-tuple-element.346, s32[]{:T(128)S(6)} %select_n.118), kind=kOutput, calls=%fused_computation.8.clone.1 | convolution fusion | flops 547356672 | bytes 9709572 | tf_op jit(solution)/shard_map/while/body/eval_jaxpr/igqp,pgd->igqd/dot_general | solution.py:90
  229.3 5.5 %bitcast_reduce_fusion.2 = (f32[128,16]{0,1:T(8,128)S(1)}, f32[1024,128,16]{1,0,2:T(8,128)}) fusion(pred[1024]{0:T(1024)(128)(4,1)S(1)} %add_compare_fusion.3, bf16[128,1,16,128]{3,0,2,1:T(8,128)(2,1)S(1)} %get-tuple-element.349, bf16[8,1024,2,1,128]{4,1,3,2,0:T(8,128)(2,1)} %get-tuple-element.346, s32[]{:T(128)S(6)} %select_n.118), kind=kOutput, calls=%fused_computation.1.clone.1 | convolution fusion | flops 543160320 | bytes 9184260 | tf_op jit(solution)/shard_map/while/body/eval_jaxpr/igqd,pgd->igqp/dot_general | solution.py:69
  235.5 5.8 %fusion.85 = f32[128,128,16]{1,0,2:T(8,128)S(1)} fusion(f32[1024,128,16]{1,0,2:T(8,128)} %get-tuple-element.304, f32[128,16]{0,1:T(8,128)S(1)} %max.47, pred[1024]{0:T(1024)(128)(4,1)S(1)} %add_compare_fusion.3, bf16[8,1024,2,1,128]{4,1,3,2,0:T(8,128)(2,1)} %get-tuple-element.346, s32[]{:T(128)S(6)} %select_n.118), kind=kOutput, calls=%fused_computation.8.clone.1 | convolution fusion | flops 547356672 | bytes 9709572 | tf_op jit(solution)/shard_map/while/body/eval_jaxpr/igqp,pgd->igqd/dot_general | solution.py:90
  245.5 4.8 %multiply_reduce_fusion = f32[128,16,128]{0,2,1:T(8,128)S(1)} fusion(f32[8,128,16,128]{1,3,2,0:T(8,128)} %get-tuple-element.146, f32[8,128,16]{1,2,0:T(8,128)S(1)} %get-tuple-element.224), kind=kLoop, calls=%fused_computation.46 | loop fusion | flops 3932160 | bytes 9502720 | tf_op jit(solution)/shard_map/reduce_sum | solution.py:114
  252.2 5.2 %all-to-all-start.2 = ((f32[4,32,2080]{2,1,0:T(8,128)}), f32[4,32,2080]{2,1,0:T(8,128)S(1)}, u32[]{:S(2)}, u32[]{:S(2)}) async-start(f32[4,32,2080]{2,1,0:T(8,128)} %concatenate.17), calls=%async_computation.2 | async-start | bytes 2228224 | tf_op jit(solution)/shard_map/all_to_all | solution.py:119
  258.7 13.1 %all-to-all-done.2 = f32[4,32,2080]{2,1,0:T(8,128)S(1)} async-done(((f32[4,32,2080]{2,1,0:T(8,128)}), f32[4,32,2080]{2,1,0:T(8,128)S(1)}, u32[]{:S(2)}, u32[]{:S(2)}) %all-to-all-start.2) | async-done | bytes 1064992 | tf_op jit(solution)/shard_map/all_to_all | solution.py:119
  (150 shorter events, 38.4 us)
Async XLA Ops:
  0.0 78.3 %copy-start = (bf16[32,128]{1,0:T(8,128)(2,1)S(1)}, bf16[32,128]{1,0:T(8,128)(2,1)}, u32[]{:S(2)}) copy-start(bf16[32,128]{1,0:T(8,128)(2,1)} %param.13) | copy-start | bytes 24580
  0.0 20.2 %all-to-all-start.1 = ((bf16[4,8,2048]{2,0,1:T(4,128)(2,1)}), bf16[4,8,2048]{2,0,1:T(4,128)(2,1)S(1)}, u32[]{:S(2)}, u32[]{:S(2)}) async-start(bf16[4,8,2048]{2,0,1:T(4,128)(2,1)} %bitcast.168), calls=%async_computation.1 | async-start | bytes 262144 | tf_op jit(solution)/shard_map/all_to_all | solution.py:45
  16.0 10.9 %copy-start.3 = (s32[8]{0:T(128)S(1)}, s32[8]{0:T(128)}, u32[]{:S(2)}) copy-start(s32[8]{0:T(128)} %param.17) | copy-start | bytes 100
  16.0 11.5 %copy-start.2 = (s32[8,128]{1,0:T(8,128)S(1)}, s32[8,128]{1,0:T(8,128)}, u32[]{:S(2)}) copy-start(s32[8,128]{1,0:T(8,128)} %param.15) | copy-start | bytes 12292
  20.2 58.3 %all-to-all-start = ((bf16[8,1024,256]{1,2,0:T(8,128)(2,1)}), bf16[8,1024,256]{1,2,0:T(8,128)(2,1)}, u32[]{:S(2)}, u32[]{:S(2)}) async-start(bf16[8,1024,256]{1,2,0:T(8,128)(2,1)} %pad_maximum_fusion), calls=%async_computation | async-start | bytes 8388608 | tf_op jit(solution)/shard_map/all_to_all | solution.py:50
  26.8 58.1 %copy-start.1 = (bf16[32,128]{1,0:T(8,128)(2,1)S(1)}, bf16[32,128]{1,0:T(8,128)(2,1)}, u32[]{:S(2)}) copy-start(bf16[32,128]{1,0:T(8,128)(2,1)} %param.14) | copy-start | bytes 24580
  95.1 5.9 %slice-start = ((s8[8388608]{0:T(1024)(128)(4,1)}), s8[4194304]{0:T(1024)(128)(4,1)S(1)}, s32[]{:S(2)}) async-start(s8[8388608]{0:T(1024)(128)(4,1)} %bitcast.160), calls=%async_computation.3 | async-start | bytes 8388608 | tf_op jit(solution)/shard_map/while
  95.2 5.9 %slice-start.1 = ((s8[8388608]{0:T(1024)(128)(4,1)}), s8[4194304]{0:T(1024)(128)(4,1)S(1)}, s32[]{:S(2)}) async-start(s8[8388608]{0:T(1024)(128)(4,1)} %bitcast.160), calls=%async_computation.4 | async-start | bytes 8388608 | tf_op jit(solution)/shard_map/while
  115.1 5.9 %slice-start = ((s8[8388608]{0:T(1024)(128)(4,1)}), s8[4194304]{0:T(1024)(128)(4,1)S(1)}, s32[]{:S(2)}) async-start(s8[8388608]{0:T(1024)(128)(4,1)} %bitcast.160), calls=%async_computation.3 | async-start | bytes 8388608 | tf_op jit(solution)/shard_map/while
  115.2 5.9 %slice-start.1 = ((s8[8388608]{0:T(1024)(128)(4,1)}), s8[4194304]{0:T(1024)(128)(4,1)S(1)}, s32[]{:S(2)}) async-start(s8[8388608]{0:T(1024)(128)(4,1)} %bitcast.160), calls=%async_computation.4 | async-start | bytes 8388608 | tf_op jit(solution)/shard_map/while
  135.2 5.9 %slice-start = ((s8[8388608]{0:T(1024)(128)(4,1)}), s8[4194304]{0:T(1024)(128)(4,1)S(1)}, s32[]{:S(2)}) async-start(s8[8388608]{0:T(1024)(128)(4,1)} %bitcast.160), calls=%async_computation.3 | async-start | bytes 8388608 | tf_op jit(solution)/shard_map/while
  135.3 5.9 %slice-start.1 = ((s8[8388608]{0:T(1024)(128)(4,1)}), s8[4194304]{0:T(1024)(128)(4,1)S(1)}, s32[]{:S(2)}) async-start(s8[8388608]{0:T(1024)(128)(4,1)} %bitcast.160), calls=%async_computation.4 | async-start | bytes 8388608 | tf_op jit(solution)/shard_map/while
  155.2 5.9 %slice-start = ((s8[8388608]{0:T(1024)(128)(4,1)}), s8[4194304]{0:T(1024)(128)(4,1)S(1)}, s32[]{:S(2)}) async-start(s8[8388608]{0:T(1024)(128)(4,1)} %bitcast.160), calls=%async_computation.3 | async-start | bytes 8388608 | tf_op jit(solution)/shard_map/while
  155.3 5.9 %slice-start.1 = ((s8[8388608]{0:T(1024)(128)(4,1)}), s8[4194304]{0:T(1024)(128)(4,1)S(1)}, s32[]{:S(2)}) async-start(s8[8388608]{0:T(1024)(128)(4,1)} %bitcast.160), calls=%async_computation.4 | async-start | bytes 8388608 | tf_op jit(solution)/shard_map/while
  175.3 5.9 %slice-start = ((s8[8388608]{0:T(1024)(128)(4,1)}), s8[4194304]{0:T(1024)(128)(4,1)S(1)}, s32[]{:S(2)}) async-start(s8[8388608]{0:T(1024)(128)(4,1)} %bitcast.160), calls=%async_computation.3 | async-start | bytes 8388608 | tf_op jit(solution)/shard_map/while
  175.4 5.9 %slice-start.1 = ((s8[8388608]{0:T(1024)(128)(4,1)}), s8[4194304]{0:T(1024)(128)(4,1)S(1)}, s32[]{:S(2)}) async-start(s8[8388608]{0:T(1024)(128)(4,1)} %bitcast.160), calls=%async_computation.4 | async-start | bytes 8388608 | tf_op jit(solution)/shard_map/while
  195.3 5.9 %slice-start = ((s8[8388608]{0:T(1024)(128)(4,1)}), s8[4194304]{0:T(1024)(128)(4,1)S(1)}, s32[]{:S(2)}) async-start(s8[8388608]{0:T(1024)(128)(4,1)} %bitcast.160), calls=%async_computation.3 | async-start | bytes 8388608 | tf_op jit(solution)/shard_map/while
  195.4 5.9 %slice-start.1 = ((s8[8388608]{0:T(1024)(128)(4,1)}), s8[4194304]{0:T(1024)(128)(4,1)S(1)}, s32[]{:S(2)}) async-start(s8[8388608]{0:T(1024)(128)(4,1)} %bitcast.160), calls=%async_computation.4 | async-start | bytes 8388608 | tf_op jit(solution)/shard_map/while
  215.4 5.9 %slice-start = ((s8[8388608]{0:T(1024)(128)(4,1)}), s8[4194304]{0:T(1024)(128)(4,1)S(1)}, s32[]{:S(2)}) async-start(s8[8388608]{0:T(1024)(128)(4,1)} %bitcast.160), calls=%async_computation.3 | async-start | bytes 8388608 | tf_op jit(solution)/shard_map/while
  215.5 5.9 %slice-start.1 = ((s8[8388608]{0:T(1024)(128)(4,1)}), s8[4194304]{0:T(1024)(128)(4,1)S(1)}, s32[]{:S(2)}) async-start(s8[8388608]{0:T(1024)(128)(4,1)} %bitcast.160), calls=%async_computation.4 | async-start | bytes 8388608 | tf_op jit(solution)/shard_map/while
  235.4 5.9 %slice-start = ((s8[8388608]{0:T(1024)(128)(4,1)}), s8[4194304]{0:T(1024)(128)(4,1)S(1)}, s32[]{:S(2)}) async-start(s8[8388608]{0:T(1024)(128)(4,1)} %bitcast.160), calls=%async_computation.3 | async-start | bytes 8388608 | tf_op jit(solution)/shard_map/while
  235.5 5.9 %slice-start.1 = ((s8[8388608]{0:T(1024)(128)(4,1)}), s8[4194304]{0:T(1024)(128)(4,1)S(1)}, s32[]{:S(2)}) async-start(s8[8388608]{0:T(1024)(128)(4,1)} %bitcast.160), calls=%async_computation.4 | async-start | bytes 8388608 | tf_op jit(solution)/shard_map/while
  245.5 11.9 %copy-start.4 = (s32[8]{0:T(128)S(1)}, s32[8]{0:T(128)}, u32[]{:S(2)}) copy-start(s32[8]{0:T(128)} %param.16) | copy-start | bytes 100
  252.2 19.5 %all-to-all-start.2 = ((f32[4,32,2080]{2,1,0:T(8,128)}), f32[4,32,2080]{2,1,0:T(8,128)S(1)}, u32[]{:S(2)}, u32[]{:S(2)}) async-start(f32[4,32,2080]{2,1,0:T(8,128)} %concatenate.17), calls=%async_computation.2 | async-start | bytes 2228224 | tf_op jit(solution)/shard_map/all_to_all | solution.py:119

commit v2 on v1

v2 whole, which is shorter than its diff:
```python
import functools
import math

import jax
import jax.numpy as jnp
from jax import lax
from jax.experimental import pallas as pl
from jax.experimental.pallas import tpu as pltpu
from jax.sharding import Mesh
from jax.sharding import PartitionSpec as P

NH = 128
KVH = 8
HD = 128


negative_fill = -1e30


def ancestry(parents):
    node_count = parents.shape[1]
    node_ids = jnp.arange(node_count, dtype=jnp.int32)
    linked = jnp.logical_or(
        parents[:, :, None] == node_ids[None, None, :], node_ids[:, None] == node_ids[None, :]
    )
    reached = linked.astype(jnp.bfloat16)
    for doubling in range((node_count - 1).bit_length()):
        squared = jnp.einsum("aij,ajk->aik", reached, reached, preferred_element_type=jnp.float32)
        reached = jnp.minimum(squared, 1.0).astype(jnp.bfloat16)
    return reached


def attend_kernel(
    info_ref, q_ref, k_ref, v_ref, tk_ref, tv_ref, tmask_ref, acc_ref, top_ref, den_ref, *, scale
):
    s = pl.program_id(0)
    length = info_ref[0]
    request = info_ref[1]
    quarter = info_ref[2]
    n_lo = info_ref[3]
    rows = q_ref.shape[0]
    heads = q_ref.shape[1] // HD
    block_len = k_ref.shape[0]
    start = (s * n_lo + quarter) * block_len

    @pl.when(s == 0)
    def _():
        acc_ref[...] = jnp.zeros_like(acc_ref)
        top_ref[...] = jnp.full_like(top_ref, negative_fill)
        den_ref[...] = jnp.zeros_like(den_ref)

    def group(with_tree):
        def head(h, carry):
            col = pl.multiple_of(h * HD, HD)
            qh = q_ref[:, pl.ds(col, HD)]
            sc = (
                lax.dot_general(
                    qh, k_ref[...], (((1,), (1,)), ((), ())), preferred_element_type=jnp.float32
                )
                * scale
            )
            pos = start + lax.broadcasted_iota(jnp.int32, sc.shape, 1)
            live = pos < length
            sc = jnp.where(live, sc, negative_fill)
            peak = jnp.max(sc, axis=1, keepdims=True)
            if with_tree:
                st = (
                    lax.dot_general(
                        qh,
                        tk_ref[...],
                        (((1,), (1,)), ((), ())),
                        preferred_element_type=jnp.float32,
                    )
                    * scale
                )
                tlive = tmask_ref[...] > 0.5
                st = jnp.where(tlive, st, negative_fill)
                peak = jnp.maximum(peak, jnp.max(st, axis=1, keepdims=True))
            w = jnp.where(live, jnp.exp(sc - peak), 0.0)
            tot = jnp.sum(w, axis=1, keepdims=True)
            gs = jnp.dot(w.astype(jnp.bfloat16), v_ref[...], preferred_element_type=jnp.float32)
            if with_tree:
                wt = jnp.where(tlive, jnp.exp(st - peak), 0.0)
                tot = tot + jnp.sum(wt, axis=1, keepdims=True)
                gs = gs + jnp.dot(
                    wt.astype(jnp.bfloat16), tv_ref[...], preferred_element_type=jnp.float32
                )
            floored = jnp.maximum(tot, 1.0)
            part = gs / floored
            lt = peak + jnp.log(floored)
            old = top_ref[h][:, :1]
            new = jnp.maximum(old, lt)
            keep = jnp.exp(old - new)
            add = jnp.exp(lt - new)
            acc_ref[:, pl.ds(col, HD)] = keep * acc_ref[:, pl.ds(col, HD)] + add * part
            den_ref[h] = jnp.broadcast_to(keep * den_ref[h][:, :1] + add, (rows, HD))
            top_ref[h] = jnp.broadcast_to(new, (rows, HD))
            return carry

        lax.fori_loop(0, heads, head, 0)

    @pl.when(s == request)
    def _():
        group(True)

    @pl.when(jnp.logical_and(s != request, start < length))
    def _():
        group(False)


def attend(info, query_block, kv, tree_keys, tree_values, tree_mask, n_groups):
    rows, width = query_block.shape
    heads = width // HD
    block_len = kv.shape[0] // n_groups
    tree_rows = tree_keys.shape[0]
    stats = jax.ShapeDtypeStruct((heads, rows, HD), jnp.float32)
    return pl.pallas_call(
        functools.partial(attend_kernel, scale=1.0 / math.sqrt(HD)),
        out_shape=(jax.ShapeDtypeStruct((rows, width), jnp.float32), stats, stats),
        grid_spec=pltpu.PrefetchScalarGridSpec(
            num_scalar_prefetch=1,
            grid=(n_groups,),
            in_specs=[
                pl.BlockSpec((rows, width), lambda s, info: (0, 0)),
                pl.BlockSpec((block_len, HD), lambda s, info: (s, 0)),
                pl.BlockSpec((block_len, HD), lambda s, info: (s, 1)),
                pl.BlockSpec((tree_rows, HD), lambda s, info: (0, 0)),
                pl.BlockSpec((tree_rows, HD), lambda s, info: (0, 0)),
                pl.BlockSpec((rows, tree_rows), lambda s, info: (0, 0)),
            ],
            out_specs=[
                pl.BlockSpec((rows, width), lambda s, info: (0, 0)),
                pl.BlockSpec((heads, rows, HD), lambda s, info: (0, 0, 0)),
                pl.BlockSpec((heads, rows, HD), lambda s, info: (0, 0, 0)),
            ],
        ),
        compiler_params=pltpu.CompilerParams(dimension_semantics=("arbitrary",)),
    )(info, query_block, kv, kv, tree_keys, tree_values, tree_mask)


def body(
    queries, cache_keys, cache_values, tree_keys, tree_values, parents, tree_sizes, cache_lens
):
    group_size = NH // KVH
    softmax_scale = 1.0 / math.sqrt(HD)
    request = lax.axis_index("rh")
    quarter = lax.axis_index("rl")
    n_lo = lax.axis_size("rl")
    n_hi = lax.axis_size("rh")
    cache_block = cache_keys.shape[1]
    kv_local = cache_keys.shape[2] // HD
    heads_local = kv_local * group_size
    node_count = parents.shape[1]
    rows_owned = tree_keys.shape[0]

    by_head = lax.all_to_all(queries, "head", split_axis=1, concat_axis=0, tiled=True)
    query_block = lax.all_gather(by_head, "rl", axis=0, tiled=True)

    both = jnp.concatenate([cache_keys, cache_values], axis=2)
    mine = lax.all_to_all(both, "rh", split_axis=0, concat_axis=1, tiled=True)[0]

    reached = ancestry(parents)
    ancestors = lax.dynamic_index_in_dim(reached, request, 0, keepdims=False)
    ancestors = lax.dynamic_slice_in_dim(ancestors, quarter * rows_owned, rows_owned, 1)
    tree_mask = ancestors.astype(jnp.float32)
    length = lax.dynamic_index_in_dim(cache_lens, request, 0, keepdims=False)
    info = jnp.stack([length, request, quarter, n_lo]).astype(jnp.int32)
    acc, top, den = attend(info, query_block, mine, tree_keys, tree_values, tree_mask, n_hi)
    top = top[:, :, 0].T
    den = den[:, :, 0].T

    payload = jnp.concatenate([acc, den, top], axis=1).reshape(n_lo, rows_owned, heads_local * HD + 2 * heads_local)
    gathered = lax.all_to_all(payload, "rl", split_axis=0, concat_axis=0, tiled=True)
    got_acc = gathered[:, :, : heads_local * HD].reshape(n_lo, rows_owned, heads_local, HD)
    got_den = gathered[:, :, heads_local * HD : heads_local * HD + heads_local]
    got_top = gathered[:, :, heads_local * HD + heads_local :]
    highest = jnp.max(got_top, axis=0)
    scale = jnp.exp(got_top - highest)
    num = jnp.sum(scale[..., None] * got_acc, axis=0)
    total = jnp.sum(scale * got_den, axis=0)
    merged = (num / total[..., None]).reshape(rows_owned, heads_local * HD)

    row_nodes = quarter * rows_owned + jnp.arange(rows_owned, dtype=jnp.int32)
    live_size = lax.dynamic_index_in_dim(tree_sizes, request, 0, keepdims=False)
    live_rows = row_nodes < live_size
    return jnp.where(live_rows[:, None], merged, 0.0).astype(jnp.bfloat16)


def solution(mesh):
    def run(queries, cache_keys, cache_values, tree_keys, tree_values, parents, tree_sizes, cache_lens):
        n_hi = cache_keys.shape[0]
        n_lo = mesh.shape["req"] // n_hi
        split = Mesh(mesh.devices.reshape(n_hi, n_lo, mesh.shape["head"]), ("rh", "rl", "head"))
        rows = ("rh", "rl")
        placed = (
            P(("rh", "rl", "head"), None),
            P(None, rows, "head"),
            P(None, rows, "head"),
            P(rows, "head"),
            P(rows, "head"),
            P(),
            P(),
            P(),
        )
        return jax.shard_map(
            body, mesh=split, in_specs=placed, out_specs=P(rows, "head"), check_vma=False
        )(queries, cache_keys, cache_values, tree_keys, tree_values, parents, tree_sizes, cache_lens)

    return run
```

time: 275 us -> 181 us (0.66)
  the two profiles are of different devices: /device:TPU:1 before, /device:TPU:12 now
where the time goes in v2:
time: 181 us
  Pallas kernels  81.3 us (45%)
  blocking collectives  44.2 us (24%)
  starting transfers between devices  19.3 us (11%)
  waiting for transfers between devices  18.3 us (10%)
  other arithmetic  8.37 us (5%)
  local copies, waits for them, and re-layouts  7.26 us (4%)
  matrix products  2.02 us (1%)
    pallas_call x1, Pallas kernels, attend(): pl.pallas_call(functools.partial(attend_kernel, scale=1.0 / math.sqrt(HD)...  81.3 us
    all_gather x1, blocking collectives, body(): query_block = lax.all_gather(by_head, 'rl', axis=0, tiled=True)  44.2 us
    all_to_all x1, waiting for transfers between devices, body(): lax.all_to_all(payload, 'rl', split_axis=0, concat_axis=0, tiled=True)  13.9 us
    all_to_all x1, starting transfers between devices, body(): lax.all_to_all(queries, 'head', split_axis=1, concat_axis=0, tiled=True)  8.47 us
    all_to_all x1, starting transfers between devices, body(): lax.all_to_all(both, 'rh', split_axis=0, concat_axis=1, tiled=True)[0]  7.32 us
    concatenate x1, other arithmetic, body(): both = jnp.concatenate([cache_keys, cache_values], axis=2)  4.66 us
    all_to_all x1, waiting for transfers between devices, body(): lax.all_to_all(queries, 'head', split_axis=1, concat_axis=0, tiled=True)  4.43 us
  transfers between devices with their start and end apart: 3, of which 2 were waited for; matrix products, arithmetic and copies ran while one was open for 6% of the time, Pallas kernels for 0%

profile of v2, /device:TPU:12, one launch (start us, length us, event | category | flops | bytes accessed | tf_op | source)
XLA Modules:
  0.0 180.9 jit_solution(10168317069652224022)
XLA Ops:
  0.0 8.5 %all-to-all-start = ((bf16[4,8,2048]{2,0,1:T(4,128)(2,1)}), bf16[4,8,2048]{2,0,1:T(4,128)(2,1)S(1)}, u32[]{:S(2)}, u32[]{:S(2)}) async-start(bf16[4,8,2048]{2,0,1:T(4,128)(2,1)} %bitcast.41), calls=%async_computation | async-start | bytes 262144 | tf_op jit(solution)/shard_map/all_to_all | solution.py:156
  8.5 4.7 %pad_maximum_fusion = bf16[8,1024,256]{2,1,0:T(8,128)(2,1)} fusion(bf16[8,1024,128]{2,1,0:T(8,128)(2,1)} %param.10, bf16[8,1024,128]{2,1,0:T(8,128)(2,1)} %param.9), kind=kLoop, calls=%fused_computation | loop fusion | flops 8388608 | bytes 8388608 | tf_op jit(solution)/shard_map/concatenate | solution.py:159
  13.1 4.4 %all-to-all-done = bf16[4,8,2048]{2,0,1:T(4,128)(2,1)S(1)} async-done(((bf16[4,8,2048]{2,0,1:T(4,128)(2,1)}), bf16[4,8,2048]{2,0,1:T(4,128)(2,1)S(1)}, u32[]{:S(2)}, u32[]{:S(2)}) %all-to-all-start) | async-done | bytes 131104 | tf_op jit(solution)/shard_map/all_to_all | solution.py:156
  17.6 7.3 %all-to-all-start.1 = ((bf16[8,1024,256]{2,1,0:T(8,128)(2,1)}), bf16[8,1024,256]{2,1,0:T(8,128)(2,1)}, u32[]{:S(2)}, u32[]{:S(2)}) async-start(bf16[8,1024,256]{2,1,0:T(8,128)(2,1)} %pad_maximum_fusion), calls=%async_computation.1 | async-start | bytes 8388608 | tf_op jit(solution)/shard_map/all_to_all | solution.py:160
  24.9 0.0 copy-done.2
  24.9 0.6 dynamic_slice.13
  25.5 1.3 pad_add_fusion.info_ref
  26.8 0.0 copy-done.1
  26.8 0.9 fusion.1
  27.8 0.4 fusion.3
  28.2 0.5 fusion.5
  28.7 0.2 fusion.26
  28.9 0.7 fusion.22.tmask_ref
  29.7 44.2 %all_gather.3.q_ref = bf16[128,2048]{1,0:T(8,128)(2,1)} all-gather(bf16[32,2048]{1,0:T(8,128)(2,1)S(1)} %all_to_all.27), channel_id=1, replica_groups=mesh['rh'=8,'rl'=4,'head'=8] {'rl'}, dimensions={0}, use_global_device_ids=true | all-gather | bytes 655360 | tf_op jit(solution)/shard_map/all_gather | solution.py:157
  73.9 0.0 all-to-all-done.1
  73.9 81.3 %shard_map.82 = (f32[128,2048]{1,0:T(8,128)}, f32[16,128,128]{2,1,0:T(8,128)}, f32[16,128,128]{2,1,0:T(8,128)}) custom-call(s32[4]{0:T(128)} %pad_add_fusion.info_ref, bf16[128,2048]{1,0:T(8,128)(2,1)} %all_gather.3.q_ref, bf16[8192,256]{1,0:T(8,128)(2,1)} %bitcast.5.k_ref.v_ref, bf16[8192,256]{1,0:T(8,128)(2,1)} %bitcast.5.k_ref.v_ref, ...), custom_call_target="tpu_custom_call" | custom-call | tf_op jit(solution)/shard_map/pallas_call | solution.py:117
  155.1 2.1 %copy.22 = f32[16,128,1]{0,1,2:T(8,128)S(1)} copy(f32[16,128,1]{2,1,0:T(8,128)} %bitcast.36) | data formatting | bytes 16384 | tf_op jit(solution)/shard_map/squeeze | solution.py:169
  157.3 2.1 %copy.21 = f32[16,128,1]{0,1,2:T(8,128)S(1)} copy(f32[16,128,1]{2,1,0:T(8,128)} %bitcast.35) | data formatting | bytes 16384 | tf_op jit(solution)/shard_map/squeeze | solution.py:170
  159.3 0.0 copy-done
  159.3 1.2 concatenate.7
  160.5 3.5 %all-to-all-start.2 = ((f32[4,32,2080]{2,1,0:T(8,128)}), f32[4,32,2080]{2,1,0:T(8,128)S(1)}, u32[]{:S(2)}, u32[]{:S(2)}) async-start(f32[4,32,2080]{2,1,0:T(8,128)} %bitcast.11), calls=%async_computation.2 | async-start | bytes 2228224 | tf_op jit(solution)/shard_map/all_to_all | solution.py:173
  164.0 0.0 copy-done.3
  164.0 0.6 dynamic_slice.12
  164.6 0.7 add_compare_fusion
  165.3 13.9 %all-to-all-done.2 = f32[4,32,2080]{2,1,0:T(8,128)S(1)} async-done(((f32[4,32,2080]{2,1,0:T(8,128)}), f32[4,32,2080]{2,1,0:T(8,128)S(1)}, u32[]{:S(2)}, u32[]{:S(2)}) %all-to-all-start.2) | async-done | bytes 1064992 | tf_op jit(solution)/shard_map/all_to_all | solution.py:173
  179.2 0.1 slice_reduce_fusion
  179.2 0.1 fusion.19
  179.3 0.3 mul.19
  179.7 0.2 mul.20
  179.9 0.1 fusion.6
  180.0 0.1 div.11
  180.1 0.8 fusion.11
  (6 shorter events, 0.1 us)
Async XLA Ops:
  0.0 17.6 %all-to-all-start = ((bf16[4,8,2048]{2,0,1:T(4,128)(2,1)}), bf16[4,8,2048]{2,0,1:T(4,128)(2,1)S(1)}, u32[]{:S(2)}, u32[]{:S(2)}) async-start(bf16[4,8,2048]{2,0,1:T(4,128)(2,1)} %bitcast.41), calls=%async_computation | async-start | bytes 262144 | tf_op jit(solution)/shard_map/all_to_all | solution.py:156
  13.1 11.8 %copy-start.2 = (s32[8]{0:T(128)S(1)}, s32[8]{0:T(128)}, u32[]{:S(2)}) copy-start(s32[8]{0:T(128)} %param.15) | copy-start | bytes 100
  13.1 13.7 %copy-start.1 = (s32[8,128]{1,0:T(8,128)S(1)}, s32[8,128]{1,0:T(8,128)}, u32[]{:S(2)}) copy-start(s32[8,128]{1,0:T(8,128)} %param.13) | copy-start | bytes 12292
  17.6 56.3 %all-to-all-start.1 = ((bf16[8,1024,256]{2,1,0:T(8,128)(2,1)}), bf16[8,1024,256]{2,1,0:T(8,128)(2,1)}, u32[]{:S(2)}, u32[]{:S(2)}) async-start(bf16[8,1024,256]{2,1,0:T(8,128)(2,1)} %pad_maximum_fusion), calls=%async_computation.1 | async-start | bytes 8388608 | tf_op jit(solution)/shard_map/all_to_all | solution.py:160
  155.1 4.2 %copy-start = (f32[128,2048]{1,0:T(8,128)S(1)}, f32[128,2048]{1,0:T(8,128)}, u32[]{:S(2)}) copy-start(f32[128,2048]{1,0:T(8,128)} %get-tuple-element.8) | copy-start | bytes 3145732
  159.3 4.7 %copy-start.3 = (s32[8]{0:T(128)S(1)}, s32[8]{0:T(128)}, u32[]{:S(2)}) copy-start(s32[8]{0:T(128)} %param.14) | copy-start | bytes 100
  160.5 18.7 %all-to-all-start.2 = ((f32[4,32,2080]{2,1,0:T(8,128)}), f32[4,32,2080]{2,1,0:T(8,128)S(1)}, u32[]{:S(2)}, u32[]{:S(2)}) async-start(f32[4,32,2080]{2,1,0:T(8,128)} %bitcast.11), calls=%async_computation.2 | async-start | bytes 2228224 | tf_op jit(solution)/shard_map/all_to_all | solution.py:173

commit v3 on v2

--- a/solution.py
+++ b/solution.py
@@ -153,8 +153,13 @@
     node_count = parents.shape[1]
     rows_owned = tree_keys.shape[0]
 
-    by_head = lax.all_to_all(queries, "head", split_axis=1, concat_axis=0, tiled=True)
-    query_block = lax.all_gather(by_head, "rl", axis=0, tiled=True)
+    n_head = lax.axis_size("head")
+    width = queries.shape[1] // n_head
+    sliced = queries.reshape(queries.shape[0], n_head, width).transpose(1, 0, 2)
+    sliced = jnp.broadcast_to(sliced[None], (n_lo,) + sliced.shape)
+    sliced = sliced.reshape(n_lo * n_head, queries.shape[0], width)
+    query_block = lax.all_to_all(sliced, ("rl", "head"), split_axis=0, concat_axis=0, tiled=True)
+    query_block = query_block.reshape(node_count, width)
 
     both = jnp.concatenate([cache_keys, cache_values], axis=2)
     mine = lax.all_to_all(both, "rh", split_axis=0, concat_axis=1, tiled=True)[0]

time: 181 us -> 193 us (1.066)
  the two profiles are of different devices: /device:TPU:12 before, /device:TPU:56 now
where the time goes in v3:
time: 193 us; the launch traced here: 192 us
  Pallas kernels  81.3 us (42%)
  waiting for transfers between devices  70.8 us (37%)
  starting transfers between devices  20 us (10%)
  local copies, waits for them, and re-layouts  10.5 us (5%)
  other arithmetic  7.62 us (4%)
  matrix products  2.02 us (1%)
    pallas_call x1, Pallas kernels, attend(): pl.pallas_call(functools.partial(attend_kernel, scale=1.0 / math.sqrt(HD)...  81.3 us
    all_to_all x1, waiting for transfers between devices, body(): lax.all_to_all(both, 'rh', split_axis=0, concat_axis=1, tiled=True)[0]  44 us
    all_to_all x1, waiting for transfers between devices, body(): lax.all_to_all(payload, 'rl', split_axis=0, concat_axis=0, tiled=True)  13.9 us
    all_to_all x1, waiting for transfers between devices, body(): lax.all_to_all(sliced, ('rl', 'head'), split_axis=0, concat_axis=0, tiled...  12.9 us
    all_to_all x1, starting transfers between devices, body(): lax.all_to_all(sliced, ('rl', 'head'), split_axis=0, concat_axis=0, tiled...  9.66 us
    all_to_all x1, starting transfers between devices, body(): lax.all_to_all(both, 'rh', split_axis=0, concat_axis=1, tiled=True)[0]  6.86 us
    concatenate x1, other arithmetic, body(): both = jnp.concatenate([cache_keys, cache_values], axis=2)  4.01 us
  transfers between devices with their start and end apart: 3, of which 3 were waited for; matrix products, arithmetic and copies ran while one was open for 6% of the time, Pallas kernels for 0%

profile of v3, /device:TPU:56, one launch (start us, length us, event | category | flops | bytes accessed | tf_op | source)
XLA Modules:
  0.0 192.4 jit_solution(15797485150631668156)
XLA Ops:
  0.0 1.1 copy.27
  1.1 0.1 copy.14
  1.2 1.0 broadcast_in_dim.11
  2.3 9.7 %all-to-all-start = ((bf16[32,4,2048]{2,1,0:T(4,128)(2,1)}), bf16[32,4,2048]{2,1,0:T(4,128)(2,1)S(1)}, u32[]{:S(2)}, u32[]{:S(2)}) async-start(bf16[32,4,2048]{2,1,0:T(4,128)(2,1)} %bitcast.4), calls=%async_computation | async-start | bytes 1048576 | tf_op jit(solution)/shard_map/all_to_all | solution.py:161
  12.0 4.0 %pad_maximum_fusion = bf16[8,1024,256]{2,1,0:T(8,128)(2,1)} fusion(bf16[8,1024,128]{2,1,0:T(8,128)(2,1)S(1)} %copy-done, bf16[8,1024,128]{2,1,0:T(8,128)(2,1)} %param.9), kind=kLoop, calls=%fused_computation | loop fusion | flops 8388608 | bytes 8388608 | tf_op jit(solution)/shard_map/concatenate | solution.py:164
  16.0 12.9 %all-to-all-done = bf16[32,4,2048]{2,1,0:T(4,128)(2,1)S(1)} async-done(((bf16[32,4,2048]{2,1,0:T(4,128)(2,1)}), bf16[32,4,2048]{2,1,0:T(4,128)(2,1)S(1)}, u32[]{:S(2)}, u32[]{:S(2)}) %all-to-all-start) | async-done | bytes 524320 | tf_op jit(solution)/shard_map/all_to_all | solution.py:161
  28.9 6.9 %all-to-all-start.1 = ((bf16[8,1024,256]{2,1,0:T(8,128)(2,1)}), bf16[8,1024,256]{2,1,0:T(8,128)(2,1)}, u32[]{:S(2)}, u32[]{:S(2)}) async-start(bf16[8,1024,256]{2,1,0:T(8,128)(2,1)} %pad_maximum_fusion), calls=%async_computation.1 | async-start | bytes 8388608 | tf_op jit(solution)/shard_map/all_to_all | solution.py:165
  35.8 0.0 copy-done.3
  35.8 0.6 dynamic_slice.13
  36.4 1.2 pad_add_fusion.info_ref
  37.6 0.9 fusion.1
  38.5 0.4 fusion.3
  39.0 0.5 fusion.5
  39.4 0.2 fusion.26
  39.7 0.7 fusion.22.tmask_ref
  40.4 1.0 reshape.50.q_ref
  41.3 44.0 %all-to-all-done.1 = bf16[8,1024,256]{2,1,0:T(8,128)(2,1)} async-done(((bf16[8,1024,256]{2,1,0:T(8,128)(2,1)}), bf16[8,1024,256]{2,1,0:T(8,128)(2,1)}, u32[]{:S(2)}, u32[]{:S(2)}) %all-to-all-start.1) | async-done | bytes 4194336 | tf_op jit(solution)/shard_map/all_to_all | solution.py:165
  85.4 81.3 %shard_map.82 = (f32[128,2048]{1,0:T(8,128)}, f32[16,128,128]{2,1,0:T(8,128)}, f32[16,128,128]{2,1,0:T(8,128)}) custom-call(s32[4]{0:T(128)} %pad_add_fusion.info_ref, bf16[128,2048]{1,0:T(8,128)(2,1)} %reshape.50.q_ref, bf16[8192,256]{1,0:T(8,128)(2,1)} %bitcast.5.k_ref.v_ref, bf16[8192,256]{1,0:T(8,128)(2,1)} %bitcast.5.k_ref.v_ref, ...), custom_call_target="tpu_custom_call" | custom-call | tf_op jit(solution)/shard_map/pallas_call | solution.py:117
  166.6 2.1 %copy.22 = f32[16,128,1]{0,1,2:T(8,128)S(1)} copy(f32[16,128,1]{2,1,0:T(8,128)} %bitcast.42) | data formatting | bytes 16384 | tf_op jit(solution)/shard_map/squeeze | solution.py:174
  168.8 2.1 %copy.21 = f32[16,128,1]{0,1,2:T(8,128)S(1)} copy(f32[16,128,1]{2,1,0:T(8,128)} %bitcast.41) | data formatting | bytes 16384 | tf_op jit(solution)/shard_map/squeeze | solution.py:175
  170.8 1.2 concatenate.7
  172.0 3.5 %all-to-all-start.2 = ((f32[4,32,2080]{2,1,0:T(8,128)}), f32[4,32,2080]{2,1,0:T(8,128)S(1)}, u32[]{:S(2)}, u32[]{:S(2)}) async-start(f32[4,32,2080]{2,1,0:T(8,128)} %bitcast.11), calls=%async_computation.2 | async-start | bytes 2228224 | tf_op jit(solution)/shard_map/all_to_all | solution.py:178
  175.5 0.6 dynamic_slice.12
  176.1 0.7 add_compare_fusion
  176.8 13.9 %all-to-all-done.2 = f32[4,32,2080]{2,1,0:T(8,128)S(1)} async-done(((f32[4,32,2080]{2,1,0:T(8,128)}), f32[4,32,2080]{2,1,0:T(8,128)S(1)}, u32[]{:S(2)}, u32[]{:S(2)}) %all-to-all-start.2) | async-done | bytes 1064992 | tf_op jit(solution)/shard_map/all_to_all | solution.py:178
  190.7 0.1 slice_reduce_fusion
  190.7 0.1 fusion.19
  190.8 0.3 mul.19
  191.2 0.2 mul.20
  191.3 0.1 fusion.6
  191.5 0.1 div.11
  191.6 0.8 fusion.11
  (10 shorter events, 0.0 us)
Async XLA Ops:
  0.0 12.0 %copy-start = (bf16[8,1024,128]{2,1,0:T(8,128)(2,1)S(1)}, bf16[8,1024,128]{2,1,0:T(8,128)(2,1)}, u32[]{:S(2)}) copy-start(bf16[8,1024,128]{2,1,0:T(8,128)(2,1)} %param.10) | copy-start | bytes 6291460
  2.3 26.6 %all-to-all-start = ((bf16[32,4,2048]{2,1,0:T(4,128)(2,1)}), bf16[32,4,2048]{2,1,0:T(4,128)(2,1)S(1)}, u32[]{:S(2)}, u32[]{:S(2)}) async-start(bf16[32,4,2048]{2,1,0:T(4,128)(2,1)} %bitcast.4), calls=%async_computation | async-start | bytes 1048576 | tf_op jit(solution)/shard_map/all_to_all | solution.py:161
  16.0 19.8 %copy-start.3 = (s32[8]{0:T(128)S(1)}, s32[8]{0:T(128)}, u32[]{:S(2)}) copy-start(s32[8]{0:T(128)} %param.15) | copy-start | bytes 100
  16.0 21.6 %copy-start.2 = (s32[8,128]{1,0:T(8,128)S(1)}, s32[8,128]{1,0:T(8,128)}, u32[]{:S(2)}) copy-start(s32[8,128]{1,0:T(8,128)} %param.13) | copy-start | bytes 12292
  28.9 56.5 %all-to-all-start.1 = ((bf16[8,1024,256]{2,1,0:T(8,128)(2,1)}), bf16[8,1024,256]{2,1,0:T(8,128)(2,1)}, u32[]{:S(2)}, u32[]{:S(2)}) async-start(bf16[8,1024,256]{2,1,0:T(8,128)(2,1)} %pad_maximum_fusion), calls=%async_computation.1 | async-start | bytes 8388608 | tf_op jit(solution)/shard_map/all_to_all | solution.py:165
  166.6 4.2 %copy-start.1 = (f32[128,2048]{1,0:T(8,128)S(1)}, f32[128,2048]{1,0:T(8,128)}, u32[]{:S(2)}) copy-start(f32[128,2048]{1,0:T(8,128)} %get-tuple-element.8) | copy-start | bytes 3145732
  170.8 4.7 %copy-start.4 = (s32[8]{0:T(128)S(1)}, s32[8]{0:T(128)}, u32[]{:S(2)}) copy-start(s32[8]{0:T(128)} %param.14) | copy-start | bytes 100
  172.0 18.7 %all-to-all-start.2 = ((f32[4,32,2080]{2,1,0:T(8,128)}), f32[4,32,2080]{2,1,0:T(8,128)S(1)}, u32[]{:S(2)}, u32[]{:S(2)}) async-start(f32[4,32,2080]{2,1,0:T(8,128)} %bitcast.11), calls=%async_computation.2 | async-start | bytes 2228224 | tf_op jit(solution)/shard_map/all_to_all | solution.py:178

commit v4 on v3

--- a/solution.py
+++ b/solution.py
@@ -31,17 +31,19 @@
 
 
 def attend_kernel(
-    info_ref, q_ref, k_ref, v_ref, tk_ref, tv_ref, tmask_ref, acc_ref, top_ref, den_ref, *, scale
+    info_ref, q_ref, kt_ref, v_ref, tkt_ref, tv_ref, tmask_ref, acc_ref, top_ref, den_ref, *, scale
 ):
     s = pl.program_id(0)
     length = info_ref[0]
     request = info_ref[1]
     quarter = info_ref[2]
     n_lo = info_ref[3]
+    live_nodes = info_ref[4]
     rows = q_ref.shape[0]
     heads = q_ref.shape[1] // HD
-    block_len = k_ref.shape[0]
+    block_len = kt_ref.shape[1]
     start = (s * n_lo + quarter) * block_len
+    full = start + block_len <= length
 
     @pl.when(s == 0)
     def _():
@@ -49,34 +51,24 @@
         top_ref[...] = jnp.full_like(top_ref, negative_fill)
         den_ref[...] = jnp.zeros_like(den_ref)
 
-    def group(with_tree):
+    def group(with_tree, masked, count):
         def head(h, carry):
             col = pl.multiple_of(h * HD, HD)
-            qh = q_ref[:, pl.ds(col, HD)]
-            sc = (
-                lax.dot_general(
-                    qh, k_ref[...], (((1,), (1,)), ((), ())), preferred_element_type=jnp.float32
-                )
-                * scale
-            )
-            pos = start + lax.broadcasted_iota(jnp.int32, sc.shape, 1)
-            live = pos < length
-            sc = jnp.where(live, sc, negative_fill)
+            qh = q_ref[:count, pl.ds(col, HD)]
+            sc = jnp.dot(qh, kt_ref[...], preferred_element_type=jnp.float32) * scale
+            if masked:
+                pos = start + lax.broadcasted_iota(jnp.int32, sc.shape, 1)
+                live = pos < length
+                sc = jnp.where(live, sc, negative_fill)
             peak = jnp.max(sc, axis=1, keepdims=True)
             if with_tree:
-                st = (
-                    lax.dot_general(
-                        qh,
-                        tk_ref[...],
-                        (((1,), (1,)), ((), ())),
-                        preferred_element_type=jnp.float32,
-                    )
-                    * scale
-                )
-                tlive = tmask_ref[...] > 0.5
+                st = jnp.dot(qh, tkt_ref[...], preferred_element_type=jnp.float32) * scale
+                tlive = tmask_ref[:count, :] > 0.5
                 st = jnp.where(tlive, st, negative_fill)
                 peak = jnp.maximum(peak, jnp.max(st, axis=1, keepdims=True))
-            w = jnp.where(live, jnp.exp(sc - peak), 0.0)
+            w = jnp.exp(sc - peak)
+            if masked:
+                w = jnp.where(live, w, 0.0)
             tot = jnp.sum(w, axis=1, keepdims=True)
             gs = jnp.dot(w.astype(jnp.bfloat16), v_ref[...], preferred_element_type=jnp.float32)
             if with_tree:
@@ -88,31 +80,37 @@
             floored = jnp.maximum(tot, 1.0)
             part = gs / floored
             lt = peak + jnp.log(floored)
-            old = top_ref[h][:, :1]
+            old = top_ref[h, :count, :][:, :1]
             new = jnp.maximum(old, lt)
             keep = jnp.exp(old - new)
             add = jnp.exp(lt - new)
-            acc_ref[:, pl.ds(col, HD)] = keep * acc_ref[:, pl.ds(col, HD)] + add * part
-            den_ref[h] = jnp.broadcast_to(keep * den_ref[h][:, :1] + add, (rows, HD))
-            top_ref[h] = jnp.broadcast_to(new, (rows, HD))
+            acc_ref[:count, pl.ds(col, HD)] = (
+                keep * acc_ref[:count, pl.ds(col, HD)] + add * part
+            )
+            den_ref[h, :count, :] = jnp.broadcast_to(
+                keep * den_ref[h, :count, :][:, :1] + add, (count, HD)
+            )
+            top_ref[h, :count, :] = jnp.broadcast_to(new, (count, HD))
             return carry
 
         lax.fori_loop(0, heads, head, 0)
 
-    @pl.when(s == request)
-    def _():
-        group(True)
-
-    @pl.when(jnp.logical_and(s != request, start < length))
-    def _():
-        group(False)
-
-
-def attend(info, query_block, kv, tree_keys, tree_values, tree_mask, n_groups):
+    half = rows // 2
+    for with_tree in (True, False):
+        mine = s == request if with_tree else jnp.logical_and(s != request, start < length)
+        for masked in (False, True):
+            case = jnp.logical_and(mine, jnp.logical_not(full) if masked else full)
+            for count in (half, rows):
+                few = live_nodes <= half
+                pick = jnp.logical_and(case, few if count == half else jnp.logical_not(few))
+                pl.when(pick)(functools.partial(group, with_tree, masked, count))
+
+
+def attend(info, query_block, keys_t, values, tree_keys_t, tree_values, tree_mask):
     rows, width = query_block.shape
     heads = width // HD
-    block_len = kv.shape[0] // n_groups
-    tree_rows = tree_keys.shape[0]
+    n_groups, _, block_len = keys_t.shape
+    tree_rows = tree_values.shape[0]
     stats = jax.ShapeDtypeStruct((heads, rows, HD), jnp.float32)
     return pl.pallas_call(
         functools.partial(attend_kernel, scale=1.0 / math.sqrt(HD)),
@@ -122,9 +120,9 @@
             grid=(n_groups,),
             in_specs=[
                 pl.BlockSpec((rows, width), lambda s, info: (0, 0)),
-                pl.BlockSpec((block_len, HD), lambda s, info: (s, 0)),
-                pl.BlockSpec((block_len, HD), lambda s, info: (s, 1)),
-                pl.BlockSpec((tree_rows, HD), lambda s, info: (0, 0)),
+                pl.BlockSpec((None, HD, block_len), lambda s, info: (s, 0, 0)),
+                pl.BlockSpec((None, block_len, HD), lambda s, info: (s, 0, 0)),
+                pl.BlockSpec((HD, tree_rows), lambda s, info: (0, 0)),
                 pl.BlockSpec((tree_rows, HD), lambda s, info: (0, 0)),
                 pl.BlockSpec((rows, tree_rows), lambda s, info: (0, 0)),
             ],
@@ -135,7 +133,7 @@
             ],
         ),
         compiler_params=pltpu.CompilerParams(dimension_semantics=("arbitrary",)),
-    )(info, query_block, kv, kv, tree_keys, tree_values, tree_mask)
+    )(info, query_block, keys_t, values, tree_keys_t, tree_values, tree_mask)
 
 
 def body(
@@ -169,8 +167,12 @@
     ancestors = lax.dynamic_slice_in_dim(ancestors, quarter * rows_owned, rows_owned, 1)
     tree_mask = ancestors.astype(jnp.float32)
     length = lax.dynamic_index_in_dim(cache_lens, request, 0, keepdims=False)
-    info = jnp.stack([length, request, quarter, n_lo]).astype(jnp.int32)
-    acc, top, den = attend(info, query_block, mine, tree_keys, tree_values, tree_mask, n_hi)
+    live_size = lax.dynamic_index_in_dim(tree_sizes, request, 0, keepdims=False)
+    info = jnp.stack([length, request, quarter, n_lo, live_size]).astype(jnp.int32)
+    mine = mine.reshape(n_hi, cache_block, 2 * HD)
+    keys_t = mine[:, :, :HD].transpose(0, 2, 1)
+    values = mine[:, :, HD:]
+    acc, top, den = attend(info, query_block, keys_t, values, tree_keys.T, tree_values, tree_mask)
     top = top[:, :, 0].T
     den = den[:, :, 0].T
 
@@ -186,7 +188,6 @@
     merged = (num / total[..., None]).reshape(rows_owned, heads_local * HD)
 
     row_nodes = quarter * rows_owned + jnp.arange(rows_owned, dtype=jnp.int32)
-    live_size = lax.dynamic_index_in_dim(tree_sizes, request, 0, keepdims=False)
     live_rows = row_nodes < live_size
     return jnp.where(live_rows[:, None], merged, 0.0).astype(jnp.bfloat16)
 

time: 193 us -> 184 us (0.953)
  the two profiles are of different devices: /device:TPU:56 before, /device:TPU:40 now
where the time goes in v4:
time: 184 us
  waiting for transfers between devices  69.7 us (38%)
  Pallas kernels  65.7 us (36%)
  starting transfers between devices  20.3 us (11%)
  local copies, waits for them, and re-layouts  19.4 us (11%)
  other arithmetic  6.36 us (3%)
  matrix products  2.01 us (1%)
    pallas_call x1, Pallas kernels, attend(): pl.pallas_call(functools.partial(attend_kernel, scale=1.0 / math.sqrt(HD)...  65.7 us
    all_to_all x1, waiting for transfers between devices, body(): lax.all_to_all(both, 'rh', split_axis=0, concat_axis=1, tiled=True)[0]  42.2 us
    all_to_all x1, waiting for transfers between devices, body(): lax.all_to_all(payload, 'rl', split_axis=0, concat_axis=0, tiled=True)  14.6 us
    all_to_all x1, waiting for transfers between devices, body(): lax.all_to_all(sliced, ('rl', 'head'), split_axis=0, concat_axis=0, tiled...  12.9 us
    all_to_all x1, starting transfers between devices, body(): lax.all_to_all(sliced, ('rl', 'head'), split_axis=0, concat_axis=0, tiled...  9.66 us
    all_to_all x1, starting transfers between devices, body(): lax.all_to_all(both, 'rh', split_axis=0, concat_axis=1, tiled=True)[0]  7.08 us
    concatenate x1, other arithmetic, body(): both = jnp.concatenate([cache_keys, cache_values], axis=2)  4.02 us
    slice x1, local copies, waits for them, and re-layouts, body(): values = mine[:, :, HD:]  3.91 us
  transfers between devices with their start and end apart: 3, of which 3 were waited for; matrix products, arithmetic and copies ran while one was open for 7% of the time, Pallas kernels for 0%

profile of v4, /device:TPU:40, one launch (start us, length us, event | category | flops | bytes accessed | tf_op | source)
XLA Modules:
  0.0 183.5 jit_solution(16133236470659559917)
XLA Ops:
  0.0 1.1 copy.31
  1.1 0.1 copy.16
  1.2 1.0 broadcast_in_dim.11
  2.3 9.7 %all-to-all-start = ((bf16[32,4,2048]{2,1,0:T(4,128)(2,1)}), bf16[32,4,2048]{2,1,0:T(4,128)(2,1)S(1)}, u32[]{:S(2)}, u32[]{:S(2)}) async-start(bf16[32,4,2048]{2,1,0:T(4,128)(2,1)} %bitcast.4), calls=%async_computation | async-start | bytes 1048576 | tf_op jit(solution)/shard_map/all_to_all | solution.py:159
  12.0 4.0 %pad_maximum_fusion = bf16[8,1024,256]{2,1,0:T(8,128)(2,1)} fusion(bf16[8,1024,128]{2,1,0:T(8,128)(2,1)S(1)} %copy-done, bf16[8,1024,128]{2,1,0:T(8,128)(2,1)} %param.9), kind=kLoop, calls=%fused_computation | loop fusion | flops 8388608 | bytes 8388608 | tf_op jit(solution)/shard_map/concatenate | solution.py:162
  16.0 12.9 %all-to-all-done = bf16[32,4,2048]{2,1,0:T(4,128)(2,1)S(1)} async-done(((bf16[32,4,2048]{2,1,0:T(4,128)(2,1)}), bf16[32,4,2048]{2,1,0:T(4,128)(2,1)S(1)}, u32[]{:S(2)}, u32[]{:S(2)}) %all-to-all-start) | async-done | bytes 524320 | tf_op jit(solution)/shard_map/all_to_all | solution.py:159
  28.9 7.1 %all-to-all-start.1 = ((bf16[8,1024,256]{2,1,0:T(8,128)(2,1)}), bf16[8,1024,256]{2,1,0:T(8,128)(2,1)}, u32[]{:S(2)}, u32[]{:S(2)}) async-start(bf16[8,1024,256]{2,1,0:T(8,128)(2,1)} %pad_maximum_fusion), calls=%async_computation.1 | async-start | bytes 8388608 | tf_op jit(solution)/shard_map/all_to_all | solution.py:163
  36.0 0.6 dynamic_slice.12
  36.6 0.6 dynamic_slice.13
  37.2 0.7 copy.17
  37.9 1.8 stack.13.info_ref
  39.7 0.9 fusion.1
  40.6 0.4 fusion.3
  41.0 0.4 fusion.5
  41.5 0.2 fusion.27
  41.7 0.7 fusion.22.tmask_ref
  42.4 1.0 reshape.50.q_ref
  43.4 42.2 %all-to-all-done.1 = bf16[8,1024,256]{2,1,0:T(8,128)(2,1)} async-done(((bf16[8,1024,256]{2,1,0:T(8,128)(2,1)}), bf16[8,1024,256]{2,1,0:T(8,128)(2,1)}, u32[]{:S(2)}, u32[]{:S(2)}) %all-to-all-start.1) | async-done | bytes 4194336 | tf_op jit(solution)/shard_map/all_to_all | solution.py:163
  85.6 3.9 %fusion.26 = (bf16[8,1024,128]{2,1,0:T(8,128)(2,1)}, bf16[8,128,1024]{1,2,0:T(8,128)(2,1)S(1)}) fusion(bf16[8,1024,256]{2,1,0:T(8,128)(2,1)} %all-to-all-done.1), kind=kLoop, calls=%fused_computation.40 | loop fusion | bytes 8388608 | tf_op jit(solution)/shard_map/slice | solution.py:174
  89.5 2.6 %copy.20.kt_ref = bf16[8,128,1024]{2,1,0:T(8,128)(2,1)} copy(bf16[8,128,1024]{1,2,0:T(8,128)(2,1)S(1)} %get-tuple-element.14) | data formatting | bytes 4194304 | tf_op jit(solution)/shard_map/transpose | solution.py:173
  92.1 65.7 %shard_map.82 = (f32[128,2048]{1,0:T(8,128)}, f32[16,128,128]{2,1,0:T(8,128)}, f32[16,128,128]{2,1,0:T(8,128)}) custom-call(s32[5]{0:T(128)} %stack.13.info_ref, bf16[128,2048]{1,0:T(8,128)(2,1)} %reshape.50.q_ref, bf16[8,128,1024]{2,1,0:T(8,128)(2,1)} %copy.20.kt_ref, bf16[8,1024,128]{2,1,0:T(8,128)(2,1)} %get-tuple-element.13.v_ref, ...), custom_call_target="tpu_custom_call" | custom-call | tf_op jit(solution)/shard_map/pallas_call | solution.py:115
  157.8 2.1 %copy.26 = f32[16,128,1]{0,1,2:T(8,128)S(1)} copy(f32[16,128,1]{2,1,0:T(8,128)} %bitcast.44) | data formatting | bytes 16384 | tf_op jit(solution)/shard_map/squeeze | solution.py:176
  159.9 2.1 %copy.25 = f32[16,128,1]{0,1,2:T(8,128)S(1)} copy(f32[16,128,1]{2,1,0:T(8,128)} %bitcast.43) | data formatting | bytes 16384 | tf_op jit(solution)/shard_map/squeeze | solution.py:177
  162.0 1.2 concatenate.7
  163.1 3.5 %all-to-all-start.2 = ((f32[4,32,2080]{2,1,0:T(8,128)}), f32[4,32,2080]{2,1,0:T(8,128)S(1)}, u32[]{:S(2)}, u32[]{:S(2)}) async-start(f32[4,32,2080]{2,1,0:T(8,128)} %bitcast.12), calls=%async_computation.2 | async-start | bytes 2228224 | tf_op jit(solution)/shard_map/all_to_all | solution.py:180
  166.7 0.6 add_compare_fusion
  167.2 14.6 %all-to-all-done.2 = f32[4,32,2080]{2,1,0:T(8,128)S(1)} async-done(((f32[4,32,2080]{2,1,0:T(8,128)}), f32[4,32,2080]{2,1,0:T(8,128)S(1)}, u32[]{:S(2)}, u32[]{:S(2)}) %all-to-all-start.2) | async-done | bytes 1064992 | tf_op jit(solution)/shard_map/all_to_all | solution.py:180
  182.0 0.3 mul.19
  182.3 0.2 mul.20
  182.5 0.1 fusion.6
  182.6 0.1 div.11
  182.7 0.8 fusion.11
  (15 shorter events, 0.2 us)
Async XLA Ops:
  0.0 12.0 %copy-start = (bf16[8,1024,128]{2,1,0:T(8,128)(2,1)S(1)}, bf16[8,1024,128]{2,1,0:T(8,128)(2,1)}, u32[]{:S(2)}) copy-start(bf16[8,1024,128]{2,1,0:T(8,128)(2,1)} %param.10) | copy-start | bytes 6291460
  2.3 26.6 %all-to-all-start = ((bf16[32,4,2048]{2,1,0:T(4,128)(2,1)}), bf16[32,4,2048]{2,1,0:T(4,128)(2,1)S(1)}, u32[]{:S(2)}, u32[]{:S(2)}) async-start(bf16[32,4,2048]{2,1,0:T(4,128)(2,1)} %bitcast.4), calls=%async_computation | async-start | bytes 1048576 | tf_op jit(solution)/shard_map/all_to_all | solution.py:159
  16.0 20.0 %copy-start.4 = (s32[8]{0:T(128)S(1)}, s32[8]{0:T(128)}, u32[]{:S(2)}) copy-start(s32[8]{0:T(128)} %param.14) | copy-start | bytes 100
  16.0 20.6 %copy-start.5 = (s32[8]{0:T(128)S(1)}, s32[8]{0:T(128)}, u32[]{:S(2)}) copy-start(s32[8]{0:T(128)} %param.15) | copy-start | bytes 100
  16.0 21.2 %copy-start.2 = (bf16[32,128]{1,0:T(8,128)(2,1)S(1)}, bf16[32,128]{1,0:T(8,128)(2,1)}, u32[]{:S(2)}) copy-start(bf16[32,128]{1,0:T(8,128)(2,1)} %param.11) | copy-start | bytes 24580
  16.0 23.7 %copy-start.3 = (s32[8,128]{1,0:T(8,128)S(1)}, s32[8,128]{1,0:T(8,128)}, u32[]{:S(2)}) copy-start(s32[8,128]{1,0:T(8,128)} %param.13) | copy-start | bytes 12292
  28.9 56.7 %all-to-all-start.1 = ((bf16[8,1024,256]{2,1,0:T(8,128)(2,1)}), bf16[8,1024,256]{2,1,0:T(8,128)(2,1)}, u32[]{:S(2)}, u32[]{:S(2)}) async-start(bf16[8,1024,256]{2,1,0:T(8,128)(2,1)} %pad_maximum_fusion), calls=%async_computation.1 | async-start | bytes 8388608 | tf_op jit(solution)/shard_map/all_to_all | solution.py:163
  157.8 4.2 %copy-start.1 = (f32[128,2048]{1,0:T(8,128)S(1)}, f32[128,2048]{1,0:T(8,128)}, u32[]{:S(2)}) copy-start(f32[128,2048]{1,0:T(8,128)} %get-tuple-element.8) | copy-start | bytes 3145732
  163.1 18.7 %all-to-all-start.2 = ((f32[4,32,2080]{2,1,0:T(8,128)}), f32[4,32,2080]{2,1,0:T(8,128)S(1)}, u32[]{:S(2)}, u32[]{:S(2)}) async-start(f32[4,32,2080]{2,1,0:T(8,128)} %bitcast.12), calls=%async_computation.2 | async-start | bytes 2228224 | tf_op jit(solution)/shard_map/all_to_all | solution.py:180

commit v5 on v4

--- a/solution.py
+++ b/solution.py
@@ -30,28 +30,22 @@
     return reached
 
 
-def attend_kernel(
-    info_ref, q_ref, kt_ref, v_ref, tkt_ref, tv_ref, tmask_ref, acc_ref, top_ref, den_ref, *, scale
+def group_kernel(
+    info_ref, q_ref, kt_ref, v_ref, tkt_ref, tv_ref, tmask_ref, part_ref, lt_ref, *, scale, own
 ):
-    s = pl.program_id(0)
     length = info_ref[0]
     request = info_ref[1]
     quarter = info_ref[2]
     n_lo = info_ref[3]
     live_nodes = info_ref[4]
+    s = info_ref[5]
     rows = q_ref.shape[0]
     heads = q_ref.shape[1] // HD
     block_len = kt_ref.shape[1]
     start = (s * n_lo + quarter) * block_len
     full = start + block_len <= length
 
-    @pl.when(s == 0)
-    def _():
-        acc_ref[...] = jnp.zeros_like(acc_ref)
-        top_ref[...] = jnp.full_like(top_ref, negative_fill)
-        den_ref[...] = jnp.zeros_like(den_ref)
-
-    def group(with_tree, masked, count):
+    def compute(with_tree, masked, count):
         def head(h, carry):
             col = pl.multiple_of(h * HD, HD)
             qh = q_ref[:count, pl.ds(col, HD)]
@@ -78,61 +72,44 @@
                     wt.astype(jnp.bfloat16), tv_ref[...], preferred_element_type=jnp.float32
                 )
             floored = jnp.maximum(tot, 1.0)
-            part = gs / floored
-            lt = peak + jnp.log(floored)
-            old = top_ref[h, :count, :][:, :1]
-            new = jnp.maximum(old, lt)
-            keep = jnp.exp(old - new)
-            add = jnp.exp(lt - new)
-            acc_ref[:count, pl.ds(col, HD)] = (
-                keep * acc_ref[:count, pl.ds(col, HD)] + add * part
-            )
-            den_ref[h, :count, :] = jnp.broadcast_to(
-                keep * den_ref[h, :count, :][:, :1] + add, (count, HD)
-            )
-            top_ref[h, :count, :] = jnp.broadcast_to(new, (count, HD))
+            part_ref[:count, pl.ds(col, HD)] = gs / floored
+            lt_ref[h, :count, :] = jnp.broadcast_to(peak + jnp.log(floored), (count, HD))
             return carry
 
         lax.fori_loop(0, heads, head, 0)
+        if count < rows:
+            part_ref[count:, :] = jnp.zeros((rows - count, part_ref.shape[1]), jnp.float32)
+            lt_ref[:, count:, :] = jnp.full((heads, rows - count, HD), negative_fill, jnp.float32)
 
     half = rows // 2
-    for with_tree in (True, False):
-        mine = s == request if with_tree else jnp.logical_and(s != request, start < length)
-        for masked in (False, True):
-            case = jnp.logical_and(mine, jnp.logical_not(full) if masked else full)
-            for count in (half, rows):
-                few = live_nodes <= half
-                pick = jnp.logical_and(case, few if count == half else jnp.logical_not(few))
-                pl.when(pick)(functools.partial(group, with_tree, masked, count))
-
-
-def attend(info, query_block, keys_t, values, tree_keys_t, tree_values, tree_mask):
+    mine = True if own else start < length
+    for masked in (False, True):
+        case = jnp.logical_and(mine, jnp.logical_not(full) if masked else full)
+        for count in (half, rows):
+            few = live_nodes <= half
+            pick = jnp.logical_and(case, few if count == half else jnp.logical_not(few))
+            pl.when(pick)(functools.partial(compute, own, masked, count))
+
+    if not own:
+
+        @pl.when(start >= length)
+        def _():
+            part_ref[...] = jnp.zeros_like(part_ref)
+            lt_ref[...] = jnp.full_like(lt_ref, negative_fill)
+
+
+def attend_group(info, query_block, keys_t, values, tree_keys_t, tree_values, tree_mask, own):
     rows, width = query_block.shape
     heads = width // HD
-    n_groups, _, block_len = keys_t.shape
-    tree_rows = tree_values.shape[0]
-    stats = jax.ShapeDtypeStruct((heads, rows, HD), jnp.float32)
+    vmem = pl.BlockSpec(memory_space=pltpu.VMEM)
     return pl.pallas_call(
-        functools.partial(attend_kernel, scale=1.0 / math.sqrt(HD)),
-        out_shape=(jax.ShapeDtypeStruct((rows, width), jnp.float32), stats, stats),
-        grid_spec=pltpu.PrefetchScalarGridSpec(
-            num_scalar_prefetch=1,
-            grid=(n_groups,),
-            in_specs=[
-                pl.BlockSpec((rows, width), lambda s, info: (0, 0)),
-                pl.BlockSpec((None, HD, block_len), lambda s, info: (s, 0, 0)),
-                pl.BlockSpec((None, block_len, HD), lambda s, info: (s, 0, 0)),
-                pl.BlockSpec((HD, tree_rows), lambda s, info: (0, 0)),
-                pl.BlockSpec((tree_rows, HD), lambda s, info: (0, 0)),
-                pl.BlockSpec((rows, tree_rows), lambda s, info: (0, 0)),
-            ],
-            out_specs=[
-                pl.BlockSpec((rows, width), lambda s, info: (0, 0)),
-                pl.BlockSpec((heads, rows, HD), lambda s, info: (0, 0, 0)),
-                pl.BlockSpec((heads, rows, HD), lambda s, info: (0, 0, 0)),
-            ],
+        functools.partial(group_kernel, scale=1.0 / math.sqrt(HD), own=own),
+        out_shape=(
+            jax.ShapeDtypeStruct((rows, width), jnp.float32),
+            jax.ShapeDtypeStruct((heads, rows, HD), jnp.float32),
         ),
-        compiler_params=pltpu.CompilerParams(dimension_semantics=("arbitrary",)),
+        in_specs=[pl.BlockSpec(memory_space=pltpu.SMEM)] + [vmem] * 6,
+        out_specs=(vmem, vmem),
     )(info, query_block, keys_t, values, tree_keys_t, tree_values, tree_mask)
 
 
@@ -159,22 +136,51 @@
     query_block = lax.all_to_all(sliced, ("rl", "head"), split_axis=0, concat_axis=0, tiled=True)
     query_block = query_block.reshape(node_count, width)
 
-    both = jnp.concatenate([cache_keys, cache_values], axis=2)
-    mine = lax.all_to_all(both, "rh", split_axis=0, concat_axis=1, tiled=True)[0]
-
     reached = ancestry(parents)
     ancestors = lax.dynamic_index_in_dim(reached, request, 0, keepdims=False)
     ancestors = lax.dynamic_slice_in_dim(ancestors, quarter * rows_owned, rows_owned, 1)
     tree_mask = ancestors.astype(jnp.float32)
     length = lax.dynamic_index_in_dim(cache_lens, request, 0, keepdims=False)
     live_size = lax.dynamic_index_in_dim(tree_sizes, request, 0, keepdims=False)
-    info = jnp.stack([length, request, quarter, n_lo, live_size]).astype(jnp.int32)
-    mine = mine.reshape(n_hi, cache_block, 2 * HD)
-    keys_t = mine[:, :, :HD].transpose(0, 2, 1)
-    values = mine[:, :, HD:]
-    acc, top, den = attend(info, query_block, keys_t, values, tree_keys.T, tree_values, tree_mask)
-    top = top[:, :, 0].T
-    den = den[:, :, 0].T
+    keys_t = cache_keys.transpose(0, 2, 1)
+    tree_keys_t = tree_keys.T
+
+    def run_group(s, block_keys_t, block_values, own):
+        info = jnp.stack([length, request, quarter, n_lo, live_size, s]).astype(jnp.int32)
+        part, lt = attend_group(
+            info, query_block, block_keys_t, block_values, tree_keys_t, tree_values, tree_mask, own
+        )
+        return part, lt[:, :, 0].T
+
+    results = [
+        run_group(
+            request,
+            lax.dynamic_index_in_dim(keys_t, request, 0, keepdims=False),
+            lax.dynamic_index_in_dim(cache_values, request, 0, keepdims=False),
+            True,
+        )
+    ]
+    for shift in range(1, n_hi):
+        target = (request + shift) % n_hi
+        pairs = [(i, (i + shift) % n_hi) for i in range(n_hi)]
+        got_keys_t, got_values = lax.ppermute(
+            (
+                lax.dynamic_index_in_dim(keys_t, target, 0, keepdims=False),
+                lax.dynamic_index_in_dim(cache_values, target, 0, keepdims=False),
+            ),
+            "rh",
+            pairs,
+        )
+        results.append(run_group((request - shift) % n_hi, got_keys_t, got_values, False))
+
+    parts = jnp.stack([r[0] for r in results])
+    lts = jnp.stack([r[1] for r in results])
+    top = jnp.max(lts, axis=0)
+    weights = jnp.exp(lts - top)
+    den = jnp.sum(weights, axis=0)
+    acc = jnp.sum(
+        jnp.repeat(weights, HD, axis=2) * parts, axis=0
+    )
 
     payload = jnp.concatenate([acc, den, top], axis=1).reshape(n_lo, rows_owned, heads_local * HD + 2 * heads_local)
     gathered = lax.all_to_all(payload, "rl", split_axis=0, concat_axis=0, tiled=True)

time: 184 us -> 199 us (1.082)
  the two profiles are of different devices: /device:TPU:40 before, /device:TPU:12 now
where the time goes in v5:
time: 199 us; the launch traced here: 198 us
  Pallas kernels  80.6 us (41%)
  local copies, waits for them, and re-layouts  47.6 us (24%)
  starting transfers between devices  43.3 us (22%)
  waiting for transfers between devices  14.5 us (7%)
  matrix products  6.16 us (3%)
  other arithmetic  5.09 us (3%)
    pallas_call x8, Pallas kernels, attend_group(): pl.pallas_call(functools.partial(group_kernel, scale=1.0 / math.sqrt(HD),...  80.6 us
    ppermute x14, starting transfers between devices, body(): lax.ppermute((lax.dynamic_index_in_dim(keys_t, target, 0, keepdims=False)...  30.3 us
    another operation x8, local copies, waits for them, and re-layouts, run_group(): jnp.stack([length, request, quarter, n_lo, live_size, s]).astype(jnp.int32)  15.4 us
    all_to_all x1, waiting for transfers between devices, body(): lax.all_to_all(payload, 'rl', split_axis=0, concat_axis=0, tiled=True)  14.5 us
    unnamed x64, local copies, waits for them, and re-layouts  13.6 us
    all_to_all x1, starting transfers between devices, body(): lax.all_to_all(sliced, ('rl', 'head'), split_axis=0, concat_axis=0, tiled...  9.49 us
    slice x4, local copies, waits for them, and re-layouts, run_group(): return (part, lt[:, :, 0].T)  8.59 us
    dot_general x4, matrix products, ancestry(): jnp.einsum('aij,ajk->aik', reached, reached, preferred_element_type=jnp.f...  6.16 us
  transfers between devices with their start and end apart: 16, of which 1 were waited for; matrix products, arithmetic and copies ran while one was open for 20% of the time, Pallas kernels for 35%

profile of v5, /device:TPU:12, one launch (start us, length us, event | category | flops | bytes accessed | tf_op | source)
XLA Modules:
  0.0 198.0 jit_solution(1275453129100867525)
XLA Ops:
  0.1 2.5 %dynamic-slice_bitcast_fusion = (bf16[1024,128]{1,0:T(8,128)(2,1)}, bf16[1024,128]{1,0:T(8,128)(2,1)S(1)}, bf16[1024,128]{1,0:T(8,128)(2,1)}, bf16[1024,128]{1,0...) fusion(bf16[8,1024,128]{2,1,0:T(8,128)(2,1)} %param.10, ...), kind=kLoop, calls=%fused_computation.36 | loop fusion | bytes 4194336 | tf_op jit(solution)/shard_map/jit(dynamic_index_in_dim)/squeeze | solution.py:169
  5.6 3.0 %collective-permute-start.10 = (bf16[128,1024]{1,0:T(8,128)(2,1)}, bf16[128,1024]{1,0:T(8,128)(2,1)}, u32[]{:S(2)}, u32[]{:S(2)}) collective-permute-start(bf16[128,1024]{1,0:T(8,128)(2,1)} %bitcast.45), channel_id=1, source_target_pairs={{0,192},{32,224},{64,0},{96,32},{128,64},{160,96},{192,128},{224,1... | collective-permute-start | bytes 786440 | tf_op jit(solution)/shard_map/ppermute | solution.py:166
  9.9 9.5 %all-to-all-start = ((bf16[32,4,2048]{2,1,0:T(4,128)(2,1)}), bf16[32,4,2048]{2,1,0:T(4,128)(2,1)S(1)}, u32[]{:S(2)}, u32[]{:S(2)}) async-start(bf16[32,4,2048]{2,1,0:T(4,128)(2,1)} %bitcast.4), calls=%async_computation | async-start | bytes 1048576 | tf_op jit(solution)/shard_map/all_to_all | solution.py:136
  21.1 2.9 %collective-permute-start.12 = (bf16[128,1024]{1,0:T(8,128)(2,1)}, bf16[128,1024]{1,0:T(8,128)(2,1)}, u32[]{:S(2)}, u32[]{:S(2)}) collective-permute-start(bf16[128,1024]{1,0:T(8,128)(2,1)} %bitcast.202), channel_id=1, source_target_pairs={{0,224},{32,0},{64,32},{96,64},{128,96},{160,128},{192,160},{224,1... | collective-permute-start | bytes 786440 | tf_op jit(solution)/shard_map/ppermute | solution.py:166
  25.7 2.5 %fusion.3 = bf16[8,128,128]{2,1,0:T(8,128)(2,1)} fusion(bf16[8,128,128]{2,1,0:T(8,128)(2,1)} %fusion.1), kind=kOutput, calls=%fused_computation.10 | convolution fusion | flops 67633152 | bytes 524288 | tf_op jit(solution)/shard_map/aij,ajk->aik/dot_general | solution.py:28
  31.4 1.9 stack.138.info_ref
  33.3 1.9 stack.156.info_ref
  35.9 2.0 stack.159.info_ref
  38.7 1.9 stack.150.info_ref
  40.8 1.9 stack.153.info_ref
  42.9 1.9 stack.144.info_ref
  45.0 2.0 stack.147.info_ref
  47.1 1.9 stack.141.info_ref
  50.1 3.6 %collective-permute-start.6 = (bf16[128,1024]{1,0:T(8,128)(2,1)}, bf16[128,1024]{1,0:T(8,128)(2,1)}, u32[]{:S(2)}, u32[]{:S(2)}) collective-permute-start(bf16[128,1024]{1,0:T(8,128)(2,1)} %bitcast.207), channel_id=1, source_target_pairs={{0,128},{32,160},{64,192},{96,224},{128,0},{160,32},{192,64},{224,... | collective-permute-start | bytes 786440 | tf_op jit(solution)/shard_map/ppermute | solution.py:166
  54.4 5.1 %collective-permute-start.8 = (bf16[128,1024]{1,0:T(8,128)(2,1)S(1)}, bf16[128,1024]{1,0:T(8,128)(2,1)}, u32[]{:S(2)}, u32[]{:S(2)}) collective-permute-start(bf16[128,1024]{1,0:T(8,128)(2,1)S(1)} %bitcast.206), channel_id=1, source_target_pairs={{0,160},{32,192},{64,224},{96,0},{128,32},{160,64},{192,96},{224,1... | collective-permute-start | bytes 786440 | tf_op jit(solution)/shard_map/ppermute | solution.py:166
  61.1 10.9 %shard_map.88 = (f32[128,2048]{1,0:T(8,128)}, f32[16,128,128]{2,1,0:T(8,128)}) custom-call(s32[6]{0:T(128)} %stack.156.info_ref, bf16[128,2048]{1,0:T(8,128)(2,1)} %reshape.126.q_ref, bf16[128,1024]{1,0:T(8,128)(2,1)} %collective-permute-done.10.kt_ref, bf16[1024,128]{1,0:T(8,128)(2,1)} %collective-permute-done.11.v_ref, bf16[128,32]{1,0:T(8,128)(2,1)} %bitcast.181, ...), custom_call_target="tpu_custom_call" | custom-call | tf_op jit(solution)/shard_map/pallas_call | solution.py:105
  72.0 10.9 %shard_map.89 = (f32[128,2048]{1,0:T(8,128)}, f32[16,128,128]{2,1,0:T(8,128)}) custom-call(s32[6]{0:T(128)} %stack.159.info_ref, bf16[128,2048]{1,0:T(8,128)(2,1)} %reshape.126.q_ref, bf16[128,1024]{1,0:T(8,128)(2,1)} %collective-permute-done.12.kt_ref, bf16[1024,128]{1,0:T(8,128)(2,1)} %collective-permute-done.13.v_ref, bf16[128,32]{1,0:T(8,128)(2,1)} %bitcast.182, ...), custom_call_target="tpu_custom_call" | custom-call | tf_op jit(solution)/shard_map/pallas_call | solution.py:105
  82.9 2.1 %slice_reduce_fusion = (f32[16,128]{1,0:T(8,128)S(1)}, f32[16,128]{1,0:T(8,128)S(1)}) fusion(f32[16,128,128]{2,1,0:T(8,128)} %get-tuple-element.28, f32[16,128,128]{2,1,0:T(8,128)} %get-tuple-element.27), kind=kLoop, calls=%fused_computation.23 | loop fusion | bytes 32768 | tf_op jit(solution)/shard_map/slice | solution.py:153
  85.1 3.6 %collective-permute-start.3 = (bf16[1024,128]{1,0:T(8,128)(2,1)S(1)}, bf16[1024,128]{1,0:T(8,128)(2,1)S(1)}, u32[]{:S(2)}, u32[]{:S(2)}) collective-permute-start(bf16[1024,128]{1,0:T(8,128)(2,1)S(1)} %get-tuple-element.45), channel_id=1, source_target_pairs={{0,64},{32,96},{64,128},{96,160},{128,192},{160,224},{192,0},{224,... | collective-permute-start | bytes 786440 | tf_op jit(solution)/shard_map/ppermute | solution.py:166
  88.7 2.7 %shard_map.86 = (f32[128,2048]{1,0:T(8,128)}, f32[16,128,128]{2,1,0:T(8,128)}) custom-call(s32[6]{0:T(128)} %stack.150.info_ref, bf16[128,2048]{1,0:T(8,128)(2,1)} %reshape.126.q_ref, bf16[128,1024]{1,0:T(8,128)(2,1)} %collective-permute-done.6.kt_ref, bf16[1024,128]{1,0:T(8,128)(2,1)} %collective-permute-done.7.v_ref, bf16[128,32]{1,0:T(8,128)(2,1)} %bitcast.183, ...), custom_call_target="tpu_custom_call" | custom-call | tf_op jit(solution)/shard_map/pallas_call | solution.py:105
  91.5 9.4 %collective-permute-start.5 = (bf16[1024,128]{1,0:T(8,128)(2,1)S(1)}, bf16[1024,128]{1,0:T(8,128)(2,1)S(1)}, u32[]{:S(2)}, u32[]{:S(2)}) collective-permute-start(bf16[1024,128]{1,0:T(8,128)(2,1)S(1)} %get-tuple-element.44), channel_id=1, source_target_pairs={{0,96},{32,128},{64,160},{96,192},{128,224},{160,0},{192,32},{224,... | collective-permute-start | bytes 786440 | tf_op jit(solution)/shard_map/ppermute | solution.py:166
  100.9 11.0 %shard_map.87 = (f32[128,2048]{1,0:T(8,128)}, f32[16,128,128]{2,1,0:T(8,128)}) custom-call(s32[6]{0:T(128)} %stack.153.info_ref, bf16[128,2048]{1,0:T(8,128)(2,1)} %reshape.126.q_ref, bf16[128,1024]{1,0:T(8,128)(2,1)} %collective-permute-done.8.kt_ref, bf16[1024,128]{1,0:T(8,128)(2,1)} %copy-done.5, bf16[128,32]{1,0:T(8,128)(2,1)} %bitcast.184, ...), custom_call_target="tpu_custom_call" | custom-call | tf_op jit(solution)/shard_map/pallas_call | solution.py:105
  111.9 2.1 %slice_reduce_fusion.2 = (f32[16,128]{1,0:T(8,128)S(1)}, f32[16,128]{1,0:T(8,128)S(1)}) fusion(f32[16,128,128]{2,1,0:T(8,128)} %get-tuple-element.26, f32[16,128,128]{2,1,0:T(8,128)} %get-tuple-element.25), kind=kLoop, calls=%fused_computation.25 | loop fusion | bytes 32768 | tf_op jit(solution)/shard_map/slice | solution.py:153
  114.1 12.1 %shard_map.82 = (f32[128,2048]{1,0:T(8,128)}, f32[16,128,128]{2,1,0:T(8,128)}) custom-call(s32[6]{0:T(128)} %stack.138.info_ref, bf16[128,2048]{1,0:T(8,128)(2,1)} %reshape.126.q_ref, bf16[128,1024]{1,0:T(8,128)(2,1)} %bitcast.198, bf16[1024,128]{1,0:T(8,128)(2,1)} %get-tuple-element.47.v_ref, bf16[128,32]{1,0:T(8,128)(2,1)} %bitcast.185, ...), custom_call_target="tpu_custom_call" | custom-call | tf_op jit(solution)/shard_map/pallas_call | solution.py:105
  127.6 11.2 %shard_map.83 = (f32[128,2048]{1,0:T(8,128)}, f32[16,128,128]{2,1,0:T(8,128)}) custom-call(s32[6]{0:T(128)} %stack.141.info_ref, bf16[128,2048]{1,0:T(8,128)(2,1)} %reshape.126.q_ref, bf16[128,1024]{1,0:T(8,128)(2,1)} %copy-done.9, bf16[1024,128]{1,0:T(8,128)(2,1)} %copy-done.6, bf16[128,32]{1,0:T(8,128)(2,1)} %bitcast.186, bf16[32,128]{1,0:T(8,128)(2,1)} %tv_ref.15, ...), custom_call_target="tpu_custom_call" | custom-call | tf_op jit(solution)/shard_map/pallas_call | solution.py:105
  138.8 2.1 %slice_reduce_fusion.6 = (f32[16,128]{1,0:T(8,128)S(1)}, f32[16,128]{1,0:T(8,128)S(1)}) fusion(f32[16,128,128]{2,1,0:T(8,128)} %get-tuple-element.22, f32[16,128,128]{2,1,0:T(8,128)} %get-tuple-element.21), kind=kLoop, calls=%fused_computation.29 | loop fusion | bytes 32768 | tf_op jit(solution)/shard_map/slice | solution.py:153
  141.7 10.9 %shard_map.84 = (f32[128,2048]{1,0:T(8,128)}, f32[16,128,128]{2,1,0:T(8,128)}) custom-call(s32[6]{0:T(128)} %stack.144.info_ref, bf16[128,2048]{1,0:T(8,128)(2,1)} %reshape.126.q_ref, bf16[128,1024]{1,0:T(8,128)(2,1)} %collective-permute-done.2.kt_ref, bf16[1024,128]{1,0:T(8,128)(2,1)} %copy-done.7, bf16[128,32]{1,0:T(8,128)(2,1)} %bitcast.187, ...), custom_call_target="tpu_custom_call" | custom-call | tf_op jit(solution)/shard_map/pallas_call | solution.py:105
  154.0 10.9 %shard_map.85 = (f32[128,2048]{1,0:T(8,128)}, f32[16,128,128]{2,1,0:T(8,128)}) custom-call(s32[6]{0:T(128)} %stack.147.info_ref, bf16[128,2048]{1,0:T(8,128)(2,1)} %reshape.126.q_ref, bf16[128,1024]{1,0:T(8,128)(2,1)} %copy-done.10, bf16[1024,128]{1,0:T(8,128)(2,1)} %copy-done.8, bf16[128,32]{1,0:T(8,128)(2,1)} %bitcast.188, bf16[32,128]{1,0:T(8,128)(2,1)} %tv_ref.15, ...), custom_call_target="tpu_custom_call" | custom-call | tf_op jit(solution)/shard_map/pallas_call | solution.py:105
  164.9 2.1 %slice_reduce_fusion.4 = (f32[16,128]{1,0:T(8,128)S(1)}, f32[16,128]{1,0:T(8,128)S(1)}) fusion(f32[16,128,128]{2,1,0:T(8,128)} %get-tuple-element.24, f32[16,128,128]{2,1,0:T(8,128)} %get-tuple-element.23), kind=kLoop, calls=%fused_computation.27 | loop fusion | bytes 32768 | tf_op jit(solution)/shard_map/slice | solution.py:153
  173.6 2.7 %multiply_reduce_fusion = f32[128,16,128]{2,1,0:T(8,128)S(1)} fusion(f32[8,128,16,128]{3,2,1,0:T(8,128)S(1)} %bitcast_dynamic-update-slice_fusion, f32[8,128,16]{2,1,0:T(8,128)S(1)} %copy.207), kind=kLoop, calls=%fused_computation | loop fusion | flops 3932160 | bytes 9502720 | tf_op jit(solution)/shard_map/reduce_sum | solution.py:181
  177.7 3.5 %all-to-all-start.1 = ((f32[4,32,2080]{2,1,0:T(8,128)}), f32[4,32,2080]{2,1,0:T(8,128)S(1)}, u32[]{:S(2)}, u32[]{:S(2)}) async-start(f32[4,32,2080]{2,1,0:T(8,128)} %concatenate.11), calls=%async_computation.1 | async-start | bytes 2228224 | tf_op jit(solution)/shard_map/all_to_all | solution.py:186
  181.8 14.5 %all-to-all-done.1 = f32[4,32,2080]{2,1,0:T(8,128)S(1)} async-done(((f32[4,32,2080]{2,1,0:T(8,128)}), f32[4,32,2080]{2,1,0:T(8,128)S(1)}, u32[]{:S(2)}, u32[]{:S(2)}) %all-to-all-start.1) | async-done | bytes 1064992 | tf_op jit(solution)/shard_map/all_to_all | solution.py:186
  (115 shorter events, 29.8 us)
Async XLA Ops:
  0.0 8.7 %copy-start.11 = (bf16[4,16384]{1,0:T(4,128)(2,1)S(1)}, bf16[4,16384]{1,0:T(4,128)(2,1)}, u32[]{:S(2)}) copy-start(bf16[4,16384]{1,0:T(4,128)(2,1)} %param.8) | copy-start | bytes 393220
  0.0 24.0 %copy-start.13 = (s32[8,128]{1,0:T(8,128)S(1)}, s32[8,128]{1,0:T(8,128)}, u32[]{:S(2)}) copy-start(s32[8,128]{1,0:T(8,128)} %param.13) | copy-start | bytes 12292
  0.0 30.1 %copy-start.14 = (s32[8]{0:T(128)S(1)}, s32[8]{0:T(128)}, u32[]{:S(2)}) copy-start(s32[8]{0:T(128)} %param.14) | copy-start | bytes 100
  0.0 30.8 %copy-start.15 = (s32[8]{0:T(128)S(1)}, s32[8]{0:T(128)}, u32[]{:S(2)}) copy-start(s32[8]{0:T(128)} %param.15) | copy-start | bytes 100
  0.0 35.2 %copy-start.12 = (bf16[32,128]{1,0:T(8,128)(2,1)S(1)}, bf16[32,128]{1,0:T(8,128)(2,1)}, u32[]{:S(2)}) copy-start(bf16[32,128]{1,0:T(8,128)(2,1)} %param.11) | copy-start | bytes 24580
  2.7 47.4 %collective-permute-start.11 = (bf16[1024,128]{1,0:T(8,128)(2,1)}, bf16[1024,128]{1,0:T(8,128)(2,1)}, u32[]{:S(2)}, u32[]{:S(2)}) collective-permute-start(bf16[1024,128]{1,0:T(8,128)(2,1)} %get-tuple-element.48), channel_id=1, source_target_pairs={{0,192},{32,224},{64,0},{96,32},{128,64},{160,96},{192,128},{224,1... | collective-permute-start | bytes 786440 | tf_op jit(solution)/shard_map/ppermute | solution.py:166
  5.6 48.0 %collective-permute-start.10 = (bf16[128,1024]{1,0:T(8,128)(2,1)}, bf16[128,1024]{1,0:T(8,128)(2,1)}, u32[]{:S(2)}, u32[]{:S(2)}) collective-permute-start(bf16[128,1024]{1,0:T(8,128)(2,1)} %bitcast.45), channel_id=1, source_target_pairs={{0,192},{32,224},{64,0},{96,32},{128,64},{160,96},{192,128},{224,1... | collective-permute-start | bytes 786440 | tf_op jit(solution)/shard_map/ppermute | solution.py:166
  9.9 50.3 %all-to-all-start = ((bf16[32,4,2048]{2,1,0:T(4,128)(2,1)}), bf16[32,4,2048]{2,1,0:T(4,128)(2,1)S(1)}, u32[]{:S(2)}, u32[]{:S(2)}) async-start(bf16[32,4,2048]{2,1,0:T(4,128)(2,1)} %bitcast.4), calls=%async_computation | async-start | bytes 1048576 | tf_op jit(solution)/shard_map/all_to_all | solution.py:136
  19.4 35.0 %collective-permute-start.13 = (bf16[1024,128]{1,0:T(8,128)(2,1)}, bf16[1024,128]{1,0:T(8,128)(2,1)}, u32[]{:S(2)}, u32[]{:S(2)}) collective-permute-start(bf16[1024,128]{1,0:T(8,128)(2,1)} %get-tuple-element.41), channel_id=1, source_target_pairs={{0,224},{32,0},{64,32},{96,64},{128,96},{160,128},{192,160},{224,1... | collective-permute-start | bytes 786440 | tf_op jit(solution)/shard_map/ppermute | solution.py:166
  21.1 50.9 %collective-permute-start.12 = (bf16[128,1024]{1,0:T(8,128)(2,1)}, bf16[128,1024]{1,0:T(8,128)(2,1)}, u32[]{:S(2)}, u32[]{:S(2)}) collective-permute-start(bf16[128,1024]{1,0:T(8,128)(2,1)} %bitcast.202), channel_id=1, source_target_pairs={{0,224},{32,0},{64,32},{96,64},{128,96},{160,128},{192,160},{224,1... | collective-permute-start | bytes 786440 | tf_op jit(solution)/shard_map/ppermute | solution.py:166
  24.0 58.9 %collective-permute-start.7 = (bf16[1024,128]{1,0:T(8,128)(2,1)}, bf16[1024,128]{1,0:T(8,128)(2,1)}, u32[]{:S(2)}, u32[]{:S(2)}) collective-permute-start(bf16[1024,128]{1,0:T(8,128)(2,1)} %get-tuple-element.43), channel_id=1, source_target_pairs={{0,128},{32,160},{64,192},{96,224},{128,0},{160,32},{192,64},{224,... | collective-permute-start | bytes 786440 | tf_op jit(solution)/shard_map/ppermute | solution.py:166
  50.1 35.0 %collective-permute-start.6 = (bf16[128,1024]{1,0:T(8,128)(2,1)}, bf16[128,1024]{1,0:T(8,128)(2,1)}, u32[]{:S(2)}, u32[]{:S(2)}) collective-permute-start(bf16[128,1024]{1,0:T(8,128)(2,1)} %bitcast.207), channel_id=1, source_target_pairs={{0,128},{32,160},{64,192},{96,224},{128,0},{160,32},{192,64},{224,... | collective-permute-start | bytes 786440 | tf_op jit(solution)/shard_map/ppermute | solution.py:166
  53.7 37.7 %collective-permute-start.9 = (bf16[1024,128]{1,0:T(8,128)(2,1)S(1)}, bf16[1024,128]{1,0:T(8,128)(2,1)S(1)}, u32[]{:S(2)}, u32[]{:S(2)}) collective-permute-start(bf16[1024,128]{1,0:T(8,128)(2,1)S(1)} %get-tuple-element.42), channel_id=1, source_target_pairs={{0,160},{32,192},{64,224},{96,0},{128,32},{160,64},{192,96},{224,1... | collective-permute-start | bytes 786440 | tf_op jit(solution)/shard_map/ppermute | solution.py:166
  54.4 37.1 %collective-permute-start.8 = (bf16[128,1024]{1,0:T(8,128)(2,1)S(1)}, bf16[128,1024]{1,0:T(8,128)(2,1)}, u32[]{:S(2)}, u32[]{:S(2)}) collective-permute-start(bf16[128,1024]{1,0:T(8,128)(2,1)S(1)} %bitcast.206), channel_id=1, source_target_pairs={{0,160},{32,192},{64,224},{96,0},{128,32},{160,64},{192,96},{224,1... | collective-permute-start | bytes 786440 | tf_op jit(solution)/shard_map/ppermute | solution.py:166
  72.0 54.1 %collective-permute-start.1 = (bf16[1024,128]{1,0:T(8,128)(2,1)S(1)}, bf16[1024,128]{1,0:T(8,128)(2,1)S(1)}, u32[]{:S(2)}, u32[]{:S(2)}) collective-permute-start(bf16[1024,128]{1,0:T(8,128)(2,1)S(1)} %get-tuple-element.46), channel_id=1, source_target_pairs={{0,32},{32,64},{64,96},{96,128},{128,160},{160,192},{192,224},{224... | collective-permute-start | bytes 786440 | tf_op jit(solution)/shard_map/ppermute | solution.py:166
  82.9 43.7 %collective-permute-start = (bf16[128,1024]{1,0:T(8,128)(2,1)S(1)}, bf16[128,1024]{1,0:T(8,128)(2,1)S(1)}, u32[]{:S(2)}, u32[]{:S(2)}) collective-permute-start(bf16[128,1024]{1,0:T(8,128)(2,1)S(1)} %bitcast.205), channel_id=1, source_target_pairs={{0,32},{32,64},{64,96},{96,128},{128,160},{160,192},{192,224},{224... | collective-permute-start | bytes 786440 | tf_op jit(solution)/shard_map/ppermute | solution.py:166
  85.1 55.8 %collective-permute-start.3 = (bf16[1024,128]{1,0:T(8,128)(2,1)S(1)}, bf16[1024,128]{1,0:T(8,128)(2,1)S(1)}, u32[]{:S(2)}, u32[]{:S(2)}) collective-permute-start(bf16[1024,128]{1,0:T(8,128)(2,1)S(1)} %get-tuple-element.45), channel_id=1, source_target_pairs={{0,64},{32,96},{64,128},{96,160},{128,192},{160,224},{192,0},{224,... | collective-permute-start | bytes 786440 | tf_op jit(solution)/shard_map/ppermute | solution.py:166
  91.4 9.5 %copy-start.5 = (bf16[1024,128]{1,0:T(8,128)(2,1)}, bf16[1024,128]{1,0:T(8,128)(2,1)S(1)}, u32[]{:S(2)}) copy-start(bf16[1024,128]{1,0:T(8,128)(2,1)S(1)} %collective-permute-done.9.v_ref) | copy-start | bytes 786436
  91.4 49.5 %collective-permute-start.2 = (bf16[128,1024]{1,0:T(8,128)(2,1)S(1)}, bf16[128,1024]{1,0:T(8,128)(2,1)}, u32[]{:S(2)}, u32[]{:S(2)}) collective-permute-start(bf16[128,1024]{1,0:T(8,128)(2,1)S(1)} %bitcast.204), channel_id=1, source_target_pairs={{0,64},{32,96},{64,128},{96,160},{128,192},{160,224},{192,0},{224,... | collective-permute-start | bytes 786440 | tf_op jit(solution)/shard_map/ppermute | solution.py:166
  91.5 61.1 %collective-permute-start.5 = (bf16[1024,128]{1,0:T(8,128)(2,1)S(1)}, bf16[1024,128]{1,0:T(8,128)(2,1)S(1)}, u32[]{:S(2)}, u32[]{:S(2)}) collective-permute-start(bf16[1024,128]{1,0:T(8,128)(2,1)S(1)} %get-tuple-element.44), channel_id=1, source_target_pairs={{0,96},{32,128},{64,160},{96,192},{128,224},{160,0},{192,32},{224,... | collective-permute-start | bytes 786440 | tf_op jit(solution)/shard_map/ppermute | solution.py:166
  126.1 0.7 copy-start.6
  126.1 26.4 %collective-permute-start.4 = (bf16[128,1024]{1,0:T(8,128)(2,1)S(1)}, bf16[128,1024]{1,0:T(8,128)(2,1)S(1)}, u32[]{:S(2)}, u32[]{:S(2)}) collective-permute-start(bf16[128,1024]{1,0:T(8,128)(2,1)S(1)} %bitcast.203), channel_id=1, source_target_pairs={{0,96},{32,128},{64,160},{96,192},{128,224},{160,0},{192,32},{224,... | collective-permute-start | bytes 786440 | tf_op jit(solution)/shard_map/ppermute | solution.py:166
  126.9 0.7 copy-start.9
  140.9 31.3 %copy-start.2 = (f32[128,2048]{1,0:T(8,128)S(1)}, f32[128,2048]{1,0:T(8,128)}, u32[]{:S(2)}) copy-start(f32[128,2048]{1,0:T(8,128)} %get-tuple-element.33) | copy-start | bytes 3145732
  140.9 0.7 copy-start.7
  152.6 0.7 copy-start.8
  153.3 0.7 copy-start.10
  167.1 5.5 %copy-start = (f32[128,2048]{1,0:T(8,128)S(1)}, f32[128,2048]{1,0:T(8,128)}, u32[]{:S(2)}) copy-start(f32[128,2048]{1,0:T(8,128)} %get-tuple-element.35) | copy-start | bytes 3145732
  167.5 4.5 %copy-start.4 = (f32[128,2048]{1,0:T(8,128)S(1)}, f32[128,2048]{1,0:T(8,128)}, u32[]{:S(2)}) copy-start(f32[128,2048]{1,0:T(8,128)} %get-tuple-element.32) | copy-start | bytes 3145732
  167.5 4.9 %copy-start.3 = (f32[128,2048]{1,0:T(8,128)S(1)}, f32[128,2048]{1,0:T(8,128)}, u32[]{:S(2)}) copy-start(f32[128,2048]{1,0:T(8,128)} %get-tuple-element.34) | copy-start | bytes 3145732
  167.5 5.3 %copy-start.1 = (f32[128,2048]{1,0:T(8,128)S(1)}, f32[128,2048]{1,0:T(8,128)}, u32[]{:S(2)}) copy-start(f32[128,2048]{1,0:T(8,128)} %get-tuple-element.36) | copy-start | bytes 3145732
  177.7 18.7 %all-to-all-start.1 = ((f32[4,32,2080]{2,1,0:T(8,128)}), f32[4,32,2080]{2,1,0:T(8,128)S(1)}, u32[]{:S(2)}, u32[]{:S(2)}) async-start(f32[4,32,2080]{2,1,0:T(8,128)} %concatenate.11), calls=%async_computation.1 | async-start | bytes 2228224 | tf_op jit(solution)/shard_map/all_to_all | solution.py:186

commit v6 on v5

--- a/solution.py
+++ b/solution.py
@@ -31,14 +31,16 @@
 
 
 def group_kernel(
-    info_ref, q_ref, kt_ref, v_ref, tkt_ref, tv_ref, tmask_ref, part_ref, lt_ref, *, scale, own
+    info_ref, q_ref, kt_ref, v_ref, tkt_ref, tv_ref, tmask_ref, part_ref, lt_ref, *, scale, shift
 ):
+    own = shift == 0
     length = info_ref[0]
     request = info_ref[1]
     quarter = info_ref[2]
     n_lo = info_ref[3]
     live_nodes = info_ref[4]
-    s = info_ref[5]
+    n_hi = info_ref[5]
+    s = lax.rem(request - shift + n_hi, n_hi)
     rows = q_ref.shape[0]
     heads = q_ref.shape[1] // HD
     block_len = kt_ref.shape[1]
@@ -46,7 +48,7 @@
     full = start + block_len <= length
 
     def compute(with_tree, masked, count):
-        def head(h, carry):
+        def head(h, lts):
             col = pl.multiple_of(h * HD, HD)
             qh = q_ref[:count, pl.ds(col, HD)]
             sc = jnp.dot(qh, kt_ref[...], preferred_element_type=jnp.float32) * scale
@@ -73,13 +75,16 @@
                 )
             floored = jnp.maximum(tot, 1.0)
             part_ref[:count, pl.ds(col, HD)] = gs / floored
-            lt_ref[h, :count, :] = jnp.broadcast_to(peak + jnp.log(floored), (count, HD))
-            return carry
-
-        lax.fori_loop(0, heads, head, 0)
+            lane = lax.broadcasted_iota(jnp.int32, lts.shape, 1)
+            return jnp.where(lane == h, peak + jnp.log(floored), lts)
+
+        lts = lax.fori_loop(
+            0, heads, head, jnp.full((count, HD), negative_fill, jnp.float32)
+        )
+        lt_ref[:count, :] = lts
         if count < rows:
             part_ref[count:, :] = jnp.zeros((rows - count, part_ref.shape[1]), jnp.float32)
-            lt_ref[:, count:, :] = jnp.full((heads, rows - count, HD), negative_fill, jnp.float32)
+            lt_ref[count:, :] = jnp.full((rows - count, HD), negative_fill, jnp.float32)
 
     half = rows // 2
     mine = True if own else start < length
@@ -98,15 +103,15 @@
             lt_ref[...] = jnp.full_like(lt_ref, negative_fill)
 
 
-def attend_group(info, query_block, keys_t, values, tree_keys_t, tree_values, tree_mask, own):
+def attend_group(info, query_block, keys_t, values, tree_keys_t, tree_values, tree_mask, shift):
     rows, width = query_block.shape
     heads = width // HD
     vmem = pl.BlockSpec(memory_space=pltpu.VMEM)
     return pl.pallas_call(
-        functools.partial(group_kernel, scale=1.0 / math.sqrt(HD), own=own),
+        functools.partial(group_kernel, scale=1.0 / math.sqrt(HD), shift=shift),
         out_shape=(
             jax.ShapeDtypeStruct((rows, width), jnp.float32),
-            jax.ShapeDtypeStruct((heads, rows, HD), jnp.float32),
+            jax.ShapeDtypeStruct((rows, HD), jnp.float32),
         ),
         in_specs=[pl.BlockSpec(memory_space=pltpu.SMEM)] + [vmem] * 6,
         out_specs=(vmem, vmem),
@@ -145,19 +150,20 @@
     keys_t = cache_keys.transpose(0, 2, 1)
     tree_keys_t = tree_keys.T
 
-    def run_group(s, block_keys_t, block_values, own):
-        info = jnp.stack([length, request, quarter, n_lo, live_size, s]).astype(jnp.int32)
+    info = jnp.stack([length, request, quarter, n_lo, live_size, n_hi]).astype(jnp.int32)
+
+    def run_group(shift, block_keys_t, block_values):
         part, lt = attend_group(
-            info, query_block, block_keys_t, block_values, tree_keys_t, tree_values, tree_mask, own
-        )
-        return part, lt[:, :, 0].T
-
+            info, query_block, block_keys_t, block_values, tree_keys_t, tree_values, tree_mask, shift
+        )
+        return part, lt[:, :heads_local]
+
+    query_block, keys_t, values_all = lax.optimization_barrier((query_block, keys_t, cache_values))
     results = [
         run_group(
-            request,
+            0,
             lax.dynamic_index_in_dim(keys_t, request, 0, keepdims=False),
-            lax.dynamic_index_in_dim(cache_values, request, 0, keepdims=False),
-            True,
+            lax.dynamic_index_in_dim(values_all, request, 0, keepdims=False),
         )
     ]
     for shift in range(1, n_hi):
@@ -166,12 +172,12 @@
         got_keys_t, got_values = lax.ppermute(
             (
                 lax.dynamic_index_in_dim(keys_t, target, 0, keepdims=False),
-                lax.dynamic_index_in_dim(cache_values, target, 0, keepdims=False),
+                lax.dynamic_index_in_dim(values_all, target, 0, keepdims=False),
             ),
             "rh",
             pairs,
         )
-        results.append(run_group((request - shift) % n_hi, got_keys_t, got_values, False))
+        results.append(run_group(shift, got_keys_t, got_values))
 
     parts = jnp.stack([r[0] for r in results])
     lts = jnp.stack([r[1] for r in results])

time: 199 us -> 254 us (1.28)
  the two profiles are of different devices: /device:TPU:12 before, /device:TPU:36 now
where the time goes in v6:
time: 254 us; the launch traced here: 252 us
  Pallas kernels  85.9 us (34%)
  local copies, waits for them, and re-layouts  53.7 us (21%)
  starting transfers between devices  51.5 us (20%)
  waiting for transfers between devices  46.3 us (18%)
  other arithmetic  10.4 us (4%)
  matrix products  4.17 us (2%)
    pallas_call x8, Pallas kernels, attend_group(): pl.pallas_call(functools.partial(group_kernel, scale=1.0 / math.sqrt(HD),...  85.9 us
    ppermute x14, starting transfers between devices, body(): lax.ppermute((lax.dynamic_index_in_dim(keys_t, target, 0, keepdims=False)...  38.6 us
    unnamed x52, local copies, waits for them, and re-layouts  30.7 us
    all_to_all x1, waiting for transfers between devices, body(): lax.all_to_all(sliced, ('rl', 'head'), split_axis=0, concat_axis=0, tiled...  16.8 us
    ppermute x14, waiting for transfers between devices, body(): lax.ppermute((lax.dynamic_index_in_dim(keys_t, target, 0, keepdims=False)...  15 us
    all_to_all x1, waiting for transfers between devices, body(): lax.all_to_all(payload, 'rl', split_axis=0, concat_axis=0, tiled=True)  14.5 us
    all_to_all x1, starting transfers between devices, body(): lax.all_to_all(sliced, ('rl', 'head'), split_axis=0, concat_axis=0, tiled...  9.36 us
    dynamic_slice x8, local copies, waits for them, and re-layouts, body(): lax.dynamic_index_in_dim(keys_t, target, 0, keepdims=False)  7 us
  transfers between devices with their start and end apart: 16, of which 4 were waited for; matrix products, arithmetic and copies ran while one was open for 11% of the time, Pallas kernels for 30%

profile of v6, /device:TPU:36, one launch (start us, length us, event | category | flops | bytes accessed | tf_op | source)
XLA Modules:
  0.0 252.4 jit_solution(10200516534384995999)
XLA Ops:
  2.3 9.4 %all-to-all-start = ((bf16[32,4,2048]{2,1,0:T(4,128)(2,1)}), bf16[32,4,2048]{2,1,0:T(4,128)(2,1)S(1)}, u32[]{:S(2)}, u32[]{:S(2)}) async-start(bf16[32,4,2048]{2,1,0:T(4,128)(2,1)} %bitcast.4), calls=%async_computation | async-start | bytes 1048576 | tf_op jit(solution)/shard_map/all_to_all | solution.py:141
  11.8 16.8 %all-to-all-done = bf16[32,4,2048]{2,1,0:T(4,128)(2,1)S(1)} async-done(((bf16[32,4,2048]{2,1,0:T(4,128)(2,1)}), bf16[32,4,2048]{2,1,0:T(4,128)(2,1)S(1)}, u32[]{:S(2)}, u32[]{:S(2)}) %all-to-all-start) | async-done | bytes 524320 | tf_op jit(solution)/shard_map/all_to_all | solution.py:141
  29.6 2.5 constant_dynamic-slice_fusion
  34.4 1.9 collective-permute-start
  36.3 2.7 %collective-permute-start.1 = (bf16[1024,128]{1,0:T(8,128)(2,1)}, bf16[1024,128]{1,0:T(8,128)(2,1)S(1)}, u32[]{:S(2)}, u32[]{:S(2)}) collective-permute-start(bf16[1024,128]{1,0:T(8,128)(2,1)} %get-tuple-element.53), channel_id=1, source_target_pairs={{0,32},{32,64},{64,96},{96,128},{128,160},{160,192},{192,224},{224... | collective-permute-start | bytes 786440 | tf_op jit(solution)/shard_map/ppermute | solution.py:172
  45.9 2.2 collective-permute-start.4
  48.3 3.8 %collective-permute-start.5 = (bf16[1024,128]{1,0:T(8,128)(2,1)}, bf16[1024,128]{1,0:T(8,128)(2,1)S(1)}, u32[]{:S(2)}, u32[]{:S(2)}) collective-permute-start(bf16[1024,128]{1,0:T(8,128)(2,1)} %get-tuple-element.51), channel_id=1, source_target_pairs={{0,96},{32,128},{64,160},{96,192},{128,224},{160,0},{192,32},{224,... | collective-permute-start | bytes 786440 | tf_op jit(solution)/shard_map/ppermute | solution.py:172
  52.2 1.8 collective-permute-start.6
  54.0 1.7 collective-permute-start.7
  55.7 12.3 %collective-permute-done.3.v_ref = bf16[1024,128]{1,0:T(8,128)(2,1)} collective-permute-done((bf16[1024,128]{1,0:T(8,128)(2,1)}, bf16[1024,128]{1,0:T(8,128)(2,1)}, u32[]{:S(2)}, u32[]{:S(2)}) %collective-permute-start.3) | collective-permute-done | bytes 262176 | tf_op jit(solution)/shard_map/ppermute | solution.py:172
  68.0 8.8 %collective-permute-start.8 = (bf16[128,1024]{1,0:T(8,128)(2,1)S(1)}, bf16[128,1024]{1,0:T(8,128)(2,1)}, u32[]{:S(2)}, u32[]{:S(2)}) collective-permute-start(bf16[128,1024]{1,0:T(8,128)(2,1)S(1)} %bitcast.146), channel_id=1, source_target_pairs={{0,160},{32,192},{64,224},{96,0},{128,32},{160,64},{192,96},{224,1... | collective-permute-start | bytes 786440 | tf_op jit(solution)/shard_map/ppermute | solution.py:172
  76.8 1.9 fusion.3
  80.3 12.0 %collective-permute-start.10 = (bf16[128,1024]{1,0:T(8,128)(2,1)}, bf16[128,1024]{1,0:T(8,128)(2,1)}, u32[]{:S(2)}, u32[]{:S(2)}) collective-permute-start(bf16[128,1024]{1,0:T(8,128)(2,1)} %bitcast.27), channel_id=1, source_target_pairs={{0,192},{32,224},{64,0},{96,32},{128,64},{160,96},{192,128},{224,1... | collective-permute-start | bytes 786440 | tf_op jit(solution)/shard_map/ppermute | solution.py:172
  92.8 2.7 %collective-permute-done.8.kt_ref = bf16[128,1024]{1,0:T(8,128)(2,1)} collective-permute-done((bf16[128,1024]{1,0:T(8,128)(2,1)S(1)}, bf16[128,1024]{1,0:T(8,128)(2,1)}, u32[]{:S(2)}, u32[]{:S(2)}) %collective-permute-start.8) | collective-permute-done | bytes 262176 | tf_op jit(solution)/shard_map/ppermute | solution.py:172
  97.8 1.9 stack.67.info_ref
  101.3 11.8 %shard_map.82 = (f32[128,2048]{1,0:T(8,128)}, f32[128,128]{1,0:T(8,128)}) custom-call(s32[6]{0:T(128)} %stack.67.info_ref, bf16[128,2048]{1,0:T(8,128)(2,1)} %reshape.126.q_ref, bf16[128,1024]{1,0:T(8,128)(2,1)} %bitcast.141, bf16[1024,128]{1,0:T(8,128)(2,1)} %get-tuple-element.54.v_ref, bf16[128,32]{1,0:T(8,128)(2,1)} %bitcast.123, ...), custom_call_target="tpu_custom_call" | custom-call | tf_op jit(solution)/shard_map/pallas_call | solution.py:110
  115.6 10.5 %shard_map.83 = (f32[128,2048]{1,0:T(8,128)}, f32[128,128]{1,0:T(8,128)}) custom-call(s32[6]{0:T(128)} %stack.67.info_ref, bf16[128,2048]{1,0:T(8,128)(2,1)} %reshape.126.q_ref, bf16[128,1024]{1,0:T(8,128)(2,1)} %copy-done.5, bf16[1024,128]{1,0:T(8,128)(2,1)} %copy-done.6, bf16[128,32]{1,0:T(8,128)(2,1)} %bitcast.124, bf16[32,128]{1,0:T(8,128)(2,1)} %tv_ref.15, ...), custom_call_target="tpu_custom_call" | custom-call | tf_op jit(solution)/shard_map/pallas_call | solution.py:110
  127.6 10.6 %shard_map.84 = (f32[128,2048]{1,0:T(8,128)}, f32[128,128]{1,0:T(8,128)}) custom-call(s32[6]{0:T(128)} %stack.67.info_ref, bf16[128,2048]{1,0:T(8,128)(2,1)} %reshape.126.q_ref, bf16[128,1024]{1,0:T(8,128)(2,1)} %copy-done.7, bf16[1024,128]{1,0:T(8,128)(2,1)} %collective-permute-done.3.v_ref, bf16[128,32]{1,0:T(8,128)(2,1)} %bitcast.125, ...), custom_call_target="tpu_custom_call" | custom-call | tf_op jit(solution)/shard_map/pallas_call | solution.py:110
  139.6 10.6 %shard_map.85 = (f32[128,2048]{1,0:T(8,128)}, f32[128,128]{1,0:T(8,128)}) custom-call(s32[6]{0:T(128)} %stack.67.info_ref, bf16[128,2048]{1,0:T(8,128)(2,1)} %reshape.126.q_ref, bf16[128,1024]{1,0:T(8,128)(2,1)} %collective-permute-done.4.kt_ref, bf16[1024,128]{1,0:T(8,128)(2,1)} %copy-done.8, bf16[128,32]{1,0:T(8,128)(2,1)} %bitcast.126, ...), custom_call_target="tpu_custom_call" | custom-call | tf_op jit(solution)/shard_map/pallas_call | solution.py:110
  151.5 10.5 %shard_map.86 = (f32[128,2048]{1,0:T(8,128)}, f32[128,128]{1,0:T(8,128)}) custom-call(s32[6]{0:T(128)} %stack.67.info_ref, bf16[128,2048]{1,0:T(8,128)(2,1)} %reshape.126.q_ref, bf16[128,1024]{1,0:T(8,128)(2,1)} %copy-done.9, bf16[1024,128]{1,0:T(8,128)(2,1)} %collective-permute-done.7.v_ref, bf16[128,32]{1,0:T(8,128)(2,1)} %bitcast.127, ...), custom_call_target="tpu_custom_call" | custom-call | tf_op jit(solution)/shard_map/pallas_call | solution.py:110
  162.1 2.4 copy.129
  164.5 10.6 %shard_map.87 = (f32[128,2048]{1,0:T(8,128)}, f32[128,128]{1,0:T(8,128)}) custom-call(s32[6]{0:T(128)} %stack.67.info_ref, bf16[128,2048]{1,0:T(8,128)(2,1)} %reshape.126.q_ref, bf16[128,1024]{1,0:T(8,128)(2,1)} %collective-permute-done.8.kt_ref, bf16[1024,128]{1,0:T(8,128)(2,1)} %collective-permute-done.9.v_ref, bf16[128,32]{1,0:T(8,128)(2,1)} %bitcast.128, ...), custom_call_target="tpu_custom_call" | custom-call | tf_op jit(solution)/shard_map/pallas_call | solution.py:110
  175.1 2.4 copy.130
  177.5 10.8 %shard_map.88 = (f32[128,2048]{1,0:T(8,128)}, f32[128,128]{1,0:T(8,128)}) custom-call(s32[6]{0:T(128)} %stack.67.info_ref, bf16[128,2048]{1,0:T(8,128)(2,1)} %reshape.126.q_ref, bf16[128,1024]{1,0:T(8,128)(2,1)} %collective-permute-done.10.kt_ref, bf16[1024,128]{1,0:T(8,128)(2,1)} %collective-permute-done.11.v_ref, bf16[128,32]{1,0:T(8,128)(2,1)} %bitcast.129, ...), custom_call_target="tpu_custom_call" | custom-call | tf_op jit(solution)/shard_map/pallas_call | solution.py:110
  188.2 2.4 copy.131
  190.6 10.6 %shard_map.89 = (f32[128,2048]{1,0:T(8,128)}, f32[128,128]{1,0:T(8,128)}) custom-call(s32[6]{0:T(128)} %stack.67.info_ref, bf16[128,2048]{1,0:T(8,128)(2,1)} %reshape.126.q_ref, bf16[128,1024]{1,0:T(8,128)(2,1)} %collective-permute-done.12.kt_ref, bf16[1024,128]{1,0:T(8,128)(2,1)} %collective-permute-done.13.v_ref, bf16[128,32]{1,0:T(8,128)(2,1)} %bitcast.130, ...), custom_call_target="tpu_custom_call" | custom-call | tf_op jit(solution)/shard_map/pallas_call | solution.py:110
  201.2 2.4 copy.132
  203.6 1.8 maximum_maximum_fusion
  219.6 2.3 bitcast_dynamic-update-slice_fusion.3
  225.2 5.4 %multiply_reduce_fusion = f32[128,16,128]{2,1,0:T(8,128)S(1)} fusion(f32[8,128,16,128]{3,2,1,0:T(8,128)} %bitcast_dynamic-update-slice_fusion, f32[8,128,16]{2,1,0:T(8,128)S(1)} %copy-done.4), kind=kLoop, calls=%fused_computation | loop fusion | flops 3932160 | bytes 9502720 | tf_op jit(solution)/shard_map/reduce_sum | solution.py:187
  232.0 3.5 %all-to-all-start.1 = ((f32[4,32,2080]{2,1,0:T(8,128)}), f32[4,32,2080]{2,1,0:T(8,128)S(1)}, u32[]{:S(2)}, u32[]{:S(2)}) async-start(f32[4,32,2080]{2,1,0:T(8,128)} %concatenate.11), calls=%async_computation.1 | async-start | bytes 2228224 | tf_op jit(solution)/shard_map/all_to_all | solution.py:192
  236.2 14.5 %all-to-all-done.1 = f32[4,32,2080]{2,1,0:T(8,128)S(1)} async-done(((f32[4,32,2080]{2,1,0:T(8,128)}), f32[4,32,2080]{2,1,0:T(8,128)S(1)}, u32[]{:S(2)}, u32[]{:S(2)}) %all-to-all-start.1) | async-done | bytes 1064992 | tf_op jit(solution)/shard_map/all_to_all | solution.py:192
  (108 shorter events, 46.7 us)
Async XLA Ops:
  0.0 32.0 %copy-start.3 = (bf16[8,1024,128]{2,1,0:T(8,128)(2,1)S(1)}, bf16[8,1024,128]{2,1,0:T(8,128)(2,1)}, u32[]{:S(2)}) copy-start(bf16[8,1024,128]{2,1,0:T(8,128)(2,1)} %param.10) | copy-start | bytes 6291460
  0.0 43.1 %copy-start.11 = (s32[8,128]{1,0:T(8,128)S(1)}, s32[8,128]{1,0:T(8,128)}, u32[]{:S(2)}) copy-start(s32[8,128]{1,0:T(8,128)} %param.13) | copy-start | bytes 12292
  2.3 26.3 %all-to-all-start = ((bf16[32,4,2048]{2,1,0:T(4,128)(2,1)}), bf16[32,4,2048]{2,1,0:T(4,128)(2,1)S(1)}, u32[]{:S(2)}, u32[]{:S(2)}) async-start(bf16[32,4,2048]{2,1,0:T(4,128)(2,1)} %bitcast.4), calls=%async_computation | async-start | bytes 1048576 | tf_op jit(solution)/shard_map/all_to_all | solution.py:141
  11.7 84.1 %copy-start.12 = (s32[8]{0:T(128)S(1)}, s32[8]{0:T(128)}, u32[]{:S(2)}) copy-start(s32[8]{0:T(128)} %param.15) | copy-start | bytes 100
  11.7 84.7 %copy-start.13 = (s32[8]{0:T(128)S(1)}, s32[8]{0:T(128)}, u32[]{:S(2)}) copy-start(s32[8]{0:T(128)} %param.14) | copy-start | bytes 100
  11.8 85.4 %copy-start.10 = (bf16[32,128]{1,0:T(8,128)(2,1)S(1)}, bf16[32,128]{1,0:T(8,128)(2,1)}, u32[]{:S(2)}) copy-start(bf16[32,128]{1,0:T(8,128)(2,1)} %param.11) | copy-start | bytes 24580
  34.4 13.9 %collective-permute-start = (bf16[128,1024]{1,0:T(8,128)(2,1)S(1)}, bf16[128,1024]{1,0:T(8,128)(2,1)S(1)}, u32[]{:S(2)}, u32[]{:S(2)}) collective-permute-start(bf16[128,1024]{1,0:T(8,128)(2,1)S(1)} %bitcast.150), channel_id=1, source_target_pairs={{0,32},{32,64},{64,96},{96,128},{128,160},{160,192},{192,224},{224... | collective-permute-start | bytes 786440 | tf_op jit(solution)/shard_map/ppermute | solution.py:172
  36.3 15.8 %collective-permute-start.1 = (bf16[1024,128]{1,0:T(8,128)(2,1)}, bf16[1024,128]{1,0:T(8,128)(2,1)S(1)}, u32[]{:S(2)}, u32[]{:S(2)}) collective-permute-start(bf16[1024,128]{1,0:T(8,128)(2,1)} %get-tuple-element.53), channel_id=1, source_target_pairs={{0,32},{32,64},{64,96},{96,128},{128,160},{160,192},{192,224},{224... | collective-permute-start | bytes 786440 | tf_op jit(solution)/shard_map/ppermute | solution.py:172
  40.2 13.8 %collective-permute-start.2 = (bf16[128,1024]{1,0:T(8,128)(2,1)S(1)}, bf16[128,1024]{1,0:T(8,128)(2,1)S(1)}, u32[]{:S(2)}, u32[]{:S(2)}) collective-permute-start(bf16[128,1024]{1,0:T(8,128)(2,1)S(1)} %bitcast.149), channel_id=1, source_target_pairs={{0,64},{32,96},{64,128},{96,160},{128,192},{160,224},{192,0},{224,... | collective-permute-start | bytes 786440 | tf_op jit(solution)/shard_map/ppermute | solution.py:172
  41.8 26.2 %collective-permute-start.3 = (bf16[1024,128]{1,0:T(8,128)(2,1)}, bf16[1024,128]{1,0:T(8,128)(2,1)}, u32[]{:S(2)}, u32[]{:S(2)}) collective-permute-start(bf16[1024,128]{1,0:T(8,128)(2,1)} %get-tuple-element.52), channel_id=1, source_target_pairs={{0,64},{32,96},{64,128},{96,160},{128,192},{160,224},{192,0},{224,... | collective-permute-start | bytes 786440 | tf_op jit(solution)/shard_map/ppermute | solution.py:172
  45.9 34.3 %collective-permute-start.4 = (bf16[128,1024]{1,0:T(8,128)(2,1)S(1)}, bf16[128,1024]{1,0:T(8,128)(2,1)}, u32[]{:S(2)}, u32[]{:S(2)}) collective-permute-start(bf16[128,1024]{1,0:T(8,128)(2,1)S(1)} %bitcast.148), channel_id=1, source_target_pairs={{0,96},{32,128},{64,160},{96,192},{128,224},{160,0},{192,32},{224,... | collective-permute-start | bytes 786440 | tf_op jit(solution)/shard_map/ppermute | solution.py:172
  48.3 67.3 %copy-start.5 = (bf16[128,1024]{1,0:T(8,128)(2,1)}, bf16[128,1024]{1,0:T(8,128)(2,1)S(1)}, u32[]{:S(2)}) copy-start(bf16[128,1024]{1,0:T(8,128)(2,1)S(1)} %collective-permute-done.kt_ref) | copy-start | bytes 786436
  48.3 31.9 %collective-permute-start.5 = (bf16[1024,128]{1,0:T(8,128)(2,1)}, bf16[1024,128]{1,0:T(8,128)(2,1)S(1)}, u32[]{:S(2)}, u32[]{:S(2)}) collective-permute-start(bf16[1024,128]{1,0:T(8,128)(2,1)} %get-tuple-element.51), channel_id=1, source_target_pairs={{0,96},{32,128},{64,160},{96,192},{128,224},{160,0},{192,32},{224,... | collective-permute-start | bytes 786440 | tf_op jit(solution)/shard_map/ppermute | solution.py:172
  52.2 63.4 %copy-start.6 = (bf16[1024,128]{1,0:T(8,128)(2,1)}, bf16[1024,128]{1,0:T(8,128)(2,1)S(1)}, u32[]{:S(2)}) copy-start(bf16[1024,128]{1,0:T(8,128)(2,1)S(1)} %collective-permute-done.1.v_ref) | copy-start | bytes 786436
  52.2 40.1 %collective-permute-start.6 = (bf16[128,1024]{1,0:T(8,128)(2,1)S(1)}, bf16[128,1024]{1,0:T(8,128)(2,1)S(1)}, u32[]{:S(2)}, u32[]{:S(2)}) collective-permute-start(bf16[128,1024]{1,0:T(8,128)(2,1)S(1)} %bitcast.147), channel_id=1, source_target_pairs={{0,128},{32,160},{64,192},{96,224},{128,0},{160,32},{192,64},{224,... | collective-permute-start | bytes 786440 | tf_op jit(solution)/shard_map/ppermute | solution.py:172
  54.0 73.6 %copy-start.7 = (bf16[128,1024]{1,0:T(8,128)(2,1)}, bf16[128,1024]{1,0:T(8,128)(2,1)S(1)}, u32[]{:S(2)}) copy-start(bf16[128,1024]{1,0:T(8,128)(2,1)S(1)} %collective-permute-done.2.kt_ref) | copy-start | bytes 786436
  54.0 38.6 %collective-permute-start.7 = (bf16[1024,128]{1,0:T(8,128)(2,1)}, bf16[1024,128]{1,0:T(8,128)(2,1)}, u32[]{:S(2)}, u32[]{:S(2)}) collective-permute-start(bf16[1024,128]{1,0:T(8,128)(2,1)} %get-tuple-element.50), channel_id=1, source_target_pairs={{0,128},{32,160},{64,192},{96,224},{128,0},{160,32},{192,64},{224,... | collective-permute-start | bytes 786440 | tf_op jit(solution)/shard_map/ppermute | solution.py:172
  68.0 27.5 %collective-permute-start.8 = (bf16[128,1024]{1,0:T(8,128)(2,1)S(1)}, bf16[128,1024]{1,0:T(8,128)(2,1)}, u32[]{:S(2)}, u32[]{:S(2)}) collective-permute-start(bf16[128,1024]{1,0:T(8,128)(2,1)S(1)} %bitcast.146), channel_id=1, source_target_pairs={{0,160},{32,192},{64,224},{96,0},{128,32},{160,64},{192,96},{224,1... | collective-permute-start | bytes 786440 | tf_op jit(solution)/shard_map/ppermute | solution.py:172
  80.2 84.3 %collective-permute-start.9 = (bf16[1024,128]{1,0:T(8,128)(2,1)}, bf16[1024,128]{1,0:T(8,128)(2,1)}, u32[]{:S(2)}, u32[]{:S(2)}) collective-permute-start(bf16[1024,128]{1,0:T(8,128)(2,1)} %get-tuple-element.49), channel_id=1, source_target_pairs={{0,160},{32,192},{64,224},{96,0},{128,32},{160,64},{192,96},{224,1... | collective-permute-start | bytes 786440 | tf_op jit(solution)/shard_map/ppermute | solution.py:172
  80.3 59.3 %copy-start.8 = (bf16[1024,128]{1,0:T(8,128)(2,1)}, bf16[1024,128]{1,0:T(8,128)(2,1)S(1)}, u32[]{:S(2)}) copy-start(bf16[1024,128]{1,0:T(8,128)(2,1)S(1)} %collective-permute-done.5.v_ref) | copy-start | bytes 786436
  80.3 97.2 %collective-permute-start.10 = (bf16[128,1024]{1,0:T(8,128)(2,1)}, bf16[128,1024]{1,0:T(8,128)(2,1)}, u32[]{:S(2)}, u32[]{:S(2)}) collective-permute-start(bf16[128,1024]{1,0:T(8,128)(2,1)} %bitcast.27), channel_id=1, source_target_pairs={{0,192},{32,224},{64,0},{96,32},{128,64},{160,96},{192,128},{224,1... | collective-permute-start | bytes 786440 | tf_op jit(solution)/shard_map/ppermute | solution.py:172
  92.3 45.9 %copy-start.9 = (bf16[128,1024]{1,0:T(8,128)(2,1)}, bf16[128,1024]{1,0:T(8,128)(2,1)S(1)}, u32[]{:S(2)}) copy-start(bf16[128,1024]{1,0:T(8,128)(2,1)S(1)} %collective-permute-done.6.kt_ref) | copy-start | bytes 786436
  92.3 85.2 %collective-permute-start.11 = (bf16[1024,128]{1,0:T(8,128)(2,1)}, bf16[1024,128]{1,0:T(8,128)(2,1)}, u32[]{:S(2)}, u32[]{:S(2)}) collective-permute-start(bf16[1024,128]{1,0:T(8,128)(2,1)} %get-tuple-element.48), channel_id=1, source_target_pairs={{0,192},{32,224},{64,0},{96,32},{128,64},{160,96},{192,128},{224,1... | collective-permute-start | bytes 786440 | tf_op jit(solution)/shard_map/ppermute | solution.py:172
  92.6 98.1 %collective-permute-start.12 = (bf16[128,1024]{1,0:T(8,128)(2,1)S(1)}, bf16[128,1024]{1,0:T(8,128)(2,1)}, u32[]{:S(2)}, u32[]{:S(2)}) collective-permute-start(bf16[128,1024]{1,0:T(8,128)(2,1)S(1)} %bitcast.145), channel_id=1, source_target_pairs={{0,224},{32,0},{64,32},{96,64},{128,96},{160,128},{192,160},{224,1... | collective-permute-start | bytes 786440 | tf_op jit(solution)/shard_map/ppermute | solution.py:172
  95.5 95.1 %collective-permute-start.13 = (bf16[1024,128]{1,0:T(8,128)(2,1)}, bf16[1024,128]{1,0:T(8,128)(2,1)}, u32[]{:S(2)}, u32[]{:S(2)}) collective-permute-start(bf16[1024,128]{1,0:T(8,128)(2,1)} %get-tuple-element.47), channel_id=1, source_target_pairs={{0,224},{32,0},{64,32},{96,64},{128,96},{160,128},{192,160},{224,1... | collective-permute-start | bytes 786440 | tf_op jit(solution)/shard_map/ppermute | solution.py:172
  216.5 5.5 %copy-start = (f32[16,8,16,128]{3,2,1,0:T(8,128)S(1)}, f32[16,8,16,128]{3,2,1,0:T(8,128)}, u32[]{:S(2)}) copy-start(f32[16,8,16,128]{3,2,1,0:T(8,128)} %copy.130) | copy-start | bytes 3145732
  216.5 6.5 %copy-start.1 = (f32[16,8,16,128]{3,2,1,0:T(8,128)S(1)}, f32[16,8,16,128]{3,2,1,0:T(8,128)}, u32[]{:S(2)}) copy-start(f32[16,8,16,128]{3,2,1,0:T(8,128)} %copy.131) | copy-start | bytes 3145732
  216.5 7.6 %copy-start.2 = (f32[16,8,16,128]{3,2,1,0:T(8,128)S(1)}, f32[16,8,16,128]{3,2,1,0:T(8,128)}, u32[]{:S(2)}) copy-start(f32[16,8,16,128]{3,2,1,0:T(8,128)} %copy.132) | copy-start | bytes 3145732
  216.5 8.7 %copy-start.4 = (f32[8,128,16]{2,1,0:T(8,128)S(1)}, f32[8,128,16]{2,1,0:T(8,128)}, u32[]{:S(2)}) copy-start(f32[8,128,16]{2,1,0:T(8,128)} %copy.113) | copy-start | bytes 196612
  232.0 18.7 %all-to-all-start.1 = ((f32[4,32,2080]{2,1,0:T(8,128)}), f32[4,32,2080]{2,1,0:T(8,128)S(1)}, u32[]{:S(2)}, u32[]{:S(2)}) async-start(f32[4,32,2080]{2,1,0:T(8,128)} %concatenate.11), calls=%async_computation.1 | async-start | bytes 2228224 | tf_op jit(solution)/shard_map/all_to_all | solution.py:192

commit v7 on v4

--- a/solution.py
+++ b/solution.py
@@ -136,6 +136,73 @@
     )(info, query_block, keys_t, values, tree_keys_t, tree_values, tree_mask)
 
 
+def exchange_kernel(src_ref, out_ref, slots, send_sem, recv_sem, own_sem, *, n_lo, n_head):
+    request = lax.axis_index("rh")
+    quarter = lax.axis_index("rl")
+    head = lax.axis_index("head")
+    me = quarter * n_head + head
+    peers = n_lo * n_head
+    mesh = pl.DeviceIdType.MESH
+
+    barrier = pltpu.get_barrier_semaphore()
+    for d in range(peers):
+        dest = (request, d // n_head, d % n_head)
+
+        @pl.when(d != me)
+        def _():
+            pl.semaphore_signal(barrier, inc=1, device_id=dest, device_id_type=mesh)
+
+    pl.semaphore_wait(barrier, peers - 1)
+
+    def push(d):
+        return pltpu.make_async_remote_copy(
+            src_ref.at[d % n_head],
+            slots.at[me],
+            send_sem.at[d],
+            recv_sem.at[me],
+            device_id=(request, d // n_head, d % n_head),
+            device_id_type=mesh,
+        )
+
+    for d in range(peers):
+        pl.when(d != me)(push(d).start)
+    own = pltpu.make_async_copy(src_ref.at[head], slots.at[me], own_sem)
+    own.start()
+    own.wait()
+    for d in range(peers):
+        pl.when(d != me)(push(d).wait_send)
+    for s in range(peers):
+        arrival = pltpu.make_async_remote_copy(
+            src_ref.at[0],
+            slots.at[s],
+            send_sem.at[s],
+            recv_sem.at[s],
+            device_id=(request, s // n_head, s % n_head),
+            device_id_type=mesh,
+        )
+        pl.when(s != me)(arrival.wait_recv)
+    out_ref[...] = slots[...]
+
+
+def exchange_queries(pieces, n_lo, n_head):
+    peers = n_lo * n_head
+    shape = (peers,) + pieces.shape[1:]
+    vmem = pl.BlockSpec(memory_space=pltpu.VMEM)
+    return pl.pallas_call(
+        functools.partial(exchange_kernel, n_lo=n_lo, n_head=n_head),
+        out_shape=jax.ShapeDtypeStruct(shape, pieces.dtype),
+        in_specs=[vmem],
+        out_specs=vmem,
+        scratch_shapes=[
+            pltpu.VMEM(shape, pieces.dtype),
+            pltpu.SemaphoreType.DMA((peers,)),
+            pltpu.SemaphoreType.DMA((peers,)),
+            pltpu.SemaphoreType.DMA(()),
+        ],
+        compiler_params=pltpu.CompilerParams(collective_id=0, has_side_effects=True),
+    )(pieces)
+
+
 def body(
     queries, cache_keys, cache_values, tree_keys, tree_values, parents, tree_sizes, cache_lens
 ):
@@ -153,10 +220,9 @@
 
     n_head = lax.axis_size("head")
     width = queries.shape[1] // n_head
-    sliced = queries.reshape(queries.shape[0], n_head, width).transpose(1, 0, 2)
-    sliced = jnp.broadcast_to(sliced[None], (n_lo,) + sliced.shape)
-    sliced = sliced.reshape(n_lo * n_head, queries.shape[0], width)
-    query_block = lax.all_to_all(sliced, ("rl", "head"), split_axis=0, concat_axis=0, tiled=True)
+    pieces = queries.reshape(queries.shape[0], n_head, width // HD, HD).transpose(1, 0, 2, 3)
+    pieces = pieces.reshape(n_head, queries.shape[0] * width // HD, HD)
+    query_block = exchange_queries(pieces, n_lo, n_head)
     query_block = query_block.reshape(node_count, width)
 
     both = jnp.concatenate([cache_keys, cache_values], axis=2)

time: 184 us -> 172 us (0.935)
  the two profiles are of different devices: /device:TPU:40 before, /device:TPU:36 now
where the time goes in v7:
time: 172 us
  Pallas kernels  118 us (69%)
  local copies, waits for them, and re-layouts  19.2 us (11%)
  waiting for transfers between devices  14.5 us (8%)
  starting transfers between devices  11.1 us (6%)
  other arithmetic  7.06 us (4%)
  matrix products  2.02 us (1%)
    pallas_call x1, Pallas kernels, attend(): pl.pallas_call(functools.partial(attend_kernel, scale=1.0 / math.sqrt(HD)...  65.7 us
    pallas_call x1, Pallas kernels, exchange_queries(): pl.pallas_call(functools.partial(exchange_kernel, n_lo=n_lo, n_head=n_hea...  52.3 us
    all_to_all x1, waiting for transfers between devices, body(): lax.all_to_all(payload, 'rl', split_axis=0, concat_axis=0, tiled=True)  14.5 us
    all_to_all x1, starting transfers between devices, body(): lax.all_to_all(both, 'rh', split_axis=0, concat_axis=1, tiled=True)[0]  7.56 us
    concatenate x1, other arithmetic, body(): both = jnp.concatenate([cache_keys, cache_values], axis=2)  4.65 us
    slice x1, local copies, waits for them, and re-layouts, body(): values = mine[:, :, HD:]  3.92 us
    all_to_all x1, starting transfers between devices, body(): lax.all_to_all(payload, 'rl', split_axis=0, concat_axis=0, tiled=True)  3.52 us
  transfers between devices with their start and end apart: 2, of which 1 were waited for; matrix products, arithmetic and copies ran while one was open for 6% of the time, Pallas kernels for 30%

profile of v7, /device:TPU:36, one launch (start us, length us, event | category | flops | bytes accessed | tf_op | source)
XLA Modules:
  0.0 172.0 jit_solution(17386896473361618240)
XLA Ops:
  0.0 4.7 %pad_maximum_fusion = bf16[8,1024,256]{2,1,0:T(8,128)(2,1)} fusion(bf16[8,1024,128]{2,1,0:T(8,128)(2,1)} %param.10, bf16[8,1024,128]{2,1,0:T(8,128)(2,1)} %param.9), kind=kLoop, calls=%fused_computation | loop fusion | flops 8388608 | bytes 8388608 | tf_op jit(solution)/shard_map/concatenate | solution.py:228
  4.7 7.6 %all-to-all-start = ((bf16[8,1024,256]{2,1,0:T(8,128)(2,1)}), bf16[8,1024,256]{2,1,0:T(8,128)(2,1)}, u32[]{:S(2)}, u32[]{:S(2)}) async-start(bf16[8,1024,256]{2,1,0:T(8,128)(2,1)} %pad_maximum_fusion), calls=%async_computation | async-start | bytes 8388608 | tf_op jit(solution)/shard_map/all_to_all | solution.py:229
  12.2 0.6 dynamic_slice.12
  12.8 0.0 copy-done.5
  12.8 0.7 dynamic_slice.13
  13.5 0.7 copy.16
  14.2 52.3 %shard_map.82 = bf16[32,64,128]{2,1,0:T(8,128)(2,1)} custom-call(bf16[8,64,128]{2,1,0:T(8,128)(2,1)} %bitcast.44), custom_call_target="tpu_custom_call" | custom-call | tf_op jit(solution)/shard_map/pallas_call | solution.py:191
  66.5 2.1 %reshape.49.q_ref = bf16[128,2048]{1,0:T(8,128)(2,1)} reshape(bf16[32,64,128]{2,1,0:T(8,128)(2,1)} %shard_map.82) | data formatting | bytes 1048576 | tf_op jit(solution)/shard_map/reshape | solution.py:226
  68.6 0.7 copy.17
  69.3 1.9 %stack.13.info_ref = s32[5]{0:T(128)} concatenate(s32[1]{0:T(128)} %dynamic_slice.13, s32[1]{0:T(128)} %bitcast.1, s32[1]{0:T(128)} %bitcast.2, s32[1]{0:T(128)} %constant.46.clone.1, s32[1]{0:T(128)} %dynamic_slice.12), dimensions={0} | concatenate | bytes 40 | tf_op jit(solution)/shard_map/stack | solution.py:237
  71.3 0.9 fusion.1
  72.2 0.4 fusion.3
  72.7 0.5 fusion.5
  73.1 0.2 fusion.27
  73.3 0.7 fusion.22.tmask_ref
  74.1 0.0 all-to-all-done
  74.1 3.9 %fusion.26 = (bf16[8,1024,128]{2,1,0:T(8,128)(2,1)}, bf16[8,128,1024]{1,2,0:T(8,128)(2,1)S(1)}) fusion(bf16[8,1024,256]{2,1,0:T(8,128)(2,1)} %all-to-all-done), kind=kLoop, calls=%fused_computation.39 | loop fusion | bytes 8388608 | tf_op jit(solution)/shard_map/slice | solution.py:240
  78.0 2.6 %copy.20.kt_ref = bf16[8,128,1024]{2,1,0:T(8,128)(2,1)} copy(bf16[8,128,1024]{1,2,0:T(8,128)(2,1)S(1)} %get-tuple-element.14) | data formatting | bytes 4194304 | tf_op jit(solution)/shard_map/transpose | solution.py:239
  80.6 65.7 %shard_map.83 = (f32[128,2048]{1,0:T(8,128)}, f32[16,128,128]{2,1,0:T(8,128)}, f32[16,128,128]{2,1,0:T(8,128)}) custom-call(s32[5]{0:T(128)} %stack.13.info_ref, bf16[128,2048]{1,0:T(8,128)(2,1)} %reshape.49.q_ref, bf16[8,128,1024]{2,1,0:T(8,128)(2,1)} %copy.20.kt_ref, bf16[8,1024,128]{2,1,0:T(8,128)(2,1)} %get-tuple-element.13.v_ref, ...), custom_call_target="tpu_custom_call" | custom-call | tf_op jit(solution)/shard_map/pallas_call | solution.py:115
  146.2 2.1 %copy.26 = f32[16,128,1]{0,1,2:T(8,128)S(1)} copy(f32[16,128,1]{2,1,0:T(8,128)} %bitcast.42) | data formatting | bytes 16384 | tf_op jit(solution)/shard_map/squeeze | solution.py:242
  148.4 2.1 %copy.25 = f32[16,128,1]{0,1,2:T(8,128)S(1)} copy(f32[16,128,1]{2,1,0:T(8,128)} %bitcast.41) | data formatting | bytes 16384 | tf_op jit(solution)/shard_map/squeeze | solution.py:243
  150.4 1.2 concatenate.7
  151.6 3.5 %all-to-all-start.1 = ((f32[4,32,2080]{2,1,0:T(8,128)}), f32[4,32,2080]{2,1,0:T(8,128)S(1)}, u32[]{:S(2)}, u32[]{:S(2)}) async-start(f32[4,32,2080]{2,1,0:T(8,128)} %bitcast.12), calls=%async_computation.1 | async-start | bytes 2228224 | tf_op jit(solution)/shard_map/all_to_all | solution.py:246
  155.1 0.6 add_compare_fusion
  155.8 14.5 %all-to-all-done.1 = f32[4,32,2080]{2,1,0:T(8,128)S(1)} async-done(((f32[4,32,2080]{2,1,0:T(8,128)}), f32[4,32,2080]{2,1,0:T(8,128)S(1)}, u32[]{:S(2)}, u32[]{:S(2)}) %all-to-all-start.1) | async-done | bytes 1064992 | tf_op jit(solution)/shard_map/all_to_all | solution.py:246
  170.3 0.1 slice_reduce_fusion
  170.4 0.1 fusion.19
  170.5 0.3 mul.19
  170.8 0.2 mul.20
  171.0 0.1 fusion.6
  171.1 0.1 div.11
  171.2 0.8 fusion.11
  (13 shorter events, 0.1 us)
Async XLA Ops:
  4.7 7.6 %copy-start.4 = (s32[8]{0:T(128)S(1)}, s32[8]{0:T(128)}, u32[]{:S(2)}) copy-start(s32[8]{0:T(128)} %param.14) | copy-start | bytes 100
  4.7 8.2 %copy-start.5 = (s32[8]{0:T(128)S(1)}, s32[8]{0:T(128)}, u32[]{:S(2)}) copy-start(s32[8]{0:T(128)} %param.15) | copy-start | bytes 100
  4.7 8.8 %copy-start.1 = (bf16[4,16384]{1,0:T(4,128)(2,1)S(1)}, bf16[4,16384]{1,0:T(4,128)(2,1)}, u32[]{:S(2)}) copy-start(bf16[4,16384]{1,0:T(4,128)(2,1)} %param.8) | copy-start | bytes 393220
  4.7 69.4 %all-to-all-start = ((bf16[8,1024,256]{2,1,0:T(8,128)(2,1)}), bf16[8,1024,256]{2,1,0:T(8,128)(2,1)}, u32[]{:S(2)}, u32[]{:S(2)}) async-start(bf16[8,1024,256]{2,1,0:T(8,128)(2,1)} %pad_maximum_fusion), calls=%async_computation | async-start | bytes 8388608 | tf_op jit(solution)/shard_map/all_to_all | solution.py:229
  12.2 56.4 %copy-start.2 = (bf16[32,128]{1,0:T(8,128)(2,1)S(1)}, bf16[32,128]{1,0:T(8,128)(2,1)}, u32[]{:S(2)}) copy-start(bf16[32,128]{1,0:T(8,128)(2,1)} %param.11) | copy-start | bytes 24580
  12.2 59.1 %copy-start.3 = (s32[8,128]{1,0:T(8,128)S(1)}, s32[8,128]{1,0:T(8,128)}, u32[]{:S(2)}) copy-start(s32[8,128]{1,0:T(8,128)} %param.13) | copy-start | bytes 12292
  146.2 4.2 %copy-start = (f32[128,2048]{1,0:T(8,128)S(1)}, f32[128,2048]{1,0:T(8,128)}, u32[]{:S(2)}) copy-start(f32[128,2048]{1,0:T(8,128)} %get-tuple-element.8) | copy-start | bytes 3145732
  151.6 18.7 %all-to-all-start.1 = ((f32[4,32,2080]{2,1,0:T(8,128)}), f32[4,32,2080]{2,1,0:T(8,128)S(1)}, u32[]{:S(2)}, u32[]{:S(2)}) async-start(f32[4,32,2080]{2,1,0:T(8,128)} %bitcast.12), calls=%async_computation.1 | async-start | bytes 2228224 | tf_op jit(solution)/shard_map/all_to_all | solution.py:246

commit v8 on v7

--- a/solution.py
+++ b/solution.py
@@ -31,44 +31,75 @@
 
 
 def attend_kernel(
-    info_ref, q_ref, kt_ref, v_ref, tkt_ref, tv_ref, tmask_ref, acc_ref, top_ref, den_ref, *, scale
+    info_ref, q_ref, kt_hbm, v_hbm, tkt_ref, tv_ref, tmask_ref, acc_ref, top_ref, den_ref,
+    kslots, vslots, send_sem, recv_sem, own_sem, *, scale, n_hi,
 ):
-    s = pl.program_id(0)
+    request = lax.axis_index("rh")
+    quarter = lax.axis_index("rl")
+    head_axis = lax.axis_index("head")
+    mesh = pl.DeviceIdType.MESH
     length = info_ref[0]
-    request = info_ref[1]
-    quarter = info_ref[2]
-    n_lo = info_ref[3]
-    live_nodes = info_ref[4]
+    n_lo = info_ref[1]
     rows = q_ref.shape[0]
     heads = q_ref.shape[1] // HD
-    block_len = kt_ref.shape[1]
-    start = (s * n_lo + quarter) * block_len
-    full = start + block_len <= length
-
-    @pl.when(s == 0)
-    def _():
-        acc_ref[...] = jnp.zeros_like(acc_ref)
-        top_ref[...] = jnp.full_like(top_ref, negative_fill)
-        den_ref[...] = jnp.zeros_like(den_ref)
-
-    def group(with_tree, masked, count):
+    block_len = kt_hbm.shape[2]
+
+    barrier = pltpu.get_barrier_semaphore()
+    for t in range(n_hi):
+
+        @pl.when(t != request)
+        def _():
+            pl.semaphore_signal(
+                barrier, inc=1, device_id=(t, quarter, head_axis), device_id_type=mesh
+            )
+
+    pl.semaphore_wait(barrier, n_hi - 1)
+
+    def pushes(t):
+        dest = (t, quarter, head_axis)
+        return (
+            pltpu.make_async_remote_copy(
+                kt_hbm.at[t], kslots.at[request], send_sem.at[t, 0], recv_sem.at[request, 0],
+                device_id=dest, device_id_type=mesh,
+            ),
+            pltpu.make_async_remote_copy(
+                v_hbm.at[t], vslots.at[request], send_sem.at[t, 1], recv_sem.at[request, 1],
+                device_id=dest, device_id_type=mesh,
+            ),
+        )
+
+    for shift in range(1, n_hi):
+        t = lax.rem(request + shift, n_hi)
+        for copy in pushes(t):
+            copy.start()
+    own_k = pltpu.make_async_copy(kt_hbm.at[request], kslots.at[request], own_sem.at[0])
+    own_v = pltpu.make_async_copy(v_hbm.at[request], vslots.at[request], own_sem.at[1])
+    own_k.start()
+    own_v.start()
+
+    acc_ref[...] = jnp.zeros_like(acc_ref)
+    top_ref[...] = jnp.full_like(top_ref, negative_fill)
+    den_ref[...] = jnp.zeros_like(den_ref)
+
+    def group(s, with_tree):
+        start = (s * n_lo + quarter) * block_len
+        kt_ref = kslots.at[s]
+        v_ref = vslots.at[s]
+
         def head(h, carry):
             col = pl.multiple_of(h * HD, HD)
-            qh = q_ref[:count, pl.ds(col, HD)]
+            qh = q_ref[:, pl.ds(col, HD)]
             sc = jnp.dot(qh, kt_ref[...], preferred_element_type=jnp.float32) * scale
-            if masked:
-                pos = start + lax.broadcasted_iota(jnp.int32, sc.shape, 1)
-                live = pos < length
-                sc = jnp.where(live, sc, negative_fill)
+            pos = start + lax.broadcasted_iota(jnp.int32, sc.shape, 1)
+            live = pos < length
+            sc = jnp.where(live, sc, negative_fill)
             peak = jnp.max(sc, axis=1, keepdims=True)
             if with_tree:
                 st = jnp.dot(qh, tkt_ref[...], preferred_element_type=jnp.float32) * scale
-                tlive = tmask_ref[:count, :] > 0.5
+                tlive = tmask_ref[...] > 0.5
                 st = jnp.where(tlive, st, negative_fill)
                 peak = jnp.maximum(peak, jnp.max(st, axis=1, keepdims=True))
-            w = jnp.exp(sc - peak)
-            if masked:
-                w = jnp.where(live, w, 0.0)
+            w = jnp.where(live, jnp.exp(sc - peak), 0.0)
             tot = jnp.sum(w, axis=1, keepdims=True)
             gs = jnp.dot(w.astype(jnp.bfloat16), v_ref[...], preferred_element_type=jnp.float32)
             if with_tree:
@@ -80,59 +111,70 @@
             floored = jnp.maximum(tot, 1.0)
             part = gs / floored
             lt = peak + jnp.log(floored)
-            old = top_ref[h, :count, :][:, :1]
+            old = top_ref[h][:, :1]
             new = jnp.maximum(old, lt)
             keep = jnp.exp(old - new)
             add = jnp.exp(lt - new)
-            acc_ref[:count, pl.ds(col, HD)] = (
-                keep * acc_ref[:count, pl.ds(col, HD)] + add * part
-            )
-            den_ref[h, :count, :] = jnp.broadcast_to(
-                keep * den_ref[h, :count, :][:, :1] + add, (count, HD)
-            )
-            top_ref[h, :count, :] = jnp.broadcast_to(new, (count, HD))
+            acc_ref[:, pl.ds(col, HD)] = keep * acc_ref[:, pl.ds(col, HD)] + add * part
+            den_ref[h] = jnp.broadcast_to(keep * den_ref[h][:, :1] + add, (rows, HD))
+            top_ref[h] = jnp.broadcast_to(new, (rows, HD))
             return carry
 
         lax.fori_loop(0, heads, head, 0)
 
-    half = rows // 2
-    for with_tree in (True, False):
-        mine = s == request if with_tree else jnp.logical_and(s != request, start < length)
-        for masked in (False, True):
-            case = jnp.logical_and(mine, jnp.logical_not(full) if masked else full)
-            for count in (half, rows):
-                few = live_nodes <= half
-                pick = jnp.logical_and(case, few if count == half else jnp.logical_not(few))
-                pl.when(pick)(functools.partial(group, with_tree, masked, count))
+    own_k.wait()
+    own_v.wait()
+    group(request, True)
+
+    def landed(s):
+        source = (s, quarter, head_axis)
+        return (
+            pltpu.make_async_remote_copy(
+                kt_hbm.at[s], kslots.at[s], send_sem.at[s, 0], recv_sem.at[s, 0],
+                device_id=source, device_id_type=mesh,
+            ),
+            pltpu.make_async_remote_copy(
+                v_hbm.at[s], vslots.at[s], send_sem.at[s, 1], recv_sem.at[s, 1],
+                device_id=source, device_id_type=mesh,
+            ),
+        )
+
+    def arrival(step, carry):
+        s = lax.rem(request - step - 1 + n_hi, n_hi)
+        for copy in landed(s):
+            copy.wait_recv()
+        group(s, False)
+        return carry
+
+    lax.fori_loop(0, n_hi - 1, arrival, 0)
+    for shift in range(1, n_hi):
+        t = lax.rem(request + shift, n_hi)
+        for copy in pushes(t):
+            copy.wait_send()
 
 
 def attend(info, query_block, keys_t, values, tree_keys_t, tree_values, tree_mask):
     rows, width = query_block.shape
     heads = width // HD
-    n_groups, _, block_len = keys_t.shape
-    tree_rows = tree_values.shape[0]
+    n_hi = keys_t.shape[0]
     stats = jax.ShapeDtypeStruct((heads, rows, HD), jnp.float32)
+    vmem = pl.BlockSpec(memory_space=pltpu.VMEM)
+    hbm = pl.BlockSpec(memory_space=pl.ANY)
     return pl.pallas_call(
-        functools.partial(attend_kernel, scale=1.0 / math.sqrt(HD)),
+        functools.partial(attend_kernel, scale=1.0 / math.sqrt(HD), n_hi=n_hi),
         out_shape=(jax.ShapeDtypeStruct((rows, width), jnp.float32), stats, stats),
-        grid_spec=pltpu.PrefetchScalarGridSpec(
-            num_scalar_prefetch=1,
-            grid=(n_groups,),
-            in_specs=[
-                pl.BlockSpec((rows, width), lambda s, info: (0, 0)),
-                pl.BlockSpec((None, HD, block_len), lambda s, info: (s, 0, 0)),
-                pl.BlockSpec((None, block_len, HD), lambda s, info: (s, 0, 0)),
-                pl.BlockSpec((HD, tree_rows), lambda s, info: (0, 0)),
-                pl.BlockSpec((tree_rows, HD), lambda s, info: (0, 0)),
-                pl.BlockSpec((rows, tree_rows), lambda s, info: (0, 0)),
-            ],
-            out_specs=[
-                pl.BlockSpec((rows, width), lambda s, info: (0, 0)),
-                pl.BlockSpec((heads, rows, HD), lambda s, info: (0, 0, 0)),
-                pl.BlockSpec((heads, rows, HD), lambda s, info: (0, 0, 0)),
-            ],
+        in_specs=[pl.BlockSpec(memory_space=pltpu.SMEM), vmem, hbm, hbm, vmem, vmem, vmem],
+        out_specs=(vmem, vmem, vmem),
+        scratch_shapes=[
+            pltpu.VMEM(keys_t.shape, keys_t.dtype),
+            pltpu.VMEM(values.shape, values.dtype),
+            pltpu.SemaphoreType.DMA((n_hi, 2)),
+            pltpu.SemaphoreType.DMA((n_hi, 2)),
+            pltpu.SemaphoreType.DMA((2,)),
+        ],
+        compiler_params=pltpu.CompilerParams(
+            collective_id=1, has_side_effects=True, vmem_limit_bytes=48 * 1024 * 1024
         ),
-        compiler_params=pltpu.CompilerParams(dimension_semantics=("arbitrary",)),
     )(info, query_block, keys_t, values, tree_keys_t, tree_values, tree_mask)
 
 
@@ -225,20 +267,15 @@
     query_block = exchange_queries(pieces, n_lo, n_head)
     query_block = query_block.reshape(node_count, width)
 
-    both = jnp.concatenate([cache_keys, cache_values], axis=2)
-    mine = lax.all_to_all(both, "rh", split_axis=0, concat_axis=1, tiled=True)[0]
-
     reached = ancestry(parents)
     ancestors = lax.dynamic_index_in_dim(reached, request, 0, keepdims=False)
     ancestors = lax.dynamic_slice_in_dim(ancestors, quarter * rows_owned, rows_owned, 1)
     tree_mask = ancestors.astype(jnp.float32)
     length = lax.dynamic_index_in_dim(cache_lens, request, 0, keepdims=False)
     live_size = lax.dynamic_index_in_dim(tree_sizes, request, 0, keepdims=False)
-    info = jnp.stack([length, request, quarter, n_lo, live_size]).astype(jnp.int32)
-    mine = mine.reshape(n_hi, cache_block, 2 * HD)
-    keys_t = mine[:, :, :HD].transpose(0, 2, 1)
-    values = mine[:, :, HD:]
-    acc, top, den = attend(info, query_block, keys_t, values, tree_keys.T, tree_values, tree_mask)
+    info = jnp.stack([length, jnp.int32(n_lo)]).astype(jnp.int32)
+    keys_t = cache_keys.transpose(0, 2, 1)
+    acc, top, den = attend(info, query_block, keys_t, cache_values, tree_keys.T, tree_values, tree_mask)
     top = top[:, :, 0].T
     den = den[:, :, 0].T
 

time: 172 us -> 157 us (0.913)
  the two profiles are of different devices: /device:TPU:36 before, /device:TPU:1 now
where the time goes in v8:
time: 157 us
  Pallas kernels  117 us (75%)
  local copies, waits for them, and re-layouts  16.2 us (10%)
  waiting for transfers between devices  13.8 us (9%)
  starting transfers between devices  4.56 us (3%)
  matrix products  2.85 us (2%)
  other arithmetic  2.47 us (2%)
    pallas_call x1, Pallas kernels, attend(): pl.pallas_call(functools.partial(attend_kernel, scale=1.0 / math.sqrt(HD)...  95.1 us
    pallas_call x1, Pallas kernels, exchange_queries(): pl.pallas_call(functools.partial(exchange_kernel, n_lo=n_lo, n_head=n_hea...  21.8 us
    all_to_all x1, waiting for transfers between devices, body(): lax.all_to_all(payload, 'rl', split_axis=0, concat_axis=0, tiled=True)  13.8 us
    unnamed x17, local copies, waits for them, and re-layouts  7.6 us
    all_to_all x1, starting transfers between devices, body(): lax.all_to_all(payload, 'rl', split_axis=0, concat_axis=0, tiled=True)  4.56 us
  transfers between devices with their start and end apart: 1, of which 1 were waited for; matrix products, arithmetic and copies ran while one was open for 1% of the time, Pallas kernels for 0%

profile of v8, /device:TPU:1, one launch (start us, length us, event | category | flops | bytes accessed | tf_op | source)
XLA Modules:
  0.0 156.9 jit_solution(17386216867113295405)
XLA Ops:
  0.0 1.3 dynamic_slice.13
  1.3 0.8 copy.18
  2.1 0.9 copy.27
  3.0 0.7 copy.16
  3.7 1.7 %fusion.1 = bf16[8,128,128]{2,1,0:T(8,128)(2,1)S(1)} fusion(s32[8,128]{1,0:T(8,128)} %param.13, pred[128,128]{1,0:T(8,128)(4,1)S(1)} %iota_compare_fusion.1), kind=kOutput, calls=%fused_computation.7 | convolution fusion | flops 67895296 | bytes 282624 | tf_op jit(solution)/shard_map/aij,ajk->aik/dot_general | solution.py:28
  5.5 0.5 fusion.3
  5.9 0.4 fusion.5
  6.4 0.2 fusion.26
  6.6 21.8 %shard_map.82 = bf16[32,64,128]{2,1,0:T(8,128)(2,1)} custom-call(bf16[8,64,128]{2,1,0:T(8,128)(2,1)} %bitcast.43), custom_call_target="tpu_custom_call" | custom-call | tf_op jit(solution)/shard_map/pallas_call | solution.py:233
  28.4 1.3 reshape.45.q_ref
  29.6 0.0 copy-start.5
  29.7 2.9 %copy.17 = bf16[8,1024,128]{1,2,0:T(8,128)(2,1)S(1)} copy(bf16[8,1024,128]{2,1,0:T(8,128)(2,1)} %param.9) | data formatting | bytes 4194304 | tf_op args[1]
  32.5 0.7 pad_add_fusion.info_ref
  33.2 0.1 fusion.22.tmask_ref
  33.3 95.1 %shard_map.83 = (f32[128,2048]{1,0:T(8,128)S(1)}, f32[16,128,128]{2,1,0:T(8,128)S(1)}, f32[16,128,128]{2,1,0:T(8,128)S(1)}) custom-call(s32[2]{0:T(128)S(1)} %pad_add_fusion.info_ref, bf16[128,2048]{1,0:T(8,128)(2,1)S(1)} %reshape.45.q_ref, bf16[8,128,1024]{2,1,0:T(8,128)(2,1)S(1)} %bitcast.38, bf16[8,1024,128]{2,1,0:T(8,128)(2,1)} %v_hbm.1, ...), custom_call_target="tpu_custom_call" | custom-call | tf_op jit(solution)/shard_map/pallas_call | solution.py:163
  128.4 1.0 copy-done
  129.4 1.0 copy-done.2
  130.4 1.0 copy-done.4
  131.4 2.2 %copy.25 = f32[16,128,1]{0,1,2:T(8,128)S(1)} copy(f32[16,128,1]{2,1,0:T(8,128)} %bitcast.40) | data formatting | bytes 16384 | tf_op jit(solution)/shard_map/squeeze | solution.py:280
  133.6 0.9 copy.26
  134.5 1.2 concatenate.3
  135.6 4.6 %all-to-all-start = ((f32[4,32,2080]{2,1,0:T(8,128)}), f32[4,32,2080]{2,1,0:T(8,128)S(1)}, u32[]{:S(2)}, u32[]{:S(2)}) async-start(f32[4,32,2080]{2,1,0:T(8,128)} %bitcast.10), calls=%async_computation | async-start | bytes 2228224 | tf_op jit(solution)/shard_map/all_to_all | solution.py:283
  140.2 0.6 dynamic_slice.12
  140.8 0.7 add_compare_fusion
  141.4 13.8 %all-to-all-done = f32[4,32,2080]{2,1,0:T(8,128)S(1)} async-done(((f32[4,32,2080]{2,1,0:T(8,128)}), f32[4,32,2080]{2,1,0:T(8,128)S(1)}, u32[]{:S(2)}, u32[]{:S(2)}) %all-to-all-start) | async-done | bytes 1064992 | tf_op jit(solution)/shard_map/all_to_all | solution.py:283
  155.2 0.1 slice_reduce_fusion
  155.3 0.1 fusion.19
  155.4 0.3 mul.19
  155.8 0.2 mul.20
  155.9 0.1 fusion.6
  156.0 0.1 div.11
  156.2 0.8 fusion.11
  (11 shorter events, 0.0 us)
Async XLA Ops:
  29.6 3.7 %copy-start.5 = (bf16[32,128]{1,0:T(8,128)(2,1)S(1)}, bf16[32,128]{1,0:T(8,128)(2,1)}, u32[]{:S(2)}) copy-start(bf16[32,128]{1,0:T(8,128)(2,1)} %tv_ref.1) | copy-start | bytes 24580
  128.4 1.0 copy-start
  129.4 1.0 copy-start.2
  130.4 1.0 copy-start.4
  131.4 2.2 %copy-start.3 = (f32[16,128,128]{2,1,0:T(8,128)S(1)}, f32[16,128,128]{2,1,0:T(8,128)}, u32[]{:S(2)}) copy-start(f32[16,128,128]{2,1,0:T(8,128)} %copy-done.2) | copy-start | bytes 3145732
  131.4 3.1 %copy-start.1 = (f32[128,2048]{1,0:T(8,128)S(1)}, f32[128,2048]{1,0:T(8,128)}, u32[]{:S(2)}) copy-start(f32[128,2048]{1,0:T(8,128)} %copy-done) | copy-start | bytes 3145732
  135.6 4.6 %copy-start.6 = (s32[8]{0:T(128)S(1)}, s32[8]{0:T(128)}, u32[]{:S(2)}) copy-start(s32[8]{0:T(128)} %param.14) | copy-start | bytes 100
  135.6 19.6 %all-to-all-start = ((f32[4,32,2080]{2,1,0:T(8,128)}), f32[4,32,2080]{2,1,0:T(8,128)S(1)}, u32[]{:S(2)}, u32[]{:S(2)}) async-start(f32[4,32,2080]{2,1,0:T(8,128)} %bitcast.10), calls=%async_computation | async-start | bytes 2228224 | tf_op jit(solution)/shard_map/all_to_all | solution.py:283

commit v9 on v8

--- a/solution.py
+++ b/solution.py
@@ -31,8 +31,9 @@
 
 
 def attend_kernel(
-    info_ref, q_ref, kt_hbm, v_hbm, tkt_ref, tv_ref, tmask_ref, acc_ref, top_ref, den_ref,
-    kslots, vslots, send_sem, recv_sem, own_sem, *, scale, n_hi,
+    info_ref, q_ref, kt_hbm, v_hbm, tkt_ref, tv_ref, tmask_ref, acc_out, stat_out,
+    kslots, vslots, send_sem, recv_sem, own_sem, acc_ref, top_ref, den_ref, stats,
+    acc_slots, stat_slots, fsend, frecv, fown, *, scale, n_hi, n_quarters,
 ):
     request = lax.axis_index("rh")
     quarter = lax.axis_index("rl")
@@ -53,7 +54,15 @@
                 barrier, inc=1, device_id=(t, quarter, head_axis), device_id_type=mesh
             )
 
-    pl.semaphore_wait(barrier, n_hi - 1)
+    for r in range(n_quarters):
+
+        @pl.when(r != quarter)
+        def _():
+            pl.semaphore_signal(
+                barrier, inc=1, device_id=(request, r, head_axis), device_id_type=mesh
+            )
+
+    pl.semaphore_wait(barrier, n_hi - 1 + n_quarters - 1)
 
     def pushes(t):
         dest = (t, quarter, head_axis)
@@ -152,24 +161,83 @@
         for copy in pushes(t):
             copy.wait_send()
 
-
-def attend(info, query_block, keys_t, values, tree_keys_t, tree_values, tree_mask):
+    lane = lax.broadcasted_iota(jnp.int32, (rows, HD), 1)
+    tops = jnp.full((rows, HD), negative_fill, jnp.float32)
+    dens = jnp.zeros((rows, HD), jnp.float32)
+    for h in range(heads):
+        tops = jnp.where(lane == h, top_ref[h], tops)
+        dens = jnp.where(lane == h, den_ref[h], dens)
+    stats[0] = tops
+    stats[1] = dens
+
+    quarter_rows = rows // n_quarters
+
+    def quarter_copies(r, slot, device):
+        piece = pl.ds(r * quarter_rows, quarter_rows)
+        return (
+            pltpu.make_async_remote_copy(
+                acc_ref.at[piece, :], acc_slots.at[slot], fsend.at[r, 0], frecv.at[slot, 0],
+                device_id=device, device_id_type=mesh,
+            ),
+            pltpu.make_async_remote_copy(
+                stats.at[:, piece, :], stat_slots.at[slot], fsend.at[r, 1], frecv.at[slot, 1],
+                device_id=device, device_id_type=mesh,
+            ),
+        )
+
+    for r in range(n_quarters):
+        for copy in quarter_copies(r, quarter, (request, r, head_axis)):
+            pl.when(r != quarter)(copy.start)
+    mine = pl.ds(pl.multiple_of(quarter * quarter_rows, quarter_rows), quarter_rows)
+    keep_acc = pltpu.make_async_copy(acc_ref.at[mine, :], acc_slots.at[quarter], fown.at[0])
+    keep_stat = pltpu.make_async_copy(stats.at[:, mine, :], stat_slots.at[quarter], fown.at[1])
+    keep_acc.start()
+    keep_stat.start()
+    keep_acc.wait()
+    keep_stat.wait()
+    for r in range(n_quarters):
+        for copy in quarter_copies(r, r, (request, r, head_axis)):
+            pl.when(r != quarter)(copy.wait_recv)
+    for r in range(n_quarters):
+        for copy in quarter_copies(r, quarter, (request, r, head_axis)):
+            pl.when(r != quarter)(copy.wait_send)
+    acc_out[...] = acc_slots[...]
+    stat_out[...] = stat_slots[...]
+
+
+def attend(info, query_block, keys_t, values, tree_keys_t, tree_values, tree_mask, n_quarters):
     rows, width = query_block.shape
     heads = width // HD
     n_hi = keys_t.shape[0]
-    stats = jax.ShapeDtypeStruct((heads, rows, HD), jnp.float32)
+    quarter_rows = rows // n_quarters
     vmem = pl.BlockSpec(memory_space=pltpu.VMEM)
     hbm = pl.BlockSpec(memory_space=pl.ANY)
+    acc_shape = (n_quarters, quarter_rows, width)
+    stat_shape = (n_quarters, 2, quarter_rows, HD)
     return pl.pallas_call(
-        functools.partial(attend_kernel, scale=1.0 / math.sqrt(HD), n_hi=n_hi),
-        out_shape=(jax.ShapeDtypeStruct((rows, width), jnp.float32), stats, stats),
+        functools.partial(
+            attend_kernel, scale=1.0 / math.sqrt(HD), n_hi=n_hi, n_quarters=n_quarters
+        ),
+        out_shape=(
+            jax.ShapeDtypeStruct(acc_shape, jnp.float32),
+            jax.ShapeDtypeStruct(stat_shape, jnp.float32),
+        ),
         in_specs=[pl.BlockSpec(memory_space=pltpu.SMEM), vmem, hbm, hbm, vmem, vmem, vmem],
-        out_specs=(vmem, vmem, vmem),
+        out_specs=(vmem, vmem),
         scratch_shapes=[
             pltpu.VMEM(keys_t.shape, keys_t.dtype),
             pltpu.VMEM(values.shape, values.dtype),
             pltpu.SemaphoreType.DMA((n_hi, 2)),
             pltpu.SemaphoreType.DMA((n_hi, 2)),
+            pltpu.SemaphoreType.DMA((2,)),
+            pltpu.VMEM((rows, width), jnp.float32),
+            pltpu.VMEM((heads, rows, HD), jnp.float32),
+            pltpu.VMEM((heads, rows, HD), jnp.float32),
+            pltpu.VMEM((2, rows, HD), jnp.float32),
+            pltpu.VMEM(acc_shape, jnp.float32),
+            pltpu.VMEM(stat_shape, jnp.float32),
+            pltpu.SemaphoreType.DMA((n_quarters, 2)),
+            pltpu.SemaphoreType.DMA((n_quarters, 2)),
             pltpu.SemaphoreType.DMA((2,)),
         ],
         compiler_params=pltpu.CompilerParams(
@@ -275,15 +343,12 @@
     live_size = lax.dynamic_index_in_dim(tree_sizes, request, 0, keepdims=False)
     info = jnp.stack([length, jnp.int32(n_lo)]).astype(jnp.int32)
     keys_t = cache_keys.transpose(0, 2, 1)
-    acc, top, den = attend(info, query_block, keys_t, cache_values, tree_keys.T, tree_values, tree_mask)
-    top = top[:, :, 0].T
-    den = den[:, :, 0].T
-
-    payload = jnp.concatenate([acc, den, top], axis=1).reshape(n_lo, rows_owned, heads_local * HD + 2 * heads_local)
-    gathered = lax.all_to_all(payload, "rl", split_axis=0, concat_axis=0, tiled=True)
-    got_acc = gathered[:, :, : heads_local * HD].reshape(n_lo, rows_owned, heads_local, HD)
-    got_den = gathered[:, :, heads_local * HD : heads_local * HD + heads_local]
-    got_top = gathered[:, :, heads_local * HD + heads_local :]
+    got_acc, got_stats = attend(
+        info, query_block, keys_t, cache_values, tree_keys.T, tree_values, tree_mask, n_lo
+    )
+    got_acc = got_acc.reshape(n_lo, rows_owned, heads_local, HD)
+    got_top = got_stats[:, 0, :, :heads_local]
+    got_den = got_stats[:, 1, :, :heads_local]
     highest = jnp.max(got_top, axis=0)
     scale = jnp.exp(got_top - highest)
     num = jnp.sum(scale[..., None] * got_acc, axis=0)

time: 157 us -> 152 us (0.968); the launches traced: 157 us -> 150 us
  Pallas kernels: 117 us -> 132 us
  waiting for transfers between devices: 13.8 us -> 0 us
  starting transfers between devices: 4.56 us -> 0 us
  local copies, waits for them, and re-layouts: 16.2 us -> 12.7 us
    pallas_call x1, Pallas kernels: 95.1 us -> 110 us  [attend(): pl.pallas_call(functools.partial(attend_kernel, scale=1.0 / math.sqrt(HD)...]
    all_to_all x1 -> x0, waiting for transfers between devices: 13.8 us -> none  [body(): lax.all_to_all(payload, 'rl', split_axis=0, concat_axis=0, tiled=True)]
    all_to_all x1 -> x0, starting transfers between devices: 4.56 us -> none  [body(): lax.all_to_all(payload, 'rl', split_axis=0, concat_axis=0, tiled=True)]
    squeeze x2 -> x0, local copies, waits for them, and re-layouts: 3.07 us -> none  [the longest x1 2.2 us: body(): den = den[:, :, 0].T]
    unnamed x17 -> x11, local copies, waits for them, and re-layouts: 7.6 us -> 7.72 us
  transfers between devices with their start and end apart: 1 -> 0, of which waited for: 1 -> 0; matrix products, arithmetic and copies ran while one was open for 1% -> 0% of each run, Pallas kernels for 0% -> 0%
where the time goes in v9:
time: 152 us; the launch traced here: 150 us
  Pallas kernels  132 us (87%)
  local copies, waits for them, and re-layouts  12.7 us (8%)
  matrix products  2.85 us (2%)
  other arithmetic  2.36 us (2%)
    pallas_call x1, Pallas kernels, attend(): pl.pallas_call(functools.partial(attend_kernel, scale=1.0 / math.sqrt(HD)...  110 us
    pallas_call x1, Pallas kernels, exchange_queries(): pl.pallas_call(functools.partial(exchange_kernel, n_lo=n_lo, n_head=n_hea...  21.8 us
    unnamed x11, local copies, waits for them, and re-layouts  7.72 us

profile of v9, /device:TPU:1, one launch (start us, length us, event | category | flops | bytes accessed | tf_op | source)
XLA Modules:
  0.0 149.9 jit_solution(3893453702472495187)
XLA Ops:
  0.0 1.2 dynamic_slice.13
  1.2 0.7 pad_add_fusion.info_ref
  2.0 1.2 dynamic_slice.12
  3.2 0.7 add_compare_fusion
  3.9 0.8 copy.11
  4.7 0.9 copy.17
  5.6 0.7 copy.9
  6.3 1.7 %fusion.1 = bf16[8,128,128]{2,1,0:T(8,128)(2,1)S(1)} fusion(s32[8,128]{1,0:T(8,128)} %param.13, pred[128,128]{1,0:T(8,128)(4,1)S(1)} %iota_compare_fusion.1), kind=kOutput, calls=%fused_computation.7 | convolution fusion | flops 67895296 | bytes 282624 | tf_op jit(solution)/shard_map/aij,ajk->aik/dot_general | solution.py:28
  8.0 0.4 fusion.3
  8.5 0.4 fusion.5
  8.9 0.2 fusion.27
  9.2 0.1 fusion.22.tmask_ref
  9.2 21.8 %shard_map.82 = bf16[32,64,128]{2,1,0:T(8,128)(2,1)} custom-call(bf16[8,64,128]{2,1,0:T(8,128)(2,1)} %bitcast.41), custom_call_target="tpu_custom_call" | custom-call | tf_op jit(solution)/shard_map/pallas_call | solution.py:301
  31.0 1.3 reshape.47.q_ref
  32.3 0.0 copy-start.3
  32.3 2.9 %copy.10 = bf16[8,1024,128]{1,2,0:T(8,128)(2,1)S(1)} copy(bf16[8,1024,128]{2,1,0:T(8,128)(2,1)} %param.9) | data formatting | bytes 4194304 | tf_op args[1]
  35.2 0.0 copy-done.3
  35.2 0.0 copy-start
  35.2 1.6 %copy-done = bf16[8,1024,128]{2,1,0:T(8,128)(2,1)S(1)} copy-done((bf16[8,1024,128]{2,1,0:T(8,128)(2,1)S(1)}, bf16[8,1024,128]{2,1,0:T(8,128)(2,1)}, u32[]{:S(2)}) %copy-start) | copy-done | bytes 2097176
  36.8 110.0 %shard_map.83 = (f32[4,32,2048]{2,1,0:T(8,128)S(1)}, f32[4,2,32,128]{3,2,1,0:T(8,128)S(1)}) custom-call(s32[2]{0:T(128)S(1)} %pad_add_fusion.info_ref, bf16[128,2048]{1,0:T(8,128)(2,1)S(1)} %reshape.47.q_ref, bf16[8,128,1024]{2,1,0:T(8,128)(2,1)S(1)} %bitcast.38, bf16[8,1024,128]{2,1,0:T(8,128)(2,1)S(1)} %copy-done, bf16[128,32]{1,0:T(8,128)(2,1)S(1)} %bitcast.39, ...), custom_call_target="tpu_custom_call" | custom-call | tf_op jit(solution)/shard_map/pallas_call | solution.py:217
  146.8 0.0 copy-start.1
  146.8 1.0 copy-done.1
  147.8 0.0 copy-start.2
  147.8 0.1 div.11
  147.9 0.3 mul.19
  148.3 0.2 mul.20
  148.5 0.5 copy-done.2
  149.0 0.1 multiply_reduce_fusion
  149.1 0.8 fusion.10
  (3 shorter events, 0.0 us)
Async XLA Ops:
  32.3 2.9 %copy-start.3 = (bf16[32,128]{1,0:T(8,128)(2,1)S(1)}, bf16[32,128]{1,0:T(8,128)(2,1)}, u32[]{:S(2)}) copy-start(bf16[32,128]{1,0:T(8,128)(2,1)} %tv_ref.1) | copy-start | bytes 24580
  35.2 1.6 %copy-start = (bf16[8,1024,128]{2,1,0:T(8,128)(2,1)S(1)}, bf16[8,1024,128]{2,1,0:T(8,128)(2,1)}, u32[]{:S(2)}) copy-start(bf16[8,1024,128]{2,1,0:T(8,128)(2,1)} %v_hbm.1) | copy-start | bytes 6291460
  146.8 1.0 copy-start.1
  147.8 1.2 copy-start.2

commit v10 on v9

--- a/solution.py
+++ b/solution.py
@@ -94,21 +94,20 @@
         start = (s * n_lo + quarter) * block_len
         kt_ref = kslots.at[s]
         v_ref = vslots.at[s]
+        pos = start + lax.broadcasted_iota(jnp.int32, (1, block_len), 1)
+        bias = jnp.where(pos < length, 0.0, negative_fill)
 
         def head(h, carry):
             col = pl.multiple_of(h * HD, HD)
             qh = q_ref[:, pl.ds(col, HD)]
-            sc = jnp.dot(qh, kt_ref[...], preferred_element_type=jnp.float32) * scale
-            pos = start + lax.broadcasted_iota(jnp.int32, sc.shape, 1)
-            live = pos < length
-            sc = jnp.where(live, sc, negative_fill)
+            sc = jnp.dot(qh, kt_ref[...], preferred_element_type=jnp.float32) * scale + bias
             peak = jnp.max(sc, axis=1, keepdims=True)
             if with_tree:
                 st = jnp.dot(qh, tkt_ref[...], preferred_element_type=jnp.float32) * scale
                 tlive = tmask_ref[...] > 0.5
                 st = jnp.where(tlive, st, negative_fill)
                 peak = jnp.maximum(peak, jnp.max(st, axis=1, keepdims=True))
-            w = jnp.where(live, jnp.exp(sc - peak), 0.0)
+            w = jnp.exp(sc - jnp.maximum(peak, 0.1 * negative_fill))
             tot = jnp.sum(w, axis=1, keepdims=True)
             gs = jnp.dot(w.astype(jnp.bfloat16), v_ref[...], preferred_element_type=jnp.float32)
             if with_tree:

time: 152 us -> 151 us (level)
  no operation moved by 1% of the time
where the time goes in v10:
time: 151 us; the launch traced here: 149 us
  Pallas kernels  131 us (87%)
  local copies, waits for them, and re-layouts  12.7 us (8%)
  matrix products  2.85 us (2%)
  other arithmetic  2.36 us (2%)
    pallas_call x1, Pallas kernels, attend(): pl.pallas_call(functools.partial(attend_kernel, scale=1.0 / math.sqrt(HD)...  109 us
    pallas_call x1, Pallas kernels, exchange_queries(): pl.pallas_call(functools.partial(exchange_kernel, n_lo=n_lo, n_head=n_hea...  21.8 us
    unnamed x11, local copies, waits for them, and re-layouts  7.72 us

profile of v10, /device:TPU:1, one launch (start us, length us, event | category | flops | bytes accessed | tf_op | source)
XLA Modules:
  0.0 148.8 jit_solution(18075566184733102587)
XLA Ops:
  0.0 1.2 dynamic_slice.13
  1.2 0.7 pad_add_fusion.info_ref
  2.0 1.2 dynamic_slice.12
  3.2 0.7 add_compare_fusion
  3.9 0.8 copy.11
  4.7 0.9 copy.17
  5.6 0.7 copy.9
  6.3 1.7 %fusion.1 = bf16[8,128,128]{2,1,0:T(8,128)(2,1)S(1)} fusion(s32[8,128]{1,0:T(8,128)} %param.13, pred[128,128]{1,0:T(8,128)(4,1)S(1)} %iota_compare_fusion.1), kind=kOutput, calls=%fused_computation.7 | convolution fusion | flops 67895296 | bytes 282624 | tf_op jit(solution)/shard_map/aij,ajk->aik/dot_general | solution.py:28
  8.0 0.4 fusion.3
  8.5 0.4 fusion.5
  8.9 0.2 fusion.27
  9.2 0.1 fusion.22.tmask_ref
  9.2 21.8 %shard_map.82 = bf16[32,64,128]{2,1,0:T(8,128)(2,1)} custom-call(bf16[8,64,128]{2,1,0:T(8,128)(2,1)} %bitcast.41), custom_call_target="tpu_custom_call" | custom-call | tf_op jit(solution)/shard_map/pallas_call | solution.py:300
  31.0 1.3 reshape.47.q_ref
  32.3 0.0 copy-start.3
  32.3 2.9 %copy.10 = bf16[8,1024,128]{1,2,0:T(8,128)(2,1)S(1)} copy(bf16[8,1024,128]{2,1,0:T(8,128)(2,1)} %param.9) | data formatting | bytes 4194304 | tf_op args[1]
  35.2 0.0 copy-done.3
  35.2 0.0 copy-start
  35.2 1.6 %copy-done = bf16[8,1024,128]{2,1,0:T(8,128)(2,1)S(1)} copy-done((bf16[8,1024,128]{2,1,0:T(8,128)(2,1)S(1)}, bf16[8,1024,128]{2,1,0:T(8,128)(2,1)}, u32[]{:S(2)}) %copy-start) | copy-done | bytes 2097176
  36.8 109.0 %shard_map.83 = (f32[4,32,2048]{2,1,0:T(8,128)S(1)}, f32[4,2,32,128]{3,2,1,0:T(8,128)S(1)}) custom-call(s32[2]{0:T(128)S(1)} %pad_add_fusion.info_ref, bf16[128,2048]{1,0:T(8,128)(2,1)S(1)} %reshape.47.q_ref, bf16[8,128,1024]{2,1,0:T(8,128)(2,1)S(1)} %bitcast.38, bf16[8,1024,128]{2,1,0:T(8,128)(2,1)S(1)} %copy-done, bf16[128,32]{1,0:T(8,128)(2,1)S(1)} %bitcast.39, ...), custom_call_target="tpu_custom_call" | custom-call | tf_op jit(solution)/shard_map/pallas_call | solution.py:216
  145.8 0.0 copy-start.1
  145.8 1.0 copy-done.1
  146.8 0.0 copy-start.2
  146.8 0.1 div.11
  146.9 0.3 mul.19
  147.3 0.2 mul.20
  147.4 0.5 copy-done.2
  148.0 0.1 multiply_reduce_fusion
  148.1 0.8 fusion.10
  (3 shorter events, 0.0 us)
Async XLA Ops:
  32.3 2.9 %copy-start.3 = (bf16[32,128]{1,0:T(8,128)(2,1)S(1)}, bf16[32,128]{1,0:T(8,128)(2,1)}, u32[]{:S(2)}) copy-start(bf16[32,128]{1,0:T(8,128)(2,1)} %tv_ref.1) | copy-start | bytes 24580
  35.2 1.6 %copy-start = (bf16[8,1024,128]{2,1,0:T(8,128)(2,1)S(1)}, bf16[8,1024,128]{2,1,0:T(8,128)(2,1)}, u32[]{:S(2)}) copy-start(bf16[8,1024,128]{2,1,0:T(8,128)(2,1)} %v_hbm.1) | copy-start | bytes 6291460
  145.8 1.0 copy-start.1
  146.8 1.2 copy-start.2

commit v11 on v10

--- a/solution.py
+++ b/solution.py
@@ -77,7 +77,8 @@
             ),
         )
 
-    for shift in range(1, n_hi):
+    ahead = 2
+    for shift in range(1, min(ahead, n_hi - 1) + 1):
         t = lax.rem(request + shift, n_hi)
         for copy in pushes(t):
             copy.start()
@@ -148,6 +149,12 @@
         )
 
     def arrival(step, carry):
+        @pl.when(step + ahead + 1 < n_hi)
+        def _():
+            t = lax.rem(request + step + ahead + 1, n_hi)
+            for copy in pushes(t):
+                copy.start()
+
         s = lax.rem(request - step - 1 + n_hi, n_hi)
         for copy in landed(s):
             copy.wait_recv()

time: 151 us -> 150 us (level)
  no operation moved by 1% of the time
where the time goes in v11:
time: 150 us; the launch traced here: 149 us
  Pallas kernels  131 us (87%)
  local copies, waits for them, and re-layouts  12.7 us (8%)
  matrix products  2.85 us (2%)
  other arithmetic  2.36 us (2%)
    pallas_call x1, Pallas kernels, attend(): pl.pallas_call(functools.partial(attend_kernel, scale=1.0 / math.sqrt(HD)...  109 us
    pallas_call x1, Pallas kernels, exchange_queries(): pl.pallas_call(functools.partial(exchange_kernel, n_lo=n_lo, n_head=n_hea...  21.8 us
    unnamed x11, local copies, waits for them, and re-layouts  7.72 us

profile of v11, /device:TPU:1, one launch (start us, length us, event | category | flops | bytes accessed | tf_op | source)
XLA Modules:
  0.0 148.9 jit_solution(12506921832269240436)
XLA Ops:
  0.0 1.2 dynamic_slice.13
  1.2 0.7 pad_add_fusion.info_ref
  2.0 1.2 dynamic_slice.12
  3.2 0.7 add_compare_fusion
  3.9 0.8 copy.11
  4.7 0.9 copy.17
  5.6 0.7 copy.9
  6.3 1.7 %fusion.1 = bf16[8,128,128]{2,1,0:T(8,128)(2,1)S(1)} fusion(s32[8,128]{1,0:T(8,128)} %param.13, pred[128,128]{1,0:T(8,128)(4,1)S(1)} %iota_compare_fusion.1), kind=kOutput, calls=%fused_computation.7 | convolution fusion | flops 67895296 | bytes 282624 | tf_op jit(solution)/shard_map/aij,ajk->aik/dot_general | solution.py:28
  8.0 0.4 fusion.3
  8.5 0.4 fusion.5
  8.9 0.2 fusion.27
  9.2 0.1 fusion.22.tmask_ref
  9.2 21.8 %shard_map.82 = bf16[32,64,128]{2,1,0:T(8,128)(2,1)} custom-call(bf16[8,64,128]{2,1,0:T(8,128)(2,1)} %bitcast.41), custom_call_target="tpu_custom_call" | custom-call | tf_op jit(solution)/shard_map/pallas_call | solution.py:307
  31.0 1.3 reshape.47.q_ref
  32.3 0.0 copy-start.3
  32.3 2.9 %copy.10 = bf16[8,1024,128]{1,2,0:T(8,128)(2,1)S(1)} copy(bf16[8,1024,128]{2,1,0:T(8,128)(2,1)} %param.9) | data formatting | bytes 4194304 | tf_op args[1]
  35.2 0.0 copy-done.3
  35.2 0.0 copy-start
  35.2 1.6 %copy-done = bf16[8,1024,128]{2,1,0:T(8,128)(2,1)S(1)} copy-done((bf16[8,1024,128]{2,1,0:T(8,128)(2,1)S(1)}, bf16[8,1024,128]{2,1,0:T(8,128)(2,1)}, u32[]{:S(2)}) %copy-start) | copy-done | bytes 2097176
  36.8 109.0 %shard_map.83 = (f32[4,32,2048]{2,1,0:T(8,128)S(1)}, f32[4,2,32,128]{3,2,1,0:T(8,128)S(1)}) custom-call(s32[2]{0:T(128)S(1)} %pad_add_fusion.info_ref, bf16[128,2048]{1,0:T(8,128)(2,1)S(1)} %reshape.47.q_ref, bf16[8,128,1024]{2,1,0:T(8,128)(2,1)S(1)} %bitcast.38, bf16[8,1024,128]{2,1,0:T(8,128)(2,1)S(1)} %copy-done, bf16[128,32]{1,0:T(8,128)(2,1)S(1)} %bitcast.39, ...), custom_call_target="tpu_custom_call" | custom-call | tf_op jit(solution)/shard_map/pallas_call | solution.py:223
  145.8 0.0 copy-start.1
  145.8 1.0 copy-done.1
  146.8 0.0 copy-start.2
  146.9 0.1 div.11
  147.0 0.3 mul.19
  147.3 0.2 mul.20
  147.5 0.5 copy-done.2
  148.0 0.1 multiply_reduce_fusion
  148.1 0.8 fusion.10
  (3 shorter events, 0.0 us)
Async XLA Ops:
  32.3 2.9 %copy-start.3 = (bf16[32,128]{1,0:T(8,128)(2,1)S(1)}, bf16[32,128]{1,0:T(8,128)(2,1)}, u32[]{:S(2)}) copy-start(bf16[32,128]{1,0:T(8,128)(2,1)} %tv_ref.1) | copy-start | bytes 24580
  35.2 1.6 %copy-start = (bf16[8,1024,128]{2,1,0:T(8,128)(2,1)S(1)}, bf16[8,1024,128]{2,1,0:T(8,128)(2,1)}, u32[]{:S(2)}) copy-start(bf16[8,1024,128]{2,1,0:T(8,128)(2,1)} %v_hbm.1) | copy-start | bytes 6291460
  145.8 1.0 copy-start.1
  146.8 1.2 copy-start.2

commit v12 on v11

--- a/solution.py
+++ b/solution.py
@@ -129,7 +129,7 @@
             top_ref[h] = jnp.broadcast_to(new, (rows, HD))
             return carry
 
-        lax.fori_loop(0, heads, head, 0)
+        lax.fori_loop(0, heads, head, 0, unroll=2)
 
     own_k.wait()
     own_v.wait()

time: 150 us -> 141 us (0.940)
  Pallas kernels: 131 us -> 123 us
    pallas_call x1, Pallas kernels: 109 us -> 101 us  [attend(): pl.pallas_call(functools.partial(attend_kernel, scale=1.0 / math.sqrt(HD)...]
where the time goes in v12:
time: 141 us
  Pallas kernels  123 us (87%)
  local copies, waits for them, and re-layouts  12.7 us (9%)
  matrix products  2.85 us (2%)
  other arithmetic  2.36 us (2%)
    pallas_call x1, Pallas kernels, attend(): pl.pallas_call(functools.partial(attend_kernel, scale=1.0 / math.sqrt(HD)...  101 us
    pallas_call x1, Pallas kernels, exchange_queries(): pl.pallas_call(functools.partial(exchange_kernel, n_lo=n_lo, n_head=n_hea...  21.8 us
    unnamed x11, local copies, waits for them, and re-layouts  7.72 us
    dot_general x4, matrix products, ancestry(): jnp.einsum('aij,ajk->aik', reached, reached, preferred_element_type=jnp.f...  2.85 us

profile of v12, /device:TPU:1, one launch (start us, length us, event | category | flops | bytes accessed | tf_op | source)
XLA Modules:
  0.0 140.6 jit_solution(1973898704938875696)
XLA Ops:
  0.0 1.2 dynamic_slice.13
  1.2 0.7 pad_add_fusion.info_ref
  2.0 1.2 dynamic_slice.12
  3.2 0.7 add_compare_fusion
  3.9 0.8 copy.11
  4.7 0.9 copy.17
  5.6 0.7 copy.9
  6.3 1.7 %fusion.1 = bf16[8,128,128]{2,1,0:T(8,128)(2,1)S(1)} fusion(s32[8,128]{1,0:T(8,128)} %param.13, pred[128,128]{1,0:T(8,128)(4,1)S(1)} %iota_compare_fusion.1), kind=kOutput, calls=%fused_computation.7 | convolution fusion | flops 67895296 | bytes 282624 | tf_op jit(solution)/shard_map/aij,ajk->aik/dot_general | solution.py:28
  8.0 0.4 fusion.3
  8.5 0.4 fusion.5
  8.9 0.2 fusion.27
  9.2 0.1 fusion.22.tmask_ref
  9.2 21.8 %shard_map.82 = bf16[32,64,128]{2,1,0:T(8,128)(2,1)} custom-call(bf16[8,64,128]{2,1,0:T(8,128)(2,1)} %bitcast.41), custom_call_target="tpu_custom_call" | custom-call | tf_op jit(solution)/shard_map/pallas_call | solution.py:307
  31.0 1.3 reshape.47.q_ref
  32.3 0.0 copy-start.3
  32.3 2.9 %copy.10 = bf16[8,1024,128]{1,2,0:T(8,128)(2,1)S(1)} copy(bf16[8,1024,128]{2,1,0:T(8,128)(2,1)} %param.9) | data formatting | bytes 4194304 | tf_op args[1]
  35.2 0.0 copy-done.3
  35.2 0.0 copy-start
  35.2 1.6 %copy-done = bf16[8,1024,128]{2,1,0:T(8,128)(2,1)S(1)} copy-done((bf16[8,1024,128]{2,1,0:T(8,128)(2,1)S(1)}, bf16[8,1024,128]{2,1,0:T(8,128)(2,1)}, u32[]{:S(2)}) %copy-start) | copy-done | bytes 2097176
  36.8 100.7 %shard_map.83 = (f32[4,32,2048]{2,1,0:T(8,128)S(1)}, f32[4,2,32,128]{3,2,1,0:T(8,128)S(1)}) custom-call(s32[2]{0:T(128)S(1)} %pad_add_fusion.info_ref, bf16[128,2048]{1,0:T(8,128)(2,1)S(1)} %reshape.47.q_ref, bf16[8,128,1024]{2,1,0:T(8,128)(2,1)S(1)} %bitcast.38, bf16[8,1024,128]{2,1,0:T(8,128)(2,1)S(1)} %copy-done, bf16[128,32]{1,0:T(8,128)(2,1)S(1)} %bitcast.39, ...), custom_call_target="tpu_custom_call" | custom-call | tf_op jit(solution)/shard_map/pallas_call | solution.py:223
  137.5 0.0 copy-start.1
  137.5 1.0 copy-done.1
  138.5 0.0 copy-start.2
  138.6 0.1 div.11
  138.7 0.3 mul.19
  139.0 0.2 mul.20
  139.2 0.5 copy-done.2
  139.7 0.1 multiply_reduce_fusion
  139.8 0.8 fusion.10
  (3 shorter events, 0.0 us)
Async XLA Ops:
  32.3 2.9 %copy-start.3 = (bf16[32,128]{1,0:T(8,128)(2,1)S(1)}, bf16[32,128]{1,0:T(8,128)(2,1)}, u32[]{:S(2)}) copy-start(bf16[32,128]{1,0:T(8,128)(2,1)} %tv_ref.1) | copy-start | bytes 24580
  35.2 1.6 %copy-start = (bf16[8,1024,128]{2,1,0:T(8,128)(2,1)S(1)}, bf16[8,1024,128]{2,1,0:T(8,128)(2,1)}, u32[]{:S(2)}) copy-start(bf16[8,1024,128]{2,1,0:T(8,128)(2,1)} %v_hbm.1) | copy-start | bytes 6291460
  137.5 1.0 copy-start.1
  138.5 1.2 copy-start.2

commit v13 on v12

--- a/solution.py
+++ b/solution.py
@@ -129,7 +129,7 @@
             top_ref[h] = jnp.broadcast_to(new, (rows, HD))
             return carry
 
-        lax.fori_loop(0, heads, head, 0, unroll=2)
+        lax.fori_loop(0, heads, head, 0, unroll=4)
 
     own_k.wait()
     own_v.wait()

time: 141 us -> 139 us (0.986); the launches traced: 141 us -> 136 us
  Pallas kernels: 123 us -> 118 us
    pallas_call x1, Pallas kernels: 101 us -> 96 us  [attend(): pl.pallas_call(functools.partial(attend_kernel, scale=1.0 / math.sqrt(HD)...]
where the time goes in v13:
time: 139 us; the launch traced here: 136 us
  Pallas kernels  118 us (85%)
  local copies, waits for them, and re-layouts  12.7 us (9%)
  matrix products  2.85 us (2%)
  other arithmetic  2.36 us (2%)
    pallas_call x1, Pallas kernels, attend(): pl.pallas_call(functools.partial(attend_kernel, scale=1.0 / math.sqrt(HD)...  96 us
    pallas_call x1, Pallas kernels, exchange_queries(): pl.pallas_call(functools.partial(exchange_kernel, n_lo=n_lo, n_head=n_hea...  21.8 us
    unnamed x11, local copies, waits for them, and re-layouts  7.72 us
    dot_general x4, matrix products, ancestry(): jnp.einsum('aij,ajk->aik', reached, reached, preferred_element_type=jnp.f...  2.85 us

profile of v13, /device:TPU:1, one launch (start us, length us, event | category | flops | bytes accessed | tf_op | source)
XLA Modules:
  0.0 135.9 jit_solution(3865412577726401619)
XLA Ops:
  0.0 1.2 dynamic_slice.13
  1.2 0.7 pad_add_fusion.info_ref
  2.0 1.2 dynamic_slice.12
  3.2 0.7 add_compare_fusion
  3.9 0.8 copy.11
  4.7 0.9 copy.17
  5.6 0.7 copy.9
  6.3 1.7 %fusion.1 = bf16[8,128,128]{2,1,0:T(8,128)(2,1)S(1)} fusion(s32[8,128]{1,0:T(8,128)} %param.13, pred[128,128]{1,0:T(8,128)(4,1)S(1)} %iota_compare_fusion.1), kind=kOutput, calls=%fused_computation.7 | convolution fusion | flops 67895296 | bytes 282624 | tf_op jit(solution)/shard_map/aij,ajk->aik/dot_general | solution.py:28
  8.0 0.4 fusion.3
  8.5 0.4 fusion.5
  8.9 0.2 fusion.27
  9.2 0.1 fusion.22.tmask_ref
  9.2 21.8 %shard_map.82 = bf16[32,64,128]{2,1,0:T(8,128)(2,1)} custom-call(bf16[8,64,128]{2,1,0:T(8,128)(2,1)} %bitcast.41), custom_call_target="tpu_custom_call" | custom-call | tf_op jit(solution)/shard_map/pallas_call | solution.py:307
  31.0 1.3 reshape.47.q_ref
  32.3 0.0 copy-start.3
  32.3 2.9 %copy.10 = bf16[8,1024,128]{1,2,0:T(8,128)(2,1)S(1)} copy(bf16[8,1024,128]{2,1,0:T(8,128)(2,1)} %param.9) | data formatting | bytes 4194304 | tf_op args[1]
  35.2 0.0 copy-done.3
  35.2 0.0 copy-start
  35.2 1.6 %copy-done = bf16[8,1024,128]{2,1,0:T(8,128)(2,1)S(1)} copy-done((bf16[8,1024,128]{2,1,0:T(8,128)(2,1)S(1)}, bf16[8,1024,128]{2,1,0:T(8,128)(2,1)}, u32[]{:S(2)}) %copy-start) | copy-done | bytes 2097176
  36.8 96.0 %shard_map.83 = (f32[4,32,2048]{2,1,0:T(8,128)S(1)}, f32[4,2,32,128]{3,2,1,0:T(8,128)S(1)}) custom-call(s32[2]{0:T(128)S(1)} %pad_add_fusion.info_ref, bf16[128,2048]{1,0:T(8,128)(2,1)S(1)} %reshape.47.q_ref, bf16[8,128,1024]{2,1,0:T(8,128)(2,1)S(1)} %bitcast.38, bf16[8,1024,128]{2,1,0:T(8,128)(2,1)S(1)} %copy-done, bf16[128,32]{1,0:T(8,128)(2,1)S(1)} %bitcast.39, ...), custom_call_target="tpu_custom_call" | custom-call | tf_op jit(solution)/shard_map/pallas_call | solution.py:223
  132.8 0.0 copy-start.1
  132.8 1.0 copy-done.1
  133.8 0.0 copy-start.2
  133.8 0.1 div.11
  133.9 0.3 mul.19
  134.3 0.2 mul.20
  134.5 0.5 copy-done.2
  135.0 0.1 multiply_reduce_fusion
  135.1 0.8 fusion.10
  (3 shorter events, 0.0 us)
Async XLA Ops:
  32.3 2.9 %copy-start.3 = (bf16[32,128]{1,0:T(8,128)(2,1)S(1)}, bf16[32,128]{1,0:T(8,128)(2,1)}, u32[]{:S(2)}) copy-start(bf16[32,128]{1,0:T(8,128)(2,1)} %tv_ref.1) | copy-start | bytes 24580
  35.2 1.6 %copy-start = (bf16[8,1024,128]{2,1,0:T(8,128)(2,1)S(1)}, bf16[8,1024,128]{2,1,0:T(8,128)(2,1)}, u32[]{:S(2)}) copy-start(bf16[8,1024,128]{2,1,0:T(8,128)(2,1)} %v_hbm.1) | copy-start | bytes 6291460
  132.8 1.0 copy-start.1
  133.8 1.2 copy-start.2

commit v14 on v13

--- a/solution.py
+++ b/solution.py
@@ -129,7 +129,7 @@
             top_ref[h] = jnp.broadcast_to(new, (rows, HD))
             return carry
 
-        lax.fori_loop(0, heads, head, 0, unroll=4)
+        lax.fori_loop(0, heads, head, 0, unroll=8)
 
     own_k.wait()
     own_v.wait()

time: 139 us -> 139 us (level)
  no operation moved by 1% of the time
where the time goes in v14:
time: 139 us; the launch traced here: 136 us
  Pallas kernels  118 us (85%)
  local copies, waits for them, and re-layouts  12.7 us (9%)
  matrix products  2.85 us (2%)
  other arithmetic  2.36 us (2%)
    pallas_call x1, Pallas kernels, attend(): pl.pallas_call(functools.partial(attend_kernel, scale=1.0 / math.sqrt(HD)...  96 us
    pallas_call x1, Pallas kernels, exchange_queries(): pl.pallas_call(functools.partial(exchange_kernel, n_lo=n_lo, n_head=n_hea...  21.8 us
    unnamed x11, local copies, waits for them, and re-layouts  7.72 us
    dot_general x4, matrix products, ancestry(): jnp.einsum('aij,ajk->aik', reached, reached, preferred_element_type=jnp.f...  2.85 us

profile of v14, /device:TPU:1, one launch (start us, length us, event | category | flops | bytes accessed | tf_op | source)
XLA Modules:
  0.0 135.8 jit_solution(1841827177124665246)
XLA Ops:
  0.0 1.2 dynamic_slice.13
  1.2 0.7 pad_add_fusion.info_ref
  2.0 1.2 dynamic_slice.12
  3.2 0.7 add_compare_fusion
  3.9 0.8 copy.11
  4.7 0.9 copy.17
  5.6 0.7 copy.9
  6.3 1.7 %fusion.1 = bf16[8,128,128]{2,1,0:T(8,128)(2,1)S(1)} fusion(s32[8,128]{1,0:T(8,128)} %param.13, pred[128,128]{1,0:T(8,128)(4,1)S(1)} %iota_compare_fusion.1), kind=kOutput, calls=%fused_computation.7 | convolution fusion | flops 67895296 | bytes 282624 | tf_op jit(solution)/shard_map/aij,ajk->aik/dot_general | solution.py:28
  8.0 0.4 fusion.3
  8.5 0.4 fusion.5
  8.9 0.2 fusion.27
  9.2 0.1 fusion.22.tmask_ref
  9.2 21.8 %shard_map.82 = bf16[32,64,128]{2,1,0:T(8,128)(2,1)} custom-call(bf16[8,64,128]{2,1,0:T(8,128)(2,1)} %bitcast.41), custom_call_target="tpu_custom_call" | custom-call | tf_op jit(solution)/shard_map/pallas_call | solution.py:307
  31.0 1.3 reshape.47.q_ref
  32.3 0.0 copy-start.3
  32.3 2.9 %copy.10 = bf16[8,1024,128]{1,2,0:T(8,128)(2,1)S(1)} copy(bf16[8,1024,128]{2,1,0:T(8,128)(2,1)} %param.9) | data formatting | bytes 4194304 | tf_op args[1]
  35.2 0.0 copy-done.3
  35.2 0.0 copy-start
  35.2 1.6 %copy-done = bf16[8,1024,128]{2,1,0:T(8,128)(2,1)S(1)} copy-done((bf16[8,1024,128]{2,1,0:T(8,128)(2,1)S(1)}, bf16[8,1024,128]{2,1,0:T(8,128)(2,1)}, u32[]{:S(2)}) %copy-start) | copy-done | bytes 2097176
  36.8 96.0 %shard_map.83 = (f32[4,32,2048]{2,1,0:T(8,128)S(1)}, f32[4,2,32,128]{3,2,1,0:T(8,128)S(1)}) custom-call(s32[2]{0:T(128)S(1)} %pad_add_fusion.info_ref, bf16[128,2048]{1,0:T(8,128)(2,1)S(1)} %reshape.47.q_ref, bf16[8,128,1024]{2,1,0:T(8,128)(2,1)S(1)} %bitcast.38, bf16[8,1024,128]{2,1,0:T(8,128)(2,1)S(1)} %copy-done, bf16[128,32]{1,0:T(8,128)(2,1)S(1)} %bitcast.39, ...), custom_call_target="tpu_custom_call" | custom-call | tf_op jit(solution)/shard_map/pallas_call | solution.py:223
  132.7 0.0 copy-start.1
  132.8 1.0 copy-done.1
  133.7 0.0 copy-start.2
  133.8 0.1 div.11
  133.9 0.3 mul.19
  134.3 0.2 mul.20
  134.4 0.5 copy-done.2
  135.0 0.1 multiply_reduce_fusion
  135.1 0.8 fusion.10
  (3 shorter events, 0.0 us)
Async XLA Ops:
  32.3 2.9 %copy-start.3 = (bf16[32,128]{1,0:T(8,128)(2,1)S(1)}, bf16[32,128]{1,0:T(8,128)(2,1)}, u32[]{:S(2)}) copy-start(bf16[32,128]{1,0:T(8,128)(2,1)} %tv_ref.1) | copy-start | bytes 24580
  35.2 1.6 %copy-start = (bf16[8,1024,128]{2,1,0:T(8,128)(2,1)S(1)}, bf16[8,1024,128]{2,1,0:T(8,128)(2,1)}, u32[]{:S(2)}) copy-start(bf16[8,1024,128]{2,1,0:T(8,128)(2,1)} %v_hbm.1) | copy-start | bytes 6291460
  132.7 1.0 copy-start.1
  133.7 1.2 copy-start.2

commit v15 on v14

--- a/solution.py
+++ b/solution.py
@@ -98,14 +98,15 @@
         pos = start + lax.broadcasted_iota(jnp.int32, (1, block_len), 1)
         bias = jnp.where(pos < length, 0.0, negative_fill)
 
-        def head(h, carry):
-            col = pl.multiple_of(h * HD, HD)
-            qh = q_ref[:, pl.ds(col, HD)]
+        def pair(p, carry):
+            col = pl.multiple_of(p * 2 * HD, 2 * HD)
+            both = q_ref[:, pl.ds(col, 2 * HD)]
+            qh = jnp.concatenate([both[:, :HD], both[:, HD:]], axis=0)
             sc = jnp.dot(qh, kt_ref[...], preferred_element_type=jnp.float32) * scale + bias
             peak = jnp.max(sc, axis=1, keepdims=True)
             if with_tree:
                 st = jnp.dot(qh, tkt_ref[...], preferred_element_type=jnp.float32) * scale
-                tlive = tmask_ref[...] > 0.5
+                tlive = jnp.concatenate([tmask_ref[...], tmask_ref[...]], axis=0) > 0.5
                 st = jnp.where(tlive, st, negative_fill)
                 peak = jnp.maximum(peak, jnp.max(st, axis=1, keepdims=True))
             w = jnp.exp(sc - jnp.maximum(peak, 0.1 * negative_fill))
@@ -120,16 +121,21 @@
             floored = jnp.maximum(tot, 1.0)
             part = gs / floored
             lt = peak + jnp.log(floored)
-            old = top_ref[h][:, :1]
-            new = jnp.maximum(old, lt)
-            keep = jnp.exp(old - new)
-            add = jnp.exp(lt - new)
-            acc_ref[:, pl.ds(col, HD)] = keep * acc_ref[:, pl.ds(col, HD)] + add * part
-            den_ref[h] = jnp.broadcast_to(keep * den_ref[h][:, :1] + add, (rows, HD))
-            top_ref[h] = jnp.broadcast_to(new, (rows, HD))
+            for half in range(2):
+                h = 2 * p + half
+                hcol = pl.multiple_of(h * HD, HD)
+                lt_h = lt[half * rows : (half + 1) * rows]
+                part_h = part[half * rows : (half + 1) * rows]
+                old = top_ref[h][:, :1]
+                new = jnp.maximum(old, lt_h)
+                keep = jnp.exp(old - new)
+                add = jnp.exp(lt_h - new)
+                acc_ref[:, pl.ds(hcol, HD)] = keep * acc_ref[:, pl.ds(hcol, HD)] + add * part_h
+                den_ref[h] = jnp.broadcast_to(keep * den_ref[h][:, :1] + add, (rows, HD))
+                top_ref[h] = jnp.broadcast_to(new, (rows, HD))
             return carry
 
-        lax.fori_loop(0, heads, head, 0, unroll=8)
+        lax.fori_loop(0, heads // 2, pair, 0, unroll=2)
 
     own_k.wait()
     own_v.wait()

time: 139 us -> 132 us (0.950)
  Pallas kernels: 118 us -> 111 us
    pallas_call x1, Pallas kernels: 96 us -> 89.6 us  [attend(): pl.pallas_call(functools.partial(attend_kernel, scale=1.0 / math.sqrt(HD)...]
where the time goes in v15:
time: 132 us; the launch traced here: 129 us
  Pallas kernels  111 us (84%)
  local copies, waits for them, and re-layouts  12.7 us (10%)
  matrix products  2.85 us (2%)
  other arithmetic  2.36 us (2%)
    pallas_call x1, Pallas kernels, attend(): pl.pallas_call(functools.partial(attend_kernel, scale=1.0 / math.sqrt(HD)...  89.6 us
    pallas_call x1, Pallas kernels, exchange_queries(): pl.pallas_call(functools.partial(exchange_kernel, n_lo=n_lo, n_head=n_hea...  21.8 us
    unnamed x11, local copies, waits for them, and re-layouts  7.72 us
    dot_general x4, matrix products, ancestry(): jnp.einsum('aij,ajk->aik', reached, reached, preferred_element_type=jnp.f...  2.85 us

profile of v15, /device:TPU:1, one launch (start us, length us, event | category | flops | bytes accessed | tf_op | source)
XLA Modules:
  0.0 129.5 jit_solution(749509414005779800)
XLA Ops:
  0.0 1.2 dynamic_slice.13
  1.2 0.7 pad_add_fusion.info_ref
  2.0 1.2 dynamic_slice.12
  3.2 0.7 add_compare_fusion
  3.9 0.8 copy.11
  4.7 0.9 copy.17
  5.6 0.7 copy.9
  6.3 1.7 %fusion.1 = bf16[8,128,128]{2,1,0:T(8,128)(2,1)S(1)} fusion(s32[8,128]{1,0:T(8,128)} %param.13, pred[128,128]{1,0:T(8,128)(4,1)S(1)} %iota_compare_fusion.1), kind=kOutput, calls=%fused_computation.7 | convolution fusion | flops 67895296 | bytes 282624 | tf_op jit(solution)/shard_map/aij,ajk->aik/dot_general | solution.py:28
  8.0 0.4 fusion.3
  8.5 0.4 fusion.5
  8.9 0.2 fusion.27
  9.2 0.1 fusion.22.tmask_ref
  9.2 21.8 %shard_map.82 = bf16[32,64,128]{2,1,0:T(8,128)(2,1)} custom-call(bf16[8,64,128]{2,1,0:T(8,128)(2,1)} %bitcast.41), custom_call_target="tpu_custom_call" | custom-call | tf_op jit(solution)/shard_map/pallas_call | solution.py:313
  31.0 1.3 reshape.47.q_ref
  32.3 0.0 copy-start.3
  32.3 2.9 %copy.10 = bf16[8,1024,128]{1,2,0:T(8,128)(2,1)S(1)} copy(bf16[8,1024,128]{2,1,0:T(8,128)(2,1)} %param.9) | data formatting | bytes 4194304 | tf_op args[1]
  35.2 0.0 copy-done.3
  35.2 0.0 copy-start
  35.2 1.6 %copy-done = bf16[8,1024,128]{2,1,0:T(8,128)(2,1)S(1)} copy-done((bf16[8,1024,128]{2,1,0:T(8,128)(2,1)S(1)}, bf16[8,1024,128]{2,1,0:T(8,128)(2,1)}, u32[]{:S(2)}) %copy-start) | copy-done | bytes 2097176
  36.8 89.6 %shard_map.83 = (f32[4,32,2048]{2,1,0:T(8,128)S(1)}, f32[4,2,32,128]{3,2,1,0:T(8,128)S(1)}) custom-call(s32[2]{0:T(128)S(1)} %pad_add_fusion.info_ref, bf16[128,2048]{1,0:T(8,128)(2,1)S(1)} %reshape.47.q_ref, bf16[8,128,1024]{2,1,0:T(8,128)(2,1)S(1)} %bitcast.38, bf16[8,1024,128]{2,1,0:T(8,128)(2,1)S(1)} %copy-done, bf16[128,32]{1,0:T(8,128)(2,1)S(1)} %bitcast.39, ...), custom_call_target="tpu_custom_call" | custom-call | tf_op jit(solution)/shard_map/pallas_call | solution.py:229
  126.4 0.0 copy-start.1
  126.4 1.0 copy-done.1
  127.4 0.0 copy-start.2
  127.4 0.1 div.11
  127.6 0.3 mul.19
  127.9 0.2 mul.20
  128.1 0.5 copy-done.2
  128.6 0.1 multiply_reduce_fusion
  128.7 0.8 fusion.10
  (3 shorter events, 0.0 us)
Async XLA Ops:
  32.3 2.9 %copy-start.3 = (bf16[32,128]{1,0:T(8,128)(2,1)S(1)}, bf16[32,128]{1,0:T(8,128)(2,1)}, u32[]{:S(2)}) copy-start(bf16[32,128]{1,0:T(8,128)(2,1)} %tv_ref.1) | copy-start | bytes 24580
  35.2 1.6 %copy-start = (bf16[8,1024,128]{2,1,0:T(8,128)(2,1)S(1)}, bf16[8,1024,128]{2,1,0:T(8,128)(2,1)}, u32[]{:S(2)}) copy-start(bf16[8,1024,128]{2,1,0:T(8,128)(2,1)} %v_hbm.1) | copy-start | bytes 6291460
  126.4 1.0 copy-start.1
  127.4 1.2 copy-start.2

commit v16 on v15

--- a/solution.py
+++ b/solution.py
@@ -98,15 +98,17 @@
         pos = start + lax.broadcasted_iota(jnp.int32, (1, block_len), 1)
         bias = jnp.where(pos < length, 0.0, negative_fill)
 
+        stack = 4
+
         def pair(p, carry):
-            col = pl.multiple_of(p * 2 * HD, 2 * HD)
-            both = q_ref[:, pl.ds(col, 2 * HD)]
-            qh = jnp.concatenate([both[:, :HD], both[:, HD:]], axis=0)
+            col = pl.multiple_of(p * stack * HD, stack * HD)
+            both = q_ref[:, pl.ds(col, stack * HD)]
+            qh = jnp.concatenate([both[:, i * HD : (i + 1) * HD] for i in range(stack)], axis=0)
             sc = jnp.dot(qh, kt_ref[...], preferred_element_type=jnp.float32) * scale + bias
             peak = jnp.max(sc, axis=1, keepdims=True)
             if with_tree:
                 st = jnp.dot(qh, tkt_ref[...], preferred_element_type=jnp.float32) * scale
-                tlive = jnp.concatenate([tmask_ref[...], tmask_ref[...]], axis=0) > 0.5
+                tlive = jnp.concatenate([tmask_ref[...]] * stack, axis=0) > 0.5
                 st = jnp.where(tlive, st, negative_fill)
                 peak = jnp.maximum(peak, jnp.max(st, axis=1, keepdims=True))
             w = jnp.exp(sc - jnp.maximum(peak, 0.1 * negative_fill))
@@ -121,8 +123,8 @@
             floored = jnp.maximum(tot, 1.0)
             part = gs / floored
             lt = peak + jnp.log(floored)
-            for half in range(2):
-                h = 2 * p + half
+            for half in range(stack):
+                h = stack * p + half
                 hcol = pl.multiple_of(h * HD, HD)
                 lt_h = lt[half * rows : (half + 1) * rows]
                 part_h = part[half * rows : (half + 1) * rows]
@@ -135,7 +137,7 @@
                 top_ref[h] = jnp.broadcast_to(new, (rows, HD))
             return carry
 
-        lax.fori_loop(0, heads // 2, pair, 0, unroll=2)
+        lax.fori_loop(0, heads // stack, pair, 0)
 
     own_k.wait()
     own_v.wait()

time: 132 us -> 136 us (1.030)
  the two profiles are of different devices: /device:TPU:1 before, /device:TPU:231 now
where the time goes in v16:
time: 136 us
  Pallas kernels  118 us (87%)
  local copies, waits for them, and re-layouts  12.7 us (9%)
  matrix products  2.85 us (2%)
  other arithmetic  2.36 us (2%)
    pallas_call x1, Pallas kernels, attend(): pl.pallas_call(functools.partial(attend_kernel, scale=1.0 / math.sqrt(HD)...  96.2 us
    pallas_call x1, Pallas kernels, exchange_queries(): pl.pallas_call(functools.partial(exchange_kernel, n_lo=n_lo, n_head=n_hea...  21.5 us
    unnamed x11, local copies, waits for them, and re-layouts  7.72 us
    dot_general x4, matrix products, ancestry(): jnp.einsum('aij,ajk->aik', reached, reached, preferred_element_type=jnp.f...  2.85 us

profile of v16, /device:TPU:231, one launch (start us, length us, event | category | flops | bytes accessed | tf_op | source)
XLA Modules:
  0.0 135.8 jit_solution(7979634023164571363)
XLA Ops:
  0.0 1.2 dynamic_slice.13
  1.2 0.7 pad_add_fusion.info_ref
  2.0 1.2 dynamic_slice.12
  3.2 0.7 add_compare_fusion
  3.9 0.8 copy.11
  4.7 0.9 copy.17
  5.6 0.7 copy.9
  6.3 1.7 %fusion.1 = bf16[8,128,128]{2,1,0:T(8,128)(2,1)S(1)} fusion(s32[8,128]{1,0:T(8,128)} %param.13, pred[128,128]{1,0:T(8,128)(4,1)S(1)} %iota_compare_fusion.1), kind=kOutput, calls=%fused_computation.7 | convolution fusion | flops 67895296 | bytes 282624 | tf_op jit(solution)/shard_map/aij,ajk->aik/dot_general | solution.py:28
  8.0 0.4 fusion.3
  8.5 0.4 fusion.5
  8.9 0.2 fusion.27
  9.2 0.1 fusion.22.tmask_ref
  9.3 21.5 %shard_map.82 = bf16[32,64,128]{2,1,0:T(8,128)(2,1)} custom-call(bf16[8,64,128]{2,1,0:T(8,128)(2,1)} %bitcast.41), custom_call_target="tpu_custom_call" | custom-call | tf_op jit(solution)/shard_map/pallas_call | solution.py:315
  30.8 1.3 reshape.47.q_ref
  32.0 0.0 copy-start.3
  32.1 2.9 %copy.10 = bf16[8,1024,128]{1,2,0:T(8,128)(2,1)S(1)} copy(bf16[8,1024,128]{2,1,0:T(8,128)(2,1)} %param.9) | data formatting | bytes 4194304 | tf_op args[1]
  34.9 0.0 copy-done.3
  34.9 0.0 copy-start
  35.0 1.6 %copy-done = bf16[8,1024,128]{2,1,0:T(8,128)(2,1)S(1)} copy-done((bf16[8,1024,128]{2,1,0:T(8,128)(2,1)S(1)}, bf16[8,1024,128]{2,1,0:T(8,128)(2,1)}, u32[]{:S(2)}) %copy-start) | copy-done | bytes 2097176
  36.5 96.2 %shard_map.83 = (f32[4,32,2048]{2,1,0:T(8,128)S(1)}, f32[4,2,32,128]{3,2,1,0:T(8,128)S(1)}) custom-call(s32[2]{0:T(128)S(1)} %pad_add_fusion.info_ref, bf16[128,2048]{1,0:T(8,128)(2,1)S(1)} %reshape.47.q_ref, bf16[8,128,1024]{2,1,0:T(8,128)(2,1)S(1)} %bitcast.38, bf16[8,1024,128]{2,1,0:T(8,128)(2,1)S(1)} %copy-done, bf16[128,32]{1,0:T(8,128)(2,1)S(1)} %bitcast.39, ...), custom_call_target="tpu_custom_call" | custom-call | tf_op jit(solution)/shard_map/pallas_call | solution.py:231
  132.7 0.0 copy-start.1
  132.7 1.0 copy-done.1
  133.7 0.0 copy-start.2
  133.8 0.1 div.11
  133.9 0.3 mul.19
  134.2 0.2 mul.20
  134.4 0.5 copy-done.2
  135.0 0.1 multiply_reduce_fusion
  135.1 0.8 fusion.10
  (3 shorter events, 0.0 us)
Async XLA Ops:
  32.0 2.9 %copy-start.3 = (bf16[32,128]{1,0:T(8,128)(2,1)S(1)}, bf16[32,128]{1,0:T(8,128)(2,1)}, u32[]{:S(2)}) copy-start(bf16[32,128]{1,0:T(8,128)(2,1)} %tv_ref.1) | copy-start | bytes 24580
  34.9 1.6 %copy-start = (bf16[8,1024,128]{2,1,0:T(8,128)(2,1)S(1)}, bf16[8,1024,128]{2,1,0:T(8,128)(2,1)}, u32[]{:S(2)}) copy-start(bf16[8,1024,128]{2,1,0:T(8,128)(2,1)} %v_hbm.1) | copy-start | bytes 6291460
  132.7 1.0 copy-start.1
  133.7 1.2 copy-start.2

commit v17 on v15

--- a/solution.py
+++ b/solution.py
@@ -135,7 +135,7 @@
                 top_ref[h] = jnp.broadcast_to(new, (rows, HD))
             return carry
 
-        lax.fori_loop(0, heads // 2, pair, 0, unroll=2)
+        lax.fori_loop(0, heads // 2, pair, 0, unroll=4)
 
     own_k.wait()
     own_v.wait()

time: 132 us -> 131 us (level)
  no operation moved by 1% of the time
where the time goes in v17:
time: 131 us; the launch traced here: 129 us
  Pallas kernels  111 us (85%)
  local copies, waits for them, and re-layouts  12.7 us (10%)
  matrix products  2.85 us (2%)
  other arithmetic  2.36 us (2%)
    pallas_call x1, Pallas kernels, attend(): pl.pallas_call(functools.partial(attend_kernel, scale=1.0 / math.sqrt(HD)...  89.1 us
    pallas_call x1, Pallas kernels, exchange_queries(): pl.pallas_call(functools.partial(exchange_kernel, n_lo=n_lo, n_head=n_hea...  21.8 us
    unnamed x11, local copies, waits for them, and re-layouts  7.72 us
    dot_general x4, matrix products, ancestry(): jnp.einsum('aij,ajk->aik', reached, reached, preferred_element_type=jnp.f...  2.85 us

profile of v17, /device:TPU:1, one launch (start us, length us, event | category | flops | bytes accessed | tf_op | source)
XLA Modules:
  0.0 129.0 jit_solution(4027703187479307004)
XLA Ops:
  0.0 1.2 dynamic_slice.13
  1.2 0.7 pad_add_fusion.info_ref
  2.0 1.2 dynamic_slice.12
  3.2 0.7 add_compare_fusion
  3.9 0.8 copy.11
  4.7 0.9 copy.17
  5.6 0.7 copy.9
  6.3 1.7 %fusion.1 = bf16[8,128,128]{2,1,0:T(8,128)(2,1)S(1)} fusion(s32[8,128]{1,0:T(8,128)} %param.13, pred[128,128]{1,0:T(8,128)(4,1)S(1)} %iota_compare_fusion.1), kind=kOutput, calls=%fused_computation.7 | convolution fusion | flops 67895296 | bytes 282624 | tf_op jit(solution)/shard_map/aij,ajk->aik/dot_general | solution.py:28
  8.0 0.4 fusion.3
  8.5 0.4 fusion.5
  8.9 0.2 fusion.27
  9.2 0.1 fusion.22.tmask_ref
  9.2 21.8 %shard_map.82 = bf16[32,64,128]{2,1,0:T(8,128)(2,1)} custom-call(bf16[8,64,128]{2,1,0:T(8,128)(2,1)} %bitcast.41), custom_call_target="tpu_custom_call" | custom-call | tf_op jit(solution)/shard_map/pallas_call | solution.py:313
  31.0 1.3 reshape.47.q_ref
  32.3 0.0 copy-start.3
  32.3 2.9 %copy.10 = bf16[8,1024,128]{1,2,0:T(8,128)(2,1)S(1)} copy(bf16[8,1024,128]{2,1,0:T(8,128)(2,1)} %param.9) | data formatting | bytes 4194304 | tf_op args[1]
  35.2 0.0 copy-done.3
  35.2 0.0 copy-start
  35.2 1.6 %copy-done = bf16[8,1024,128]{2,1,0:T(8,128)(2,1)S(1)} copy-done((bf16[8,1024,128]{2,1,0:T(8,128)(2,1)S(1)}, bf16[8,1024,128]{2,1,0:T(8,128)(2,1)}, u32[]{:S(2)}) %copy-start) | copy-done | bytes 2097176
  36.8 89.1 %shard_map.83 = (f32[4,32,2048]{2,1,0:T(8,128)S(1)}, f32[4,2,32,128]{3,2,1,0:T(8,128)S(1)}) custom-call(s32[2]{0:T(128)S(1)} %pad_add_fusion.info_ref, bf16[128,2048]{1,0:T(8,128)(2,1)S(1)} %reshape.47.q_ref, bf16[8,128,1024]{2,1,0:T(8,128)(2,1)S(1)} %bitcast.38, bf16[8,1024,128]{2,1,0:T(8,128)(2,1)S(1)} %copy-done, bf16[128,32]{1,0:T(8,128)(2,1)S(1)} %bitcast.39, ...), custom_call_target="tpu_custom_call" | custom-call | tf_op jit(solution)/shard_map/pallas_call | solution.py:229
  125.9 0.0 copy-start.1
  125.9 1.0 copy-done.1
  126.9 0.0 copy-start.2
  126.9 0.1 div.11
  127.0 0.3 mul.19
  127.4 0.2 mul.20
  127.6 0.5 copy-done.2
  128.1 0.1 multiply_reduce_fusion
  128.2 0.8 fusion.10
  (3 shorter events, 0.0 us)
Async XLA Ops:
  32.3 2.9 %copy-start.3 = (bf16[32,128]{1,0:T(8,128)(2,1)S(1)}, bf16[32,128]{1,0:T(8,128)(2,1)}, u32[]{:S(2)}) copy-start(bf16[32,128]{1,0:T(8,128)(2,1)} %tv_ref.1) | copy-start | bytes 24580
  35.2 1.6 %copy-start = (bf16[8,1024,128]{2,1,0:T(8,128)(2,1)S(1)}, bf16[8,1024,128]{2,1,0:T(8,128)(2,1)}, u32[]{:S(2)}) copy-start(bf16[8,1024,128]{2,1,0:T(8,128)(2,1)} %v_hbm.1) | copy-start | bytes 6291460
  125.9 1.0 copy-start.1
  126.9 1.2 copy-start.2

commit v18 on v17

--- a/solution.py
+++ b/solution.py
@@ -347,8 +347,8 @@
     query_block = exchange_queries(pieces, n_lo, n_head)
     query_block = query_block.reshape(node_count, width)
 
-    reached = ancestry(parents)
-    ancestors = lax.dynamic_index_in_dim(reached, request, 0, keepdims=False)
+    own_parents = lax.dynamic_slice_in_dim(parents, request, 1, 0)
+    ancestors = ancestry(own_parents)[0]
     ancestors = lax.dynamic_slice_in_dim(ancestors, quarter * rows_owned, rows_owned, 1)
     tree_mask = ancestors.astype(jnp.float32)
     length = lax.dynamic_index_in_dim(cache_lens, request, 0, keepdims=False)

time: 131 us -> 129 us (0.985)
  matrix products: 2.85 us -> 1.05 us
    dot_general x4, matrix products: 2.85 us -> 1.05 us  [ancestry(): jnp.einsum('aij,ajk->aik', reached, reached, preferred_element_type=jnp.f...]
    unnamed x11 -> x13, local copies, waits for them, and re-layouts: 7.72 us -> 7.73 us
where the time goes in v18:
time: 129 us; the launch traced here: 127 us
  Pallas kernels  111 us (86%)
  local copies, waits for them, and re-layouts  12.8 us (10%)
  other arithmetic  2.36 us (2%)
    pallas_call x1, Pallas kernels, attend(): pl.pallas_call(functools.partial(attend_kernel, scale=1.0 / math.sqrt(HD)...  89.1 us
    pallas_call x1, Pallas kernels, exchange_queries(): pl.pallas_call(functools.partial(exchange_kernel, n_lo=n_lo, n_head=n_hea...  21.6 us
    unnamed x13, local copies, waits for them, and re-layouts  7.73 us

profile of v18, /device:TPU:1, one launch (start us, length us, event | category | flops | bytes accessed | tf_op | source)
XLA Modules:
  0.0 127.0 jit_solution(12820402536758430112)
XLA Ops:
  0.0 0.0 copy-start
  0.0 1.2 dynamic_slice.16
  1.3 0.7 pad_add_fusion.info_ref
  2.0 1.2 dynamic_slice.15
  3.2 0.7 add_compare_fusion
  3.9 0.0 copy-done
  3.9 0.4 fusion.1
  4.3 0.3 fusion.3
  4.5 0.3 fusion.5
  4.8 0.1 fusion.25
  4.9 0.1 fusion.15.tmask_ref
  5.0 0.8 copy.16
  5.9 0.9 copy.20
  6.8 0.7 copy.14
  7.5 21.6 %shard_map.82 = bf16[32,64,128]{2,1,0:T(8,128)(2,1)} custom-call(bf16[8,64,128]{2,1,0:T(8,128)(2,1)} %bitcast.42), custom_call_target="tpu_custom_call" | custom-call | tf_op jit(solution)/shard_map/pallas_call | solution.py:313
  29.1 1.3 reshape.206.q_ref
  30.4 0.0 copy-start.4
  30.4 2.9 %copy.15 = bf16[8,1024,128]{1,2,0:T(8,128)(2,1)S(1)} copy(bf16[8,1024,128]{2,1,0:T(8,128)(2,1)} %param.9) | data formatting | bytes 4194304 | tf_op args[1]
  33.3 0.0 copy-done.4
  33.3 0.0 copy-start.1
  33.3 1.6 %copy-done.1 = bf16[8,1024,128]{2,1,0:T(8,128)(2,1)S(1)} copy-done((bf16[8,1024,128]{2,1,0:T(8,128)(2,1)S(1)}, bf16[8,1024,128]{2,1,0:T(8,128)(2,1)}, u32[]{:S(2)}) %copy-start.1) | copy-done | bytes 2097176
  34.9 89.1 %shard_map.83 = (f32[4,32,2048]{2,1,0:T(8,128)S(1)}, f32[4,2,32,128]{3,2,1,0:T(8,128)S(1)}) custom-call(s32[2]{0:T(128)S(1)} %pad_add_fusion.info_ref, bf16[128,2048]{1,0:T(8,128)(2,1)S(1)} %reshape.206.q_ref, bf16[8,128,1024]{2,1,0:T(8,128)(2,1)S(1)} %bitcast.39, bf16[8,1024,128]{2,1,0:T(8,128)(2,1)S(1)} %copy-done.1, bf16[128,32]{1,0:T(8,128)(2,1)S(1)} %bitcast.40, ...), custom_call_target="tpu_custom_call" | custom-call | tf_op jit(solution)/shard_map/pallas_call | solution.py:229
  123.9 0.0 copy-start.2
  124.0 1.0 copy-done.2
  124.9 0.0 copy-start.3
  125.0 0.1 div.11
  125.1 0.3 mul.19
  125.5 0.2 mul.20
  125.6 0.5 copy-done.3
  126.2 0.1 multiply_reduce_fusion
  126.3 0.8 fusion.7
  (3 shorter events, 0.0 us)
Async XLA Ops:
  0.0 3.9 %copy-start = (s32[8,128]{1,0:T(8,128)S(1)}, s32[8,128]{1,0:T(8,128)}, u32[]{:S(2)}) copy-start(s32[8,128]{1,0:T(8,128)} %param.13) | copy-start | bytes 12292
  30.4 2.9 %copy-start.4 = (bf16[32,128]{1,0:T(8,128)(2,1)S(1)}, bf16[32,128]{1,0:T(8,128)(2,1)}, u32[]{:S(2)}) copy-start(bf16[32,128]{1,0:T(8,128)(2,1)} %tv_ref.1) | copy-start | bytes 24580
  33.3 1.6 %copy-start.1 = (bf16[8,1024,128]{2,1,0:T(8,128)(2,1)S(1)}, bf16[8,1024,128]{2,1,0:T(8,128)(2,1)}, u32[]{:S(2)}) copy-start(bf16[8,1024,128]{2,1,0:T(8,128)(2,1)} %v_hbm.1) | copy-start | bytes 6291460
  123.9 1.0 copy-start.2
  124.9 1.2 copy-start.3

commit v19 on v18

--- a/solution.py
+++ b/solution.py
@@ -344,6 +344,8 @@
     width = queries.shape[1] // n_head
     pieces = queries.reshape(queries.shape[0], n_head, width // HD, HD).transpose(1, 0, 2, 3)
     pieces = pieces.reshape(n_head, queries.shape[0] * width // HD, HD)
+    keys_t = cache_keys.transpose(0, 2, 1)
+    pieces, keys_t = lax.optimization_barrier((pieces, keys_t))
     query_block = exchange_queries(pieces, n_lo, n_head)
     query_block = query_block.reshape(node_count, width)
 
@@ -354,7 +356,6 @@
     length = lax.dynamic_index_in_dim(cache_lens, request, 0, keepdims=False)
     live_size = lax.dynamic_index_in_dim(tree_sizes, request, 0, keepdims=False)
     info = jnp.stack([length, jnp.int32(n_lo)]).astype(jnp.int32)
-    keys_t = cache_keys.transpose(0, 2, 1)
     got_acc, got_stats = attend(
         info, query_block, keys_t, cache_values, tree_keys.T, tree_values, tree_mask, n_lo
     )

time: 129 us -> 129 us (level)
  no operation moved by 1% of the time
where the time goes in v19:
time: 129 us; the launch traced here: 127 us
  Pallas kernels  111 us (86%)
  local copies, waits for them, and re-layouts  12.8 us (10%)
  other arithmetic  2.36 us (2%)
    pallas_call x1, Pallas kernels, attend(): pl.pallas_call(functools.partial(attend_kernel, scale=1.0 / math.sqrt(HD)...  89.1 us
    pallas_call x1, Pallas kernels, exchange_queries(): pl.pallas_call(functools.partial(exchange_kernel, n_lo=n_lo, n_head=n_hea...  21.8 us
    unnamed x13, local copies, waits for them, and re-layouts  7.73 us

profile of v19, /device:TPU:1, one launch (start us, length us, event | category | flops | bytes accessed | tf_op | source)
XLA Modules:
  0.0 127.2 jit_solution(12459651926373049850)
XLA Ops:
  0.0 0.0 copy-start
  0.0 1.2 dynamic_slice.16
  1.3 0.7 pad_add_fusion.info_ref
  2.0 1.2 dynamic_slice.15
  3.2 0.7 add_compare_fusion
  3.9 0.0 copy-done
  3.9 0.4 fusion.1
  4.3 0.3 fusion.3
  4.5 0.3 fusion.5
  4.8 0.1 fusion.25
  4.9 0.1 fusion.15.tmask_ref
  5.0 0.8 copy.16
  5.9 0.9 copy.20
  6.8 0.7 copy.14
  7.5 0.0 copy-start.4
  7.5 2.9 %copy.15 = bf16[8,1024,128]{1,2,0:T(8,128)(2,1)S(1)} copy(bf16[8,1024,128]{2,1,0:T(8,128)(2,1)} %param.9) | data formatting | bytes 4194304 | tf_op args[1]
  10.3 21.8 %shard_map.82 = bf16[32,64,128]{2,1,0:T(8,128)(2,1)} custom-call(bf16[8,64,128]{2,1,0:T(8,128)(2,1)} %bitcast.42), custom_call_target="tpu_custom_call" | custom-call | tf_op jit(solution)/shard_map/pallas_call | solution.py:313
  32.1 1.3 reshape.206.q_ref
  33.4 0.0 copy-done.4
  33.4 0.0 copy-start.1
  33.4 1.6 %copy-done.1 = bf16[8,1024,128]{2,1,0:T(8,128)(2,1)S(1)} copy-done((bf16[8,1024,128]{2,1,0:T(8,128)(2,1)S(1)}, bf16[8,1024,128]{2,1,0:T(8,128)(2,1)}, u32[]{:S(2)}) %copy-start.1) | copy-done | bytes 2097176
  35.0 89.1 %shard_map.83 = (f32[4,32,2048]{2,1,0:T(8,128)S(1)}, f32[4,2,32,128]{3,2,1,0:T(8,128)S(1)}) custom-call(s32[2]{0:T(128)S(1)} %pad_add_fusion.info_ref, bf16[128,2048]{1,0:T(8,128)(2,1)S(1)} %reshape.206.q_ref, bf16[8,128,1024]{2,1,0:T(8,128)(2,1)S(1)} %bitcast.39, bf16[8,1024,128]{2,1,0:T(8,128)(2,1)S(1)} %copy-done.1, bf16[128,32]{1,0:T(8,128)(2,1)S(1)} %bitcast.40, ...), custom_call_target="tpu_custom_call" | custom-call | tf_op jit(solution)/shard_map/pallas_call | solution.py:229
  124.1 0.0 copy-start.2
  124.1 1.0 copy-done.2
  125.1 0.0 copy-start.3
  125.1 0.1 div.11
  125.2 0.3 mul.19
  125.6 0.2 mul.20
  125.8 0.5 copy-done.3
  126.3 0.1 multiply_reduce_fusion
  126.4 0.8 fusion.7
  (3 shorter events, 0.0 us)
Async XLA Ops:
  0.0 3.9 %copy-start = (s32[8,128]{1,0:T(8,128)S(1)}, s32[8,128]{1,0:T(8,128)}, u32[]{:S(2)}) copy-start(s32[8,128]{1,0:T(8,128)} %param.13) | copy-start | bytes 12292
  7.5 25.9 %copy-start.4 = (bf16[32,128]{1,0:T(8,128)(2,1)S(1)}, bf16[32,128]{1,0:T(8,128)(2,1)}, u32[]{:S(2)}) copy-start(bf16[32,128]{1,0:T(8,128)(2,1)} %tv_ref.1) | copy-start | bytes 24580
  33.4 1.6 %copy-start.1 = (bf16[8,1024,128]{2,1,0:T(8,128)(2,1)S(1)}, bf16[8,1024,128]{2,1,0:T(8,128)(2,1)}, u32[]{:S(2)}) copy-start(bf16[8,1024,128]{2,1,0:T(8,128)(2,1)} %v_hbm.1) | copy-start | bytes 6291460
  124.1 1.0 copy-start.2
  125.1 1.2 copy-start.3

commit v20 on v18

--- a/solution.py
+++ b/solution.py
@@ -77,7 +77,7 @@
             ),
         )
 
-    ahead = 2
+    ahead = 3
     for shift in range(1, min(ahead, n_hi - 1) + 1):
         t = lax.rem(request + shift, n_hi)
         for copy in pushes(t):

time: 129 us -> 125 us (0.969)
  Pallas kernels: 111 us -> 108 us
    pallas_call x1, Pallas kernels: 89.1 us -> 86.3 us  [attend(): pl.pallas_call(functools.partial(attend_kernel, scale=1.0 / math.sqrt(HD)...]
where the time goes in v20:
time: 125 us; the launch traced here: 124 us
  Pallas kernels  108 us (86%)
  local copies, waits for them, and re-layouts  12.8 us (10%)
  other arithmetic  2.36 us (2%)
    pallas_call x1, Pallas kernels, attend(): pl.pallas_call(functools.partial(attend_kernel, scale=1.0 / math.sqrt(HD)...  86.3 us
    pallas_call x1, Pallas kernels, exchange_queries(): pl.pallas_call(functools.partial(exchange_kernel, n_lo=n_lo, n_head=n_hea...  21.6 us
    unnamed x13, local copies, waits for them, and re-layouts  7.73 us

profile of v20, /device:TPU:1, one launch (start us, length us, event | category | flops | bytes accessed | tf_op | source)
XLA Modules:
  0.0 124.2 jit_solution(15279292813083864692)
XLA Ops:
  0.0 0.0 copy-start
  0.0 1.2 %dynamic_slice.16 = s32[1]{0:T(128)} dynamic-slice(s32[8]{0:T(128)} %param.15, s32[]{:T(128)S(6)} %select_n.13), dynamic_slice_sizes={1} | dynamic-slice | bytes 12 | tf_op jit(solution)/shard_map/jit(dynamic_index_in_dim)/dynamic_slice | solution.py:354
  1.3 0.7 pad_add_fusion.info_ref
  2.0 1.2 dynamic_slice.15
  3.2 0.7 add_compare_fusion
  3.9 0.0 copy-done
  3.9 0.4 fusion.1
  4.3 0.3 fusion.3
  4.5 0.3 fusion.5
  4.8 0.1 fusion.25
  4.9 0.1 fusion.15.tmask_ref
  5.0 0.8 copy.16
  5.9 0.9 copy.20
  6.8 0.7 copy.14
  7.5 21.6 %shard_map.82 = bf16[32,64,128]{2,1,0:T(8,128)(2,1)} custom-call(bf16[8,64,128]{2,1,0:T(8,128)(2,1)} %bitcast.42), custom_call_target="tpu_custom_call" | custom-call | tf_op jit(solution)/shard_map/pallas_call | solution.py:313
  29.1 1.3 %reshape.206.q_ref = bf16[128,2048]{1,0:T(8,128)(2,1)S(1)} reshape(bf16[32,64,128]{2,1,0:T(8,128)(2,1)} %shard_map.82) | data formatting | bytes 1048576 | tf_op jit(solution)/shard_map/reshape | solution.py:348
  30.4 0.0 copy-start.4
  30.4 2.9 %copy.15 = bf16[8,1024,128]{1,2,0:T(8,128)(2,1)S(1)} copy(bf16[8,1024,128]{2,1,0:T(8,128)(2,1)} %param.9) | data formatting | bytes 4194304 | tf_op args[1]
  33.3 0.0 copy-done.4
  33.3 0.0 copy-start.1
  33.3 1.6 %copy-done.1 = bf16[8,1024,128]{2,1,0:T(8,128)(2,1)S(1)} copy-done((bf16[8,1024,128]{2,1,0:T(8,128)(2,1)S(1)}, bf16[8,1024,128]{2,1,0:T(8,128)(2,1)}, u32[]{:S(2)}) %copy-start.1) | copy-done | bytes 2097176
  34.9 86.3 %shard_map.83 = (f32[4,32,2048]{2,1,0:T(8,128)S(1)}, f32[4,2,32,128]{3,2,1,0:T(8,128)S(1)}) custom-call(s32[2]{0:T(128)S(1)} %pad_add_fusion.info_ref, bf16[128,2048]{1,0:T(8,128)(2,1)S(1)} %reshape.206.q_ref, bf16[8,128,1024]{2,1,0:T(8,128)(2,1)S(1)} %bitcast.39, bf16[8,1024,128]{2,1,0:T(8,128)(2,1)S(1)} %copy-done.1, bf16[128,32]{1,0:T(8,128)(2,1)S(1)} %bitcast.40, ...), custom_call_target="tpu_custom_call" | custom-call | tf_op jit(solution)/shard_map/pallas_call | solution.py:229
  121.1 0.0 copy-start.2
  121.1 1.0 copy-done.2
  122.1 0.0 copy-start.3
  122.2 0.1 div.11
  122.3 0.3 mul.19
  122.6 0.2 mul.20
  122.8 0.5 copy-done.3
  123.3 0.1 multiply_reduce_fusion
  123.5 0.8 fusion.7
  (3 shorter events, 0.0 us)
Async XLA Ops:
  0.0 3.9 %copy-start = (s32[8,128]{1,0:T(8,128)S(1)}, s32[8,128]{1,0:T(8,128)}, u32[]{:S(2)}) copy-start(s32[8,128]{1,0:T(8,128)} %param.13) | copy-start | bytes 12292
  30.4 2.9 %copy-start.4 = (bf16[32,128]{1,0:T(8,128)(2,1)S(1)}, bf16[32,128]{1,0:T(8,128)(2,1)}, u32[]{:S(2)}) copy-start(bf16[32,128]{1,0:T(8,128)(2,1)} %tv_ref.1) | copy-start | bytes 24580
  33.3 1.6 %copy-start.1 = (bf16[8,1024,128]{2,1,0:T(8,128)(2,1)S(1)}, bf16[8,1024,128]{2,1,0:T(8,128)(2,1)}, u32[]{:S(2)}) copy-start(bf16[8,1024,128]{2,1,0:T(8,128)(2,1)} %v_hbm.1) | copy-start | bytes 6291460
  121.1 1.0 copy-start.2
  122.1 1.2 copy-start.3

commit v21 on v20

--- a/solution.py
+++ b/solution.py
@@ -77,7 +77,7 @@
             ),
         )
 
-    ahead = 3
+    ahead = 4
     for shift in range(1, min(ahead, n_hi - 1) + 1):
         t = lax.rem(request + shift, n_hi)
         for copy in pushes(t):

time: 125 us -> 125 us (level)
  no operation moved by 1% of the time
where the time goes in v21:
time: 125 us; the launch traced here: 124 us
  Pallas kernels  108 us (86%)
  local copies, waits for them, and re-layouts  12.8 us (10%)
  other arithmetic  2.36 us (2%)
    pallas_call x1, Pallas kernels, attend(): pl.pallas_call(functools.partial(attend_kernel, scale=1.0 / math.sqrt(HD)...  86.3 us
    pallas_call x1, Pallas kernels, exchange_queries(): pl.pallas_call(functools.partial(exchange_kernel, n_lo=n_lo, n_head=n_hea...  21.6 us
    unnamed x13, local copies, waits for them, and re-layouts  7.73 us

profile of v21, /device:TPU:1, one launch (start us, length us, event | category | flops | bytes accessed | tf_op | source)
XLA Modules:
  0.0 124.2 jit_solution(15673700407282366973)
XLA Ops:
  0.0 0.0 copy-start
  0.0 1.2 %dynamic_slice.16 = s32[1]{0:T(128)} dynamic-slice(s32[8]{0:T(128)} %param.15, s32[]{:T(128)S(6)} %select_n.13), dynamic_slice_sizes={1} | dynamic-slice | bytes 12 | tf_op jit(solution)/shard_map/jit(dynamic_index_in_dim)/dynamic_slice | solution.py:354
  1.3 0.7 pad_add_fusion.info_ref
  2.0 1.2 dynamic_slice.15
  3.2 0.7 add_compare_fusion
  3.9 0.0 copy-done
  3.9 0.4 fusion.1
  4.3 0.3 fusion.3
  4.5 0.3 fusion.5
  4.8 0.1 fusion.25
  4.9 0.1 fusion.15.tmask_ref
  5.0 0.8 copy.16
  5.9 0.9 copy.20
  6.8 0.7 copy.14
  7.5 21.6 %shard_map.82 = bf16[32,64,128]{2,1,0:T(8,128)(2,1)} custom-call(bf16[8,64,128]{2,1,0:T(8,128)(2,1)} %bitcast.42), custom_call_target="tpu_custom_call" | custom-call | tf_op jit(solution)/shard_map/pallas_call | solution.py:313
  29.1 1.3 %reshape.206.q_ref = bf16[128,2048]{1,0:T(8,128)(2,1)S(1)} reshape(bf16[32,64,128]{2,1,0:T(8,128)(2,1)} %shard_map.82) | data formatting | bytes 1048576 | tf_op jit(solution)/shard_map/reshape | solution.py:348
  30.4 0.0 copy-start.4
  30.4 2.9 %copy.15 = bf16[8,1024,128]{1,2,0:T(8,128)(2,1)S(1)} copy(bf16[8,1024,128]{2,1,0:T(8,128)(2,1)} %param.9) | data formatting | bytes 4194304 | tf_op args[1]
  33.3 0.0 copy-done.4
  33.3 0.0 copy-start.1
  33.3 1.6 %copy-done.1 = bf16[8,1024,128]{2,1,0:T(8,128)(2,1)S(1)} copy-done((bf16[8,1024,128]{2,1,0:T(8,128)(2,1)S(1)}, bf16[8,1024,128]{2,1,0:T(8,128)(2,1)}, u32[]{:S(2)}) %copy-start.1) | copy-done | bytes 2097176
  34.9 86.3 %shard_map.83 = (f32[4,32,2048]{2,1,0:T(8,128)S(1)}, f32[4,2,32,128]{3,2,1,0:T(8,128)S(1)}) custom-call(s32[2]{0:T(128)S(1)} %pad_add_fusion.info_ref, bf16[128,2048]{1,0:T(8,128)(2,1)S(1)} %reshape.206.q_ref, bf16[8,128,1024]{2,1,0:T(8,128)(2,1)S(1)} %bitcast.39, bf16[8,1024,128]{2,1,0:T(8,128)(2,1)S(1)} %copy-done.1, bf16[128,32]{1,0:T(8,128)(2,1)S(1)} %bitcast.40, ...), custom_call_target="tpu_custom_call" | custom-call | tf_op jit(solution)/shard_map/pallas_call | solution.py:229
  121.1 0.0 copy-start.2
  121.1 1.0 copy-done.2
  122.1 0.0 copy-start.3
  122.2 0.1 div.11
  122.3 0.3 mul.19
  122.6 0.2 mul.20
  122.8 0.5 copy-done.3
  123.3 0.1 multiply_reduce_fusion
  123.4 0.8 fusion.7
  (3 shorter events, 0.0 us)
Async XLA Ops:
  0.0 3.9 %copy-start = (s32[8,128]{1,0:T(8,128)S(1)}, s32[8,128]{1,0:T(8,128)}, u32[]{:S(2)}) copy-start(s32[8,128]{1,0:T(8,128)} %param.13) | copy-start | bytes 12292
  30.4 2.9 %copy-start.4 = (bf16[32,128]{1,0:T(8,128)(2,1)S(1)}, bf16[32,128]{1,0:T(8,128)(2,1)}, u32[]{:S(2)}) copy-start(bf16[32,128]{1,0:T(8,128)(2,1)} %tv_ref.1) | copy-start | bytes 24580
  33.3 1.6 %copy-start.1 = (bf16[8,1024,128]{2,1,0:T(8,128)(2,1)S(1)}, bf16[8,1024,128]{2,1,0:T(8,128)(2,1)}, u32[]{:S(2)}) copy-start(bf16[8,1024,128]{2,1,0:T(8,128)(2,1)} %v_hbm.1) | copy-start | bytes 6291460
  121.1 1.0 copy-start.2
  122.1 1.2 copy-start.3
